TPU v7x, 256 devices: a whole 4x4x8 slice. The times are simulated.
256 devices in a mesh: section: 16 (over z, core), ep: 16 (over y, x).
Axes of the slice: x: 4, y: 4, z: 8, core: 2. Of those that a mesh axis runs over, the one named last changes fastest.
Arguments:
- states: bfloat16 [4096, 3072], P(('section', 'ep')), may hold values from -6 to 6
- entering: bfloat16 [256, 3072], P('ep'), may hold values from -6 to 6
- seq_lens: int32 [17, 256], replicated, may hold values from 1 to 16, 2048 in all within a row
- routes: int32 [16, 2, 256, 2], P('section', None, 'ep'), may hold values from 0 to 7, all different within a row; in each aligned block of 16 rows (0 to 15, 16 to 31, ..., all dimensions but the last counted through in order) at most 8 rows name the same one
- attn_norm: bfloat16 [16, 3072], P('section'), may hold values from 0.099609375 to 1.8984375
- ffn_norm: bfloat16 [16, 3072], P('section'), may hold values from 0.099609375 to 1.8984375
- wq: bfloat16 [16, 3072, 4096], P('section', None, 'ep'), may hold values from -0.109375 to 0.109375
- wk: bfloat16 [16, 3072, 1024], P('section', None, 'ep'), may hold values from -0.109375 to 0.109375
- wv: bfloat16 [16, 3072, 1024], P('section', None, 'ep'), may hold values from -0.109375 to 0.109375
- wo: bfloat16 [16, 4096, 3072], P('section', 'ep'), may hold values from -0.09375 to 0.09375
- router: bfloat16 [16, 3072, 8], P('section'), may hold values from -0.21875 to 0.21875
- w_gate: bfloat16 [16, 3072, 7168], P('section', None, 'ep'), may hold values from -0.109375 to 0.109375
- w_up: bfloat16 [16, 3072, 7168], P('section', None, 'ep'), may hold values from -0.109375 to 0.109375
- w_down: bfloat16 [16, 7168, 3072], P('section', 'ep'), may hold values from -0.125 to 0.125
- cache_k: bfloat16 [16, 2, 256, 8, 16, 128], P('section', None, 'ep'), may hold values from -127 to 127, as said below
- cache_v: bfloat16 [16, 2, 256, 8, 16, 128], P('section', None, 'ep'), may hold values from -127 to 127, as said below
- k_scale: float32 [16, 2, 256, 8, 4], P('section', None, 'ep'), may hold values from 0.004 to 2.4
- v_scale: float32 [16, 2, 256, 8, 4], P('section', None, 'ep'), may hold values from 0.004 to 0.04
Outputs:
- advanced: bfloat16 [4096, 3072], P(('section', 'ep'))
Inputs may be any that keep to these rules, and one draw needn't show every extreme that they name: `seq_lens`: each row holds 256 lengths; the longest is exactly 16. `routes`: the two ids of a token differ. In the rows of one device (aligned blocks of 16 tokens of a section and step) no expert is named by more than 8 tokens. `cache_k`: whole numbers. `cache_v`: whole numbers.
All inputs are finite; a program needn't handle non-finite values.
Results may differ from a plain program's by a relative error of at most 0.033.
Values may be sent and summed in bfloat16 or wider, within the bound.
No kernel may reach another device: no remote copies, remote signals or barrier semaphores. Data moves between devices by JAX's collectives and lax.ppermute only.
A program may use at most 128 MiB of HBM per device.

v0:
```python
import jax
import jax.numpy as jnp
from jax import lax
from jax.sharding import PartitionSpec as P

D = 3072
QH = 32
KVH = 8
HD = 128
EXPERTS = 8
EXP_WIN = 1
LEN = 16
BLK = 4
CAP = 8


rope_base = 1000000.0
norm_eps = 1e-05


def in_order(pieces, dim):
    pieces = jnp.moveaxis(pieces, 0, dim)
    lengths = pieces.shape
    return pieces.reshape(*lengths[:dim], lengths[dim] * lengths[dim + 1], *lengths[dim + 2 :])


def copy_for_each(value, axis):
    copies = jnp.broadcast_to(value, (lax.axis_size(axis), *value.shape))
    return lax.all_to_all(copies, axis, split_axis=0, concat_axis=0, tiled=True)


def gather_directly(value, axis, dim):
    return in_order(copy_for_each(value, axis), dim)


def shifted(value, axis, steps):
    count = lax.axis_size(axis)
    first, last = (max(0, -steps), min(count, count - steps))
    return lax.ppermute(value, axis, [(source, source + steps) for source in range(first, last)])


def rms_scale(values, gain_vec):
    wide = values.astype(jnp.float32)
    factor = lax.rsqrt(jnp.mean(wide * wide, axis=-1, keepdims=True) + norm_eps)
    return (wide * factor * gain_vec.astype(jnp.float32)).astype(jnp.bfloat16)


def rotate(head_vals, lengths_now):
    half_dim = head_vals.shape[-1] // 2
    inv_freq = rope_base ** (-jnp.arange(half_dim, dtype=jnp.float32) * 2.0 / head_vals.shape[-1])
    angles = lengths_now.astype(jnp.float32)[:, None, None] * inv_freq[None, None, :]
    cosine_vals = jnp.cos(angles)
    sine_table = jnp.sin(angles)
    wide = head_vals.astype(jnp.float32)
    lower_half = wide[..., :half_dim]
    upper_half = wide[..., half_dim:]
    turned = jnp.concatenate(
        [
            lower_half * cosine_vals - upper_half * sine_table,
            upper_half * cosine_vals + lower_half * sine_table,
        ],
        axis=-1,
    )
    return turned.astype(jnp.bfloat16)


def local(
    states,
    entering,
    seq_lens,
    routes,
    attn_norm,
    ffn_norm,
    wq,
    wk,
    wv,
    wo,
    router,
    w_gate,
    w_up,
    w_down,
    cache_k,
    cache_v,
    k_scale,
    v_scale,
):
    ep_size = lax.axis_size("ep")
    ep_index = lax.axis_index("ep")
    section_index = lax.axis_index("section")
    token_rows = states.shape[0]
    heads_here = QH // ep_size
    group_size = QH // KVH
    kv_cols = wk.shape[2]
    q_cols = heads_here * HD
    per_device = q_cols + 2 * kv_cols
    hidden_here = w_gate.shape[2]
    expert_width = hidden_here * ep_size // EXP_WIN
    experts_here = max(1, hidden_here // expert_width)
    ranks_per = max(1, expert_width // hidden_here)
    slot_count = ep_size * experts_here * CAP
    inverse_square_root = HD ** (-0.5)
    joined = jnp.concatenate([wq[0], wk[0], wv[0]], axis=1)
    gate_mat = w_gate[0].reshape(D, experts_here, hidden_here // experts_here)
    up_weight = w_up[0].reshape(D, experts_here, hidden_here // experts_here)
    down_mat = w_down[0].reshape(experts_here, hidden_here // experts_here, D)
    slot_expert = (
        jnp.arange(ep_size, dtype=jnp.int32)[:, None] * experts_here // ranks_per
        + jnp.arange(experts_here, dtype=jnp.int32)[None, :]
    )
    out_matrix = lax.all_to_all(wo[0], "ep", split_axis=1, concat_axis=0, tiled=True)

    def run_layer(layer_in, tick_index):
        all_lengths = lax.dynamic_index_in_dim(
            seq_lens, section_index + 1 - tick_index, 0, keepdims=False
        )
        lengths_now = lax.dynamic_slice_in_dim(all_lengths, ep_index * token_rows, token_rows, 0)
        normed = rms_scale(layer_in, attn_norm[0])
        projected = jnp.dot(
            gather_directly(normed, "ep", 0), joined, preferred_element_type=jnp.float32
        ).astype(jnp.bfloat16)
        arrived = lax.all_to_all(projected, "ep", split_axis=0, concat_axis=1, tiled=True).reshape(
            token_rows, ep_size, per_device
        )
        q_all = arrived[:, :, :q_cols].reshape(token_rows, QH, HD)
        fresh_key_rows = rotate(
            arrived[:, :, q_cols : q_cols + kv_cols].reshape(token_rows, KVH, HD), lengths_now
        )
        value_new = arrived[:, :, q_cols + kv_cols :].reshape(token_rows, KVH, HD)
        query_rows = rotate(q_all, lengths_now).reshape(token_rows, KVH, group_size, HD)
        key_codes = cache_k[0, tick_index]
        value_codes = cache_v[0, tick_index]
        key_scales = jnp.repeat(k_scale[0, tick_index], BLK, axis=-1)
        value_scales = jnp.repeat(v_scale[0, tick_index], BLK, axis=-1)
        raw_scores = jnp.einsum(
            "bkgd,bkpd->bkgp", query_rows, key_codes, preferred_element_type=jnp.float32
        )
        scores = raw_scores * key_scales[:, :, None, :] * inverse_square_root
        visible = (jnp.arange(LEN, dtype=jnp.int32)[None, :] < lengths_now[:, None])[
            :, None, None, :
        ]
        current_token_score = (
            jnp.einsum(
                "rwqs,rws->rwq", query_rows, fresh_key_rows, preferred_element_type=jnp.float32
            )
            * inverse_square_root
        )
        row_top = jnp.maximum(
            jnp.max(jnp.where(visible, scores, -1e30), axis=-1), current_token_score
        )
        exponent = jnp.where(visible, jnp.exp(scores - row_top[..., None]), 0.0)
        self_weight = jnp.exp(current_token_score - row_top)
        denom_sum = jnp.sum(exponent, axis=-1) + self_weight
        weights = (exponent * value_scales[:, :, None, :]).astype(jnp.bfloat16)
        mixture = jnp.einsum(
            "bkgp,bkpd->bkgd", weights, value_codes, preferred_element_type=jnp.float32
        )
        mixture = mixture + self_weight[..., None] * value_new.astype(jnp.float32)[:, :, None, :]
        attended = (
            (mixture / denom_sum[..., None]).astype(jnp.bfloat16).reshape(token_rows, QH * HD)
        )
        column_block = jnp.dot(
            gather_directly(attended, "ep", 0), out_matrix, preferred_element_type=jnp.float32
        )
        head_total = lax.all_to_all(column_block, "ep", split_axis=0, concat_axis=1, tiled=True)
        residual = (layer_in.astype(jnp.float32) + head_total).astype(jnp.bfloat16)
        ffn_input = rms_scale(residual, ffn_norm[0])
        logits = jnp.dot(ffn_input, router[0], preferred_element_type=jnp.float32)
        chosen = routes[0, tick_index]
        hit_table = chosen[:, :, None] == jnp.arange(EXPERTS, dtype=jnp.int32)[None, None, :]
        picked = jnp.sum(jnp.where(hit_table, logits[:, None, :], 0.0), axis=-1)
        gate_probs = jax.nn.softmax(picked, axis=-1)
        earlier = jnp.arange(token_rows)[:, None] > jnp.arange(token_rows)[None, :]
        same_expert = chosen[:, :, None, None] == chosen[None, None, :, :]
        slot_rank = jnp.sum(jnp.where(same_expert & earlier[:, None, :, None], 1, 0), axis=(2, 3))
        matches = (chosen[None, None, None, :, :] == slot_expert[:, :, None, None, None]) & (
            slot_rank[None, None, None]
            == jnp.arange(CAP, dtype=jnp.int32)[None, None, :, None, None]
        )
        selector = jnp.sum(jnp.where(matches, 1.0, 0.0), axis=-1).reshape(slot_count, token_rows)
        gate_table = jnp.sum(
            jnp.where(matches, gate_probs[None, None, None], 0.0), axis=-1
        ).reshape(slot_count, token_rows)
        output_rows = jnp.dot(
            selector.astype(jnp.bfloat16), ffn_input, preferred_element_type=jnp.float32
        ).astype(jnp.bfloat16)
        output_rows = output_rows.reshape(ep_size, experts_here, CAP, D)
        landed = lax.all_to_all(output_rows, "ep", split_axis=0, concat_axis=0, tiled=True)
        gate_act = jnp.einsum(
            "sjcd,djf->sjcf", landed, gate_mat, preferred_element_type=jnp.float32
        )
        up_act = jnp.einsum("sjcd,djf->sjcf", landed, up_weight, preferred_element_type=jnp.float32)
        hidden = (jax.nn.silu(gate_act) * up_act).astype(jnp.bfloat16)
        pieces = jnp.einsum("sjcf,jfd->sjcd", hidden, down_mat, preferred_element_type=jnp.float32)
        returned = lax.all_to_all(pieces, "ep", split_axis=0, concat_axis=0, tiled=True)
        expert_sum = jnp.dot(
            gate_table.T, returned.reshape(slot_count, D), preferred_element_type=jnp.float32
        )
        return (residual.astype(jnp.float32) + expert_sum).astype(jnp.bfloat16)

    first_out = run_layer(states, 0)
    shifted_rows = shifted(first_out, "section", 1)
    second_in = jnp.where(section_index == 0, entering, shifted_rows)
    return run_layer(second_in, 1)


def solution(mesh):
    return jax.shard_map(
        local,
        mesh=mesh,
        in_specs=(
            P(("section", "ep"), None),
            P("ep", None),
            P(),
            P("section", None, "ep", None),
            P("section", None),
            P("section", None),
            P("section", None, "ep"),
            P("section", None, "ep"),
            P("section", None, "ep"),
            P("section", "ep", None),
            P("section", None, None),
            P("section", None, "ep"),
            P("section", None, "ep"),
            P("section", "ep", None),
            P("section", None, "ep", None, None, None),
            P("section", None, "ep", None, None, None),
            P("section", None, "ep", None, None),
            P("section", None, "ep", None, None),
        ),
        out_specs=P(("section", "ep"), None),
        check_vma=False,
    )
```

profile of v0, /device:TPU:96, one launch (start us, length us, event | category | flops | bytes accessed | tf_op | source)
XLA Modules:
  0.0 307.9 jit_solution(7672398181482479959)
XLA Ops:
  0.0 0.9 mul.428
  0.9 1.0 fusion.84
  1.9 1.0 fusion.86
  2.9 1.3 broadcast_in_dim.160
  4.3 7.1 %all-to-all-start = ((bf16[16,16,3072]{2,1,0:T(8,128)(2,1)}), bf16[16,16,3072]{2,1,0:T(8,128)(2,1)}, u32[]{:S(2)}, u32[]{:S(2)}) async-start(bf16[16,16,3072]{2,1,0:T(8,128)(2,1)} %broadcast_in_dim.160), calls=%async_computation | async-start | bytes 3145728 | tf_op jit(solution)/shard_map/all_to_all | solution.py:29
  11.3 1.4 copy.103
  12.7 2.4 copy.104
  15.2 1.3 slice_bitcast_fusion.3
  16.5 0.6 broadcast_in_dim.161
  17.2 1.5 copy.107
  18.7 1.3 slice_bitcast_fusion
  20.0 0.6 broadcast_in_dim.164
  20.7 1.5 copy.110
  22.2 2.6 copy.112
  24.8 1.4 fusion.142
  26.2 0.7 multiply_cosine_fusion
  27.0 8.9 %all-to-all-done = bf16[16,16,3072]{2,1,0:T(8,128)(2,1)} async-done(((bf16[16,16,3072]{2,1,0:T(8,128)(2,1)}), bf16[16,16,3072]{2,1,0:T(8,128)(2,1)}, u32[]{:S(2)}, u32[]{:S(2)}) %all-to-all-start) | async-done | bytes 1572896 | tf_op jit(solution)/shard_map/all_to_all | solution.py:29
  35.9 3.8 %convolution_convert_fusion.3 = bf16[256,384]{1,0:T(8,128)(2,1)} fusion(bf16[256,3072]{1,0:T(8,128)(2,1)} %bitcast.2, bf16[3072,64]{1,0:T(8,128)(2,1)} %copy.104, bf16[3072,64]{1,0:T(8,128)(2,1)S(1)} %copy.103, bf16[3072,256]{1,0:T(8,128)(2,1)} %bitcast.265), kind=kOutput, calls=%fused_computation.26 | convolution fusion | flops 611155968 | bytes 4128768 | tf_op jit(solution)/shard_map/dot_general | solution.py:118
  39.7 3.5 %all-to-all-start.1 = ((bf16[16,16,384]{2,1,0:T(8,128)(2,1)}), bf16[16,16,384]{2,1,0:T(8,128)(2,1)S(1)}, u32[]{:S(2)}, u32[]{:S(2)}) async-start(bf16[16,16,384]{2,1,0:T(8,128)(2,1)} %bitcast.250), calls=%async_computation.1 | async-start | bytes 393216 | tf_op jit(solution)/shard_map/all_to_all | solution.py:121
  43.2 1.3 iota_compare_fusion.2
  44.6 7.0 %all-to-all-done.1 = bf16[16,16,384]{2,1,0:T(8,128)(2,1)S(1)} async-done(((bf16[16,16,384]{2,1,0:T(8,128)(2,1)}), bf16[16,16,384]{2,1,0:T(8,128)(2,1)S(1)}, u32[]{:S(2)}, u32[]{:S(2)}) %all-to-all-start.1) | async-done | bytes 196640 | tf_op jit(solution)/shard_map/all_to_all | solution.py:121
  51.5 4.4 %all-to-all-start.3 = ((bf16[256,16,192]{0,2,1:T(8,128)(2,1)}), bf16[256,16,192]{0,2,1:T(8,128)(2,1)}, u32[]{:S(2)}, u32[]{:S(2)}) async-start(bf16[256,16,192]{0,2,1:T(8,128)(2,1)} %bitcast.232), calls=%async_computation.3 | async-start | bytes 3145728 | tf_op jit(solution)/shard_map/all_to_all | solution.py:110
  56.0 0.7 slice_convert_fusion.4
  57.3 0.9 copy.111
  58.8 1.6 select_reduce_fusion.1
  61.5 16.3 %all-to-all-done.3 = bf16[256,16,192]{0,2,1:T(8,128)(2,1)} async-done(((bf16[256,16,192]{0,2,1:T(8,128)(2,1)}), bf16[256,16,192]{0,2,1:T(8,128)(2,1)}, u32[]{:S(2)}, u32[]{:S(2)}) %all-to-all-start.3) | async-done | bytes 1572896 | tf_op jit(solution)/shard_map/all_to_all | solution.py:110
  77.8 1.5 broadcast_in_dim.165
  79.4 4.6 %all-to-all-start.2 = ((bf16[16,16,4096]{2,1,0:T(8,128)(2,1)}), bf16[16,16,4096]{2,1,0:T(8,128)(2,1)}, u32[]{:S(2)}, u32[]{:S(2)}) async-start(bf16[16,16,4096]{2,1,0:T(8,128)(2,1)} %broadcast_in_dim.165), calls=%async_computation.2 | async-start | bytes 4194304 | tf_op jit(solution)/shard_map/all_to_all | solution.py:29
  84.2 0.7 broadcast_compare_fusion.1
  84.9 3.5 %copy.113 = bf16[16,256,192]{1,0,2:T(8,128)(2,1)} copy(bf16[16,256,192]{1,2,0:T(8,128)(2,1)} %bitcast.20) | data formatting | bytes 3145728 | tf_op jit(solution)/shard_map/all_to_all | solution.py:110
  88.4 3.8 %reshape.557 = bf16[4096,192,1]{0,1,2:T(8,128)(2,1)} reshape(bf16[16,256,192]{1,0,2:T(8,128)(2,1)} %copy.113) | data formatting | bytes 3145728 | tf_op jit(solution)/shard_map/all_to_all | solution.py:110
  92.2 19.2 %all-to-all-done.2 = bf16[16,16,4096]{2,1,0:T(8,128)(2,1)} async-done(((bf16[16,16,4096]{2,1,0:T(8,128)(2,1)}), bf16[16,16,4096]{2,1,0:T(8,128)(2,1)}, u32[]{:S(2)}, u32[]{:S(2)}) %all-to-all-start.2) | async-done | bytes 2097184 | tf_op jit(solution)/shard_map/all_to_all | solution.py:29
  111.4 3.5 %fusion.146 = f32[16,16,192]{2,1,0:T(8,128)} fusion(bf16[16,16,4096]{2,1,0:T(8,128)(2,1)} %all-to-all-done.2, bf16[4096,192,1]{0,1,2:T(8,128)(2,1)} %reshape.557), kind=kOutput, calls=%fused_computation.204 | convolution fusion | flops 402653184 | bytes 3866624 | tf_op jit(solution)/shard_map/dot_general | solution.py:161
  114.9 3.5 %all-to-all-start.4 = ((f32[16,16,192]{2,1,0:T(8,128)}), f32[16,16,192]{2,1,0:T(8,128)S(1)}, u32[]{:S(2)}, u32[]{:S(2)}) async-start(f32[16,16,192]{2,1,0:T(8,128)} %fusion.146), calls=%async_computation.4 | async-start | bytes 524288 | tf_op jit(solution)/shard_map/all_to_all | solution.py:164
  119.0 8.1 %all-to-all-done.4 = f32[16,16,192]{2,1,0:T(8,128)S(1)} async-done(((f32[16,16,192]{2,1,0:T(8,128)}), f32[16,16,192]{2,1,0:T(8,128)S(1)}, u32[]{:S(2)}, u32[]{:S(2)}) %all-to-all-start.4) | async-done | bytes 196640 | tf_op jit(solution)/shard_map/all_to_all | solution.py:164
  127.8 0.7 fusion.101
  128.9 15.2 %all_to_all.123 = bf16[16,1,8,3072]{3,2,1,0:T(8,128)(2,1)S(1)} all-to-all(bf16[16,1,8,3072]{3,2,1,0:T(8,128)(2,1)S(1)} %fusion), channel_id=1, replica_groups=mesh['section'=16,'ep'=16] {'ep'}, dimensions={0} | all-to-all | bytes 1572864 | tf_op jit(solution)/shard_map/all_to_all | solution.py:187
  144.1 3.4 %fusion.22 = f32[16,1,8,448]{3,2,0,1:T(8,128)} fusion(bf16[1,3072,448]{1,2,0:T(8,128)(2,1)} %param.29, bf16[16,1,8,3072]{3,2,1,0:T(8,128)(2,1)S(1)} %all_to_all.123), kind=kOutput, calls=%fused_computation.35 | convolution fusion | flops 352321536 | bytes 3768320 | tf_op jit(solution)/shard_map/sjcd,djf->sjcf/dot_general | solution.py:188
  147.5 4.3 %convolution_bitcast_fusion.1 = bf16[16,1,8,3072]{3,2,1,0:T(8,128)(2,1)} fusion(bf16[1,448,3072]{2,1,0:T(8,128)(2,1)S(1)} %copy-done, bf16[1,3072,448]{1,2,0:T(8,128)(2,1)} %param.30, bf16[16,1,8,3072]{3,2,1,0:T(8,128)(2,1)S(1)} %all_to_all.123, f32[16,1,8,448]{3,2,0,1:T(8,128)} %fusion.22), kind=kOutput, calls=%fused_computation.1 | convolution fusion | flops 704987136 | bytes 7307264 | tf_op jit(solution)/shard_map/sjcf,jfd->sjcd/dot_general | solution.py:193
  151.8 15.2 %all_to_all.124 = bf16[16,1,8,3072]{3,2,1,0:T(8,128)(2,1)S(1)} all-to-all(bf16[16,1,8,3072]{3,2,1,0:T(8,128)(2,1)} %convolution_bitcast_fusion.1), channel_id=1, replica_groups=mesh['section'=16,'ep'=16] {'ep'}, dimensions={0} | all-to-all | bytes 1572864 | tf_op jit(solution)/shard_map/all_to_all | solution.py:194
  167.1 1.2 fusion.4
  168.2 2.1 collective-permute-start
  170.3 3.8 %collective-permute-done = bf16[16,3072]{1,0:T(8,128)(2,1)S(1)} collective-permute-done((bf16[16,3072]{1,0:T(8,128)(2,1)S(1)}, bf16[16,3072]{1,0:T(8,128)(2,1)S(1)}, u32[]{:S(2)}, u32[]{:S(2)}) %collective-permute-start) | collective-permute-done | bytes 98336 | tf_op jit(solution)/shard_map/ppermute | solution.py:39
  175.3 26.9 %all_to_all.125 = bf16[16,16,3072]{2,1,0:T(8,128)(2,1)S(1)} all-to-all(bf16[16,16,3072]{2,1,0:T(8,128)(2,1)S(1)} %broadcast_in_dim.174), channel_id=1, replica_groups=mesh['section'=16,'ep'=16] {'ep'}, dimensions={0} | all-to-all | bytes 3145728 | tf_op jit(solution)/shard_map/all_to_all | solution.py:29
  202.2 1.8 convolution_convert_fusion.2
  204.0 3.5 %all-to-all-start.8 = ((bf16[16,16,384]{2,1,0:T(8,128)(2,1)}), bf16[16,16,384]{2,1,0:T(8,128)(2,1)S(1)}, u32[]{:S(2)}, u32[]{:S(2)}) async-start(bf16[16,16,384]{2,1,0:T(8,128)(2,1)} %bitcast.52), calls=%async_computation.8 | async-start | bytes 393216 | tf_op jit(solution)/shard_map/all_to_all | solution.py:121
  207.6 0.7 copy.121
  208.3 0.7 copy.124
  209.0 6.8 %all-to-all-done.8 = bf16[16,16,384]{2,1,0:T(8,128)(2,1)S(1)} async-done(((bf16[16,16,384]{2,1,0:T(8,128)(2,1)}), bf16[16,16,384]{2,1,0:T(8,128)(2,1)S(1)}, u32[]{:S(2)}, u32[]{:S(2)}) %all-to-all-start.8) | async-done | bytes 196640 | tf_op jit(solution)/shard_map/all_to_all | solution.py:121
  215.8 0.7 slice_convert_fusion.2
  216.9 0.8 subtract_convert_fusion.2
  217.8 0.9 subtract_convert_fusion
  219.1 1.6 select_reduce_fusion
  220.7 1.1 fusion.99
  221.9 1.6 fusion.40
  223.9 30.8 %all_to_all.126 = bf16[16,16,4096]{2,1,0:T(8,128)(2,1)S(1)} all-to-all(bf16[16,16,4096]{2,1,0:T(8,128)(2,1)S(1)} %broadcast_in_dim.177), channel_id=1, replica_groups=mesh['section'=16,'ep'=16] {'ep'}, dimensions={0} | all-to-all | bytes 4194304 | tf_op jit(solution)/shard_map/all_to_all | solution.py:29
  254.7 0.7 fusion.147
  255.4 11.6 %all_to_all.127 = f32[16,16,192]{2,1,0:T(8,128)S(1)} all-to-all(f32[16,16,192]{2,1,0:T(8,128)S(1)} %fusion.147), channel_id=1, replica_groups=mesh['section'=16,'ep'=16] {'ep'}, dimensions={0} | all-to-all | bytes 393216 | tf_op jit(solution)/shard_map/all_to_all | solution.py:164
  267.8 0.7 fusion.103
  268.8 14.4 %all_to_all.128 = bf16[16,1,8,3072]{3,2,1,0:T(8,128)(2,1)S(1)} all-to-all(bf16[16,1,8,3072]{3,2,1,0:T(8,128)(2,1)S(1)} %fusion.1), channel_id=1, replica_groups=mesh['section'=16,'ep'=16] {'ep'}, dimensions={0} | all-to-all | bytes 1572864 | tf_op jit(solution)/shard_map/all_to_all | solution.py:187
  283.2 3.4 %fusion.25 = f32[16,1,8,448]{3,2,0,1:T(8,128)} fusion(bf16[1,3072,448]{1,2,0:T(8,128)(2,1)} %param.29, bf16[16,1,8,3072]{3,2,1,0:T(8,128)(2,1)S(1)} %all_to_all.128), kind=kOutput, calls=%fused_computation.36 | convolution fusion | flops 352321536 | bytes 3768320 | tf_op jit(solution)/shard_map/sjcd,djf->sjcf/dot_general | solution.py:188
  286.7 4.3 %convolution_bitcast_fusion = bf16[16,1,8,3072]{3,2,1,0:T(8,128)(2,1)} fusion(bf16[1,448,3072]{2,1,0:T(8,128)(2,1)S(1)} %copy-done, bf16[1,3072,448]{1,2,0:T(8,128)(2,1)} %param.30, bf16[16,1,8,3072]{3,2,1,0:T(8,128)(2,1)S(1)} %all_to_all.128, f32[16,1,8,448]{3,2,0,1:T(8,128)} %fusion.25), kind=kOutput, calls=%fused_computation | convolution fusion | flops 704987136 | bytes 7307264 | tf_op jit(solution)/shard_map/sjcf,jfd->sjcd/dot_general | solution.py:193
  291.0 15.1 %all_to_all.129 = bf16[16,1,8,3072]{3,2,1,0:T(8,128)(2,1)S(1)} all-to-all(bf16[16,1,8,3072]{3,2,1,0:T(8,128)(2,1)} %convolution_bitcast_fusion), channel_id=1, replica_groups=mesh['section'=16,'ep'=16] {'ep'}, dimensions={0} | all-to-all | bytes 1572864 | tf_op jit(solution)/shard_map/all_to_all | solution.py:194
  306.1 1.8 fusion.5
  (118 shorter events, 7.6 us)
Async XLA Ops:
  0.0 147.5 %copy-start = (bf16[1,448,3072]{2,1,0:T(8,128)(2,1)S(1)}, bf16[1,448,3072]{2,1,0:T(8,128)(2,1)}, u32[]{:S(2)}) copy-start(bf16[1,448,3072]{2,1,0:T(8,128)(2,1)} %param.31) | copy-start | bytes 8257540
  0.9 1.1 copy-start.11
  4.3 31.6 %all-to-all-start = ((bf16[16,16,3072]{2,1,0:T(8,128)(2,1)}), bf16[16,16,3072]{2,1,0:T(8,128)(2,1)}, u32[]{:S(2)}, u32[]{:S(2)}) async-start(bf16[16,16,3072]{2,1,0:T(8,128)(2,1)} %broadcast_in_dim.160), calls=%async_computation | async-start | bytes 3145728 | tf_op jit(solution)/shard_map/all_to_all | solution.py:29
  12.7 23.1 %copy-start.7 = (bf16[3072,64]{1,0:T(8,128)(2,1)}, bf16[3072,64]{1,0:T(8,128)(2,1)S(1)}, u32[]{:S(2)}) copy-start(bf16[3072,64]{1,0:T(8,128)(2,1)S(1)} %copy.103) | copy-start | bytes 1179652
  39.7 11.8 %all-to-all-start.1 = ((bf16[16,16,384]{2,1,0:T(8,128)(2,1)}), bf16[16,16,384]{2,1,0:T(8,128)(2,1)S(1)}, u32[]{:S(2)}, u32[]{:S(2)}) async-start(bf16[16,16,384]{2,1,0:T(8,128)(2,1)} %bitcast.250), calls=%async_computation.1 | async-start | bytes 393216 | tf_op jit(solution)/shard_map/all_to_all | solution.py:121
  51.5 26.3 %all-to-all-start.3 = ((bf16[256,16,192]{0,2,1:T(8,128)(2,1)}), bf16[256,16,192]{0,2,1:T(8,128)(2,1)}, u32[]{:S(2)}, u32[]{:S(2)}) async-start(bf16[256,16,192]{0,2,1:T(8,128)(2,1)} %bitcast.232), calls=%async_computation.3 | async-start | bytes 3145728 | tf_op jit(solution)/shard_map/all_to_all | solution.py:110
  57.0 3.4 %copy-start.19 = (pred[16,16]{1,0:T(8,128)(4,1)S(1)}, pred[16,16]{1,0:T(8,128)(4,1)}, u32[]{:S(2)}) copy-start(pred[16,16]{1,0:T(8,128)(4,1)} %get-tuple-element.60) | copy-start | bytes 772
  57.1 3.8 %copy-start.14 = (f32[16,8,16]{2,1,0:T(8,128)S(1)}, f32[16,8,16]{2,1,0:T(8,128)}, u32[]{:S(2)}) copy-start(f32[16,8,16]{2,1,0:T(8,128)} %copy.110) | copy-start | bytes 24580
  58.4 2.5 copy-start.23
  79.3 4.6 %copy-start.18 = (bf16[1,3072]{1,0:T(2,128)(2,1)S(1)}, bf16[1,3072]{1,0:T(2,128)(2,1)}, u32[]{:S(2)}) copy-start(bf16[1,3072]{1,0:T(2,128)(2,1)} %param.23) | copy-start | bytes 18436
  79.4 4.6 %copy-start.21 = (s32[1,2,16,2]{2,3,1,0:T(2,128)S(1)}, s32[1,2,16,2]{2,3,1,0:T(2,128)}, u32[]{:S(2)}) copy-start(s32[1,2,16,2]{2,3,1,0:T(2,128)} %param.21) | copy-start | bytes 772
  79.4 32.0 %all-to-all-start.2 = ((bf16[16,16,4096]{2,1,0:T(8,128)(2,1)}), bf16[16,16,4096]{2,1,0:T(8,128)(2,1)}, u32[]{:S(2)}, u32[]{:S(2)}) async-start(bf16[16,16,4096]{2,1,0:T(8,128)(2,1)} %broadcast_in_dim.165), calls=%async_computation.2 | async-start | bytes 4194304 | tf_op jit(solution)/shard_map/all_to_all | solution.py:29
  92.1 35.2 %copy-start.2 = (bf16[16,3072]{1,0:T(8,128)(2,1)S(1)}, bf16[16,3072]{1,0:T(8,128)(2,1)}, u32[]{:S(2)}) copy-start(bf16[16,3072]{1,0:T(8,128)(2,1)} %param.18) | copy-start | bytes 294916
  92.2 35.4 %copy-start.24 = (bf16[1,3072,8]{1,2,0:T(8,128)(2,1)S(1)}, bf16[1,3072,8]{1,2,0:T(8,128)(2,1)}, u32[]{:S(2)}) copy-start(bf16[1,3072,8]{1,2,0:T(8,128)(2,1)} %param.28) | copy-start | bytes 147460
  114.9 12.2 %all-to-all-start.4 = ((f32[16,16,192]{2,1,0:T(8,128)}), f32[16,16,192]{2,1,0:T(8,128)S(1)}, u32[]{:S(2)}, u32[]{:S(2)}) async-start(f32[16,16,192]{2,1,0:T(8,128)} %fusion.146), calls=%async_computation.4 | async-start | bytes 524288 | tf_op jit(solution)/shard_map/all_to_all | solution.py:164
  127.5 1.0 copy-start.6
  151.8 22.3 %copy-start.13 = (bf16[16,3072]{1,0:T(8,128)(2,1)S(1)}, bf16[16,3072]{1,0:T(8,128)(2,1)}, u32[]{:S(2)}) copy-start(bf16[16,3072]{1,0:T(8,128)(2,1)} %param.19) | copy-start | bytes 294916
  151.8 23.1 %copy-start.12 = (f32[1,3072]{1,0:T(1,128)S(1)}, f32[1,3072]{1,0:T(1,128)}, u32[]{:S(2)}) copy-start(f32[1,3072]{1,0:T(1,128)} %copy-done.11) | copy-start | bytes 36868
  168.2 5.9 %collective-permute-start = (bf16[16,3072]{1,0:T(8,128)(2,1)S(1)}, bf16[16,3072]{1,0:T(8,128)(2,1)S(1)}, u32[]{:S(2)}, u32[]{:S(2)}) collective-permute-start(bf16[16,3072]{1,0:T(8,128)(2,1)S(1)} %fusion.4), channel_id=1, source_target_pairs={{0,16},{16,32},{32,48},{48,64},{64,80},{80,96},{96,112},{112,128},... | collective-permute-start | bytes 294920 | tf_op jit(solution)/shard_map/ppermute | solution.py:39
  174.3 0.6 copy-start.3
  175.1 27.2 %copy-start.8 = (bf16[3072,64]{1,0:T(8,128)(2,1)S(1)}, bf16[3072,64]{1,0:T(8,128)(2,1)}, u32[]{:S(2)}) copy-start(bf16[3072,64]{1,0:T(8,128)(2,1)} %copy-done.7) | copy-start | bytes 1179652
  175.1 27.1 %copy-start.9 = (bf16[3072,64]{1,0:T(8,128)(2,1)S(1)}, bf16[3072,64]{1,0:T(8,128)(2,1)}, u32[]{:S(2)}) copy-start(bf16[3072,64]{1,0:T(8,128)(2,1)} %copy.104) | copy-start | bytes 1179652
  175.1 27.1 %copy-start.22 = (bf16[1,3072,256]{2,1,0:T(8,128)(2,1)S(1)}, bf16[1,3072,256]{2,1,0:T(8,128)(2,1)}, u32[]{:S(2)}) copy-start(bf16[1,3072,256]{2,1,0:T(8,128)(2,1)} %param.24) | copy-start | bytes 4718596
  202.2 5.3 %copy-start.15 = (f32[16,8,4]{0,2,1:T(4,128)S(1)}, f32[16,8,4]{0,2,1:T(4,128)}, u32[]{:S(2)}) copy-start(f32[16,8,4]{0,2,1:T(4,128)} %get-tuple-element.40) | copy-start | bytes 6148
  202.2 6.1 %copy-start.16 = (f32[16,8,4]{0,2,1:T(4,128)S(1)}, f32[16,8,4]{0,2,1:T(4,128)}, u32[]{:S(2)}) copy-start(f32[16,8,4]{0,2,1:T(4,128)} %get-tuple-element.37) | copy-start | bytes 6148
  204.0 11.8 %all-to-all-start.8 = ((bf16[16,16,384]{2,1,0:T(8,128)(2,1)}), bf16[16,16,384]{2,1,0:T(8,128)(2,1)S(1)}, u32[]{:S(2)}, u32[]{:S(2)}) async-start(bf16[16,16,384]{2,1,0:T(8,128)(2,1)} %bitcast.52), calls=%async_computation.8 | async-start | bytes 393216 | tf_op jit(solution)/shard_map/all_to_all | solution.py:121
  216.9 4.9 %copy-start.10 = (f32[16,16,64]{2,0,1:T(8,128)S(1)}, f32[16,16,64]{2,0,1:T(8,128)}, u32[]{:S(2)}) copy-start(f32[16,16,64]{2,0,1:T(8,128)} %get-tuple-element.29) | copy-start | bytes 196612
  223.9 30.8 %copy-start.1 = (bf16[4096,192,1]{0,1,2:T(8,128)(2,1)S(1)}, bf16[4096,192,1]{0,1,2:T(8,128)(2,1)}, u32[]{:S(2)}) copy-start(bf16[4096,192,1]{0,1,2:T(8,128)(2,1)} %reshape.557) | copy-start | bytes 4718596
  254.7 12.6 %copy-start.4 = (bf16[16,3072]{1,0:T(8,128)(2,1)S(1)}, bf16[16,3072]{1,0:T(8,128)(2,1)}, u32[]{:S(2)}) copy-start(bf16[16,3072]{1,0:T(8,128)(2,1)} %copy-done.3) | copy-start | bytes 294916
  254.7 12.8 %copy-start.25 = (bf16[1,3072,8]{1,2,0:T(8,128)(2,1)S(1)}, bf16[1,3072,8]{1,2,0:T(8,128)(2,1)}, u32[]{:S(2)}) copy-start(bf16[1,3072,8]{1,2,0:T(8,128)(2,1)} %param.28) | copy-start | bytes 147460
  254.7 13.1 %copy-start.17 = (pred[16,16,2]{1,2,0:T(4,128)(4,1)S(1)}, pred[16,16,2]{1,2,0:T(4,128)(4,1)}, u32[]{:S(2)}) copy-start(pred[16,16,2]{1,2,0:T(4,128)(4,1)} %get-tuple-element.52) | copy-start | bytes 1540
  254.7 13.1 %copy-start.20 = (pred[8,16,2]{1,0,2:T(8,128)(4,1)S(1)}, pred[8,16,2]{1,0,2:T(8,128)(4,1)}, u32[]{:S(2)}) copy-start(pred[8,16,2]{1,0,2:T(8,128)(4,1)} %get-tuple-element.57) | copy-start | bytes 772
  267.4 1.0 copy-start.5
where the time goes:
time: 310 us; the launch traced here: 308 us
  blocking collectives  129 us (42%)
  waiting for transfers between devices  70.1 us (23%)
  matrix products  35.5 us (11%)
  starting transfers between devices  28.7 us (9%)
  local copies, waits for them, and re-layouts  28.6 us (9%)
  other arithmetic  15.1 us (5%)
    all_to_all x2, blocking collectives, copy_for_each(): return lax.all_to_all(copies, axis, split_axis=0, concat_axis=0, tiled=True)  57.7 us
    all_to_all x2, blocking collectives, run_layer(): lax.all_to_all(pieces, 'ep', split_axis=0, concat_axis=0, tiled=True)  30.3 us
    all_to_all x2, blocking collectives, run_layer(): lax.all_to_all(output_rows, 'ep', split_axis=0, concat_axis=0, tiled=True)  29.6 us
    all_to_all x2, waiting for transfers between devices, copy_for_each(): return lax.all_to_all(copies, axis, split_axis=0, concat_axis=0, tiled=True)  28.1 us
    all_to_all x1, waiting for transfers between devices, local(): lax.all_to_all(wo[0], 'ep', split_axis=1, concat_axis=0, tiled=True)  16.3 us
    all_to_all x2, waiting for transfers between devices, run_layer(): lax.all_to_all(projected, 'ep', split_axis=0, concat_axis=1, tiled=True)  13.8 us
    all_to_all x2, starting transfers between devices, copy_for_each(): return lax.all_to_all(copies, axis, split_axis=0, concat_axis=0, tiled=True)  11.6 us
    all_to_all x1, blocking collectives, run_layer(): lax.all_to_all(column_block, 'ep', split_axis=0, concat_axis=1, tiled=True)  11.6 us
  transfers between devices with their start and end apart: 7, of which 7 were waited for; matrix products, arithmetic and copies ran while one was open for 11% of the time, Pallas kernels for 0%

commit v1 on v0

v1 whole, which is shorter than its diff:
```python
import functools

import jax
import jax.numpy as jnp
from jax import lax
from jax.experimental import pallas as pl
from jax.experimental.pallas import tpu as pltpu
from jax.sharding import PartitionSpec as P

D = 3072
QH = 32
KVH = 8
HD = 128
EXPERTS = 8
EXP_WIN = 1
LEN = 16
BLK = 4
CAP = 8
EP = 16
TOK = 16
CHUNK = 512

rope_base = 1000000.0
norm_eps = 1e-05
f32 = jnp.float32
bf16 = jnp.bfloat16


def call(body, out_shape, n_in, smem=(), name=None, scratch=()):
    specs = [
        pl.BlockSpec(memory_space=pltpu.SMEM if i in smem else pltpu.VMEM) for i in range(n_in)
    ]
    outs = jax.tree.map(lambda _: pl.BlockSpec(memory_space=pltpu.VMEM), out_shape)
    return pl.pallas_call(
        body,
        out_shape=out_shape,
        in_specs=specs,
        out_specs=outs,
        scratch_shapes=list(scratch),
        compiler_params=pltpu.CompilerParams(vmem_limit_bytes=48 << 20),
        name=name,
    )


def columns():
    return [slice(c, c + CHUNK) for c in range(0, D, CHUNK)]


def spread_normed(x_ref, gain_ref, copies_ref):
    total = jnp.zeros((TOK, 1), f32)
    for cols in columns():
        wide = x_ref[:, cols].astype(f32)
        total = total + jnp.sum(wide * wide, axis=-1, keepdims=True)
    factor = lax.rsqrt(total / D + norm_eps)
    for cols in columns():
        wide = x_ref[:, cols].astype(f32)
        rows = (wide * factor * gain_ref[:, cols].astype(f32)).astype(bf16)
        for dest in range(EP):
            copies_ref[dest, :, cols] = rows


def norm_body(x_ref, gain_ref, copies_ref):
    spread_normed(x_ref, gain_ref, copies_ref)


def norm_select_body(first_ref, entering_ref, shifted_ref, gain_ref, x_ref, copies_ref):
    is_first = first_ref[0] == 1

    @pl.when(is_first)
    def _():
        x_ref[...] = entering_ref[...]

    @pl.when(jnp.logical_not(is_first))
    def _():
        x_ref[...] = shifted_ref[...]

    spread_normed(x_ref, gain_ref, copies_ref)


def project_body(x_ref, wq_ref, wk_ref, wv_ref, out_ref):
    x = x_ref[...]
    out_ref[:, 0:256] = jnp.dot(x, wq_ref[...], preferred_element_type=f32).astype(bf16)
    key = jnp.dot(x, wk_ref[...], preferred_element_type=f32)
    value = jnp.dot(x, wv_ref[...], preferred_element_type=f32)
    out_ref[:, 256:384] = jnp.concatenate([key, value], axis=-1).astype(bf16)


def attention_body(
    tick, got_ref, lens_ref, cos_ref, sin_ref, ks_ref, vs_ref, key_ref, value_ref, out_ref
):
    scale = HD ** (-0.5)
    group = QH // KVH
    pos = TOK * LEN
    lane = lax.broadcasted_iota(jnp.int32, (TOK, HD), 1)
    low = lane < HD // 2
    cos_vals = cos_ref[...]
    sin_vals = sin_ref[...]

    def turned(rows):
        return (rows * cos_vals + pltpu.roll(rows, HD // 2, 1) * sin_vals).astype(bf16)

    blocks = KVH * LEN // BLK
    which = lax.broadcasted_iota(jnp.int32, (blocks, KVH * pos), 0)
    at = lax.broadcasted_iota(jnp.int32, (blocks, KVH * pos), 1)
    per_head = LEN // BLK
    spread = jnp.where(
        (which // per_head == at // pos) & (which % per_head == (at % LEN) // BLK), 1.0, 0.0
    ).astype(f32)
    k_all = jnp.dot(
        ks_ref[...], spread, preferred_element_type=f32, precision=lax.Precision.HIGHEST
    )
    v_all = jnp.dot(
        vs_ref[...], spread, preferred_element_type=f32, precision=lax.Precision.HIGHEST
    )
    row = lax.broadcasted_iota(jnp.int32, (TOK, pos), 0)
    col = lax.broadcasted_iota(jnp.int32, (TOK, pos), 1)
    live_one = (col // LEN == row) & (col % LEN < lens_ref[...][:, 0:1])
    live = jnp.concatenate([live_one.astype(f32)] * group, axis=0) > 0.5
    for g in range(KVH):
        first = got_ref[2 * g, :, 256:384].astype(f32)
        second = got_ref[2 * g + 1, :, 256:384].astype(f32)
        key_new = turned(jnp.where(low, first, pltpu.roll(second, HD // 2, 1))).astype(f32)
        value_new = jnp.where(low, pltpu.roll(first, HD // 2, 1), second)
        q = jnp.concatenate(
            [
                turned(got_ref[2 * g + r // 2, :, (r % 2) * HD : (r % 2 + 1) * HD].astype(f32))
                for r in range(group)
            ],
            axis=0,
        )
        keys = key_ref[0, tick, :, g].reshape(pos, HD)
        values = value_ref[0, tick, :, g].reshape(pos, HD)
        k_scale = jnp.concatenate([k_all[:, g * pos : (g + 1) * pos]] * group, axis=0)
        v_scale = jnp.concatenate([v_all[:, g * pos : (g + 1) * pos]] * group, axis=0)
        raw = lax.dot_general(q, keys, (((1,), (1,)), ((), ())), preferred_element_type=f32)
        scores = raw * k_scale * scale
        own = (
            jnp.sum(
                q.astype(f32) * jnp.concatenate([key_new] * group, axis=0), axis=-1, keepdims=True
            )
            * scale
        )
        top = jnp.maximum(jnp.max(jnp.where(live, scores, -1e30), axis=-1, keepdims=True), own)
        e = jnp.where(live, jnp.exp(jnp.where(live, scores, -1e30) - top), 0.0)
        e_own = jnp.exp(own - top)
        denom = jnp.sum(e, axis=-1, keepdims=True) + e_own
        weight = jnp.where(live, e * v_scale, 0.0).astype(bf16)
        mixed = jnp.dot(weight, values, preferred_element_type=f32)
        mixed = mixed + e_own * jnp.concatenate([value_new] * group, axis=0)
        done = (mixed / denom).astype(bf16)
        for r in range(group):
            out_ref[2 * g + r // 2, :, (r % 2) * HD : (r % 2 + 1) * HD] = done[
                r * TOK : (r + 1) * TOK
            ]


def out_body(att_ref, wo_ref, part_ref):
    part_ref[...] = jnp.dot(att_ref[...], wo_ref[0], preferred_element_type=f32).astype(bf16)


def residual_body(
    x_ref, got_ref, gain_ref, router_ref, chosen_ref, sel_ref, sel_t_ref, res_ref, copies_ref, coef_ref, ffn_ref
):
    total = jnp.zeros((TOK, 1), f32)
    for cols in columns():
        acc = got_ref[0, :, cols].astype(f32)
        for src in range(1, EP):
            acc = acc + got_ref[src, :, cols].astype(f32)
        rounded = (x_ref[:, cols].astype(f32) + acc).astype(bf16)
        res_ref[:, cols] = rounded
        wide = rounded.astype(f32)
        total = total + jnp.sum(wide * wide, axis=-1, keepdims=True)
    factor = lax.rsqrt(total / D + norm_eps)
    for cols in columns():
        wide = res_ref[:, cols].astype(f32)
        rows = (wide * factor * gain_ref[:, cols].astype(f32)).astype(bf16)
        ffn_ref[:, cols] = rows
        slots = jnp.dot(sel_ref[...], rows, preferred_element_type=f32).astype(bf16)
        for dest in range(EP):
            copies_ref[dest, :, cols] = slots
    logits = jnp.dot(ffn_ref[...], router_ref[0], preferred_element_type=f32)
    expert = lax.broadcasted_iota(jnp.int32, (TOK, EXPERTS), 1)
    one = chosen_ref[:, 0:1]
    two = chosen_ref[:, 1:2]
    pick_one = jnp.sum(jnp.where(expert == one, logits, 0.0), axis=-1, keepdims=True)
    pick_two = jnp.sum(jnp.where(expert == two, logits, 0.0), axis=-1, keepdims=True)
    top = jnp.maximum(pick_one, pick_two)
    e_one = jnp.exp(pick_one - top)
    e_two = jnp.exp(pick_two - top)
    both = e_one + e_two
    share = jnp.where(one == 0, e_one / both, 0.0) + jnp.where(two == 0, e_two / both, 0.0)
    coef_ref[...] = share * sel_t_ref[...]


def expert_body(x_ref, gate_ref, up_ref, down_ref, part_ref):
    x = x_ref[...]
    gate = jnp.dot(x, gate_ref[0], preferred_element_type=f32)
    up = jnp.dot(x, up_ref[0], preferred_element_type=f32)
    hidden = (gate * jax.nn.sigmoid(gate) * up).astype(bf16)
    part_ref[...] = jnp.dot(hidden, down_ref[0], preferred_element_type=f32).astype(bf16)


def combine_body(res_ref, coef_ref, got_ref, out_ref):
    coef = coef_ref[...]
    for cols in columns():
        acc = got_ref[0, :, cols].astype(f32)
        for src in range(1, EP):
            acc = acc + got_ref[src, :, cols].astype(f32)
        total = res_ref[:, cols].astype(f32)
        for k in range(CAP):
            total = total + coef[:, k : k + 1] * acc[k : k + 1, :]
        out_ref[:, cols] = total.astype(bf16)


def sds(shape, dtype):
    return jax.ShapeDtypeStruct(shape, dtype)


def trade(pieces):
    return lax.all_to_all(pieces, "ep", split_axis=0, concat_axis=0, tiled=True)


def local(
    states,
    entering,
    seq_lens,
    routes,
    attn_norm,
    ffn_norm,
    wq,
    wk,
    wv,
    wo,
    router,
    w_gate,
    w_up,
    w_down,
    cache_k,
    cache_v,
    k_scale,
    v_scale,
):
    ep_index = lax.axis_index("ep")
    section_index = lax.axis_index("section")
    lens = lax.dynamic_slice(seq_lens, (section_index, ep_index * TOK), (2, TOK))[::-1]
    half = HD // 2
    inv_freq = rope_base ** (-jnp.arange(half, dtype=f32) * 2.0 / HD)
    angles = lens.astype(f32)[:, :, None] * inv_freq
    cos_vals = jnp.cos(angles)
    sin_vals = jnp.sin(angles)
    cos_vals = jnp.concatenate([cos_vals, cos_vals], axis=-1)
    sin_vals = jnp.concatenate([-sin_vals, sin_vals], axis=-1)
    lens_rows = jnp.broadcast_to(lens[:, :, None], (2, TOK, HD))
    ks = k_scale[0].reshape(2, TOK, KVH * LEN // BLK)
    vs = v_scale[0].reshape(2, TOK, KVH * LEN // BLK)
    held = jnp.any(routes[0] == 0, axis=-1)
    before = jnp.arange(TOK)[:, None] > jnp.arange(TOK)[None, :]
    rank = jnp.sum(jnp.where(before & held[:, None, :], 1, 0), axis=-1)
    slot = jnp.arange(CAP, dtype=jnp.int32)
    sel = (held[:, None, :] & (rank[:, None, :] == slot[:, None])).astype(bf16)
    sel_t = (held[:, :, None] & (rank[:, :, None] == slot)).astype(f32)
    sel_t = jnp.pad(sel_t, ((0, 0), (0, 0), (0, HD - CAP)))

    def run_layer(x, copies, tick):
        everyone = trade(copies).reshape(EP * TOK, D)
        projected = call(project_body, sds((EP * TOK, 384), bf16), 4, name="project")(
            everyone, wq[0], wk[0], wv[0]
        )
        got = trade(projected.reshape(EP, TOK, 384))
        attended = call(
            functools.partial(attention_body, tick), sds((EP, TOK, 256), bf16), 8, name="attend"
        )(got, lens_rows[tick], cos_vals[tick], sin_vals[tick], ks[tick], vs[tick], cache_k, cache_v)
        heads = trade(attended).reshape(EP * TOK, 256)
        part = call(out_body, sds((EP * TOK, D), bf16), 2, name="outproj")(heads, wo)
        sums = trade(part.reshape(EP, TOK, D))
        residual, slots, coef = call(
            residual_body,
            (sds((TOK, D), bf16), sds((EP, CAP, D), bf16), sds((TOK, HD), f32)),
            7,
            name="residual",
            scratch=[pltpu.VMEM((TOK, D), bf16)],
        )(x, sums, ffn_norm, router, routes[0, tick], sel[tick], sel_t[tick])
        landed = trade(slots).reshape(EP * CAP, D)
        pieces = call(expert_body, sds((EP * CAP, D), bf16), 4, name="expert")(
            landed, w_gate, w_up, w_down
        )
        returned = trade(pieces.reshape(EP, CAP, D))
        return call(combine_body, sds((TOK, D), bf16), 3, name="combine")(
            residual, coef, returned
        )

    copies = call(norm_body, sds((EP, TOK, D), bf16), 2, name="norm")(states, attn_norm)
    first_out = run_layer(states, copies, 0)
    count = lax.axis_size("section")
    shifted = lax.ppermute(first_out, "section", [(i, i + 1) for i in range(count - 1)])
    is_first = (section_index == 0).astype(jnp.int32).reshape(1)
    second_in, copies = call(
        norm_select_body,
        (sds((TOK, D), bf16), sds((EP, TOK, D), bf16)),
        4,
        smem=(0,),
        name="select_norm",
    )(is_first, entering, shifted, attn_norm)
    return run_layer(second_in, copies, 1)


def solution(mesh):
    return jax.shard_map(
        local,
        mesh=mesh,
        in_specs=(
            P(("section", "ep"), None),
            P("ep", None),
            P(),
            P("section", None, "ep", None),
            P("section", None),
            P("section", None),
            P("section", None, "ep"),
            P("section", None, "ep"),
            P("section", None, "ep"),
            P("section", "ep", None),
            P("section", None, None),
            P("section", None, "ep"),
            P("section", None, "ep"),
            P("section", "ep", None),
            P("section", None, "ep", None, None, None),
            P("section", None, "ep", None, None, None),
            P("section", None, "ep", None, None),
            P("section", None, "ep", None, None),
        ),
        out_specs=P(("section", "ep"), None),
        check_vma=False,
    )
```

time: 310 us -> 273 us (0.88)
  matrix products: 35.5 us -> 0 us
  blocking collectives: 129 us -> 96.6 us
  Pallas kernels: 0 us -> 25.9 us
  other arithmetic: 15.1 us -> 2.33 us
  waiting for transfers between devices: 70.1 us -> 79.4 us
  local copies, waits for them, and re-layouts: 28.6 us -> 37.9 us
    dot_general x20 -> x0, matrix products: 35.5 us -> none  [the longest x2 8.6 us: run_layer(): jnp.einsum('sjcf,jfd->sjcd', hidden, down_mat, preferred_element_type=jnp...]
    all_to_all x7 -> x6, blocking collectives: 129 us -> 96.6 us  [trade(): return lax.all_to_all(pieces, 'ep', split_axis=0, concat_axis=0, tiled=True)]
    unnamed x53 -> x87, local copies, waits for them, and re-layouts: 3.31 us -> 30.2 us
    pallas_call x0 -> x14, Pallas kernels: none -> 25.9 us  [the longest x2 8.92 us: run_layer(): call(expert_body, sds((EP * CAP, D), bf16), 4, name='expert')]
    all_to_all x6, waiting for transfers between devices: 66.3 us -> 75.1 us  [trade(): return lax.all_to_all(pieces, 'ep', split_axis=0, concat_axis=0, tiled=True)]
    all_to_all x6 -> x0, local copies, waits for them, and re-layouts: 7.8 us -> none  [the longest x2 7.24 us: local(): lax.all_to_all(wo[0], 'ep', split_axis=1, concat_axis=0, tiled=True)]
    mul x4 -> x0, local copies, waits for them, and re-layouts: 4.51 us -> none  [the longest x2 2.26 us: run_layer(): scores = raw_scores * key_scales[:, :, None, :] * inverse_square_root]
    reduce_sum x13 -> x1, other arithmetic: 4.57 us -> 0.12 us  [local(): rank = jnp.sum(jnp.where(before & held[:, None, :], 1, 0), axis=-1)]
  transfers between devices with their start and end apart: 7 -> 7, of which waited for: 7 -> 7; matrix products, arithmetic and copies ran while one was open for 11% -> 7% of each run, Pallas kernels for 0% -> 0%
where the time goes in v1:
time: 273 us; the launch traced here: 272 us
  blocking collectives  96.6 us (35%)
  waiting for transfers between devices  79.4 us (29%)
  local copies, waits for them, and re-layouts  37.9 us (14%)
  starting transfers between devices  29.1 us (11%)
  Pallas kernels  25.9 us (9%)
    all_to_all x6, blocking collectives, trade(): return lax.all_to_all(pieces, 'ep', split_axis=0, concat_axis=0, tiled=True)  96.6 us
    all_to_all x6, waiting for transfers between devices, trade(): return lax.all_to_all(pieces, 'ep', split_axis=0, concat_axis=0, tiled=True)  75.1 us
    unnamed x87, local copies, waits for them, and re-layouts  30.2 us
    all_to_all x6, starting transfers between devices, trade(): return lax.all_to_all(pieces, 'ep', split_axis=0, concat_axis=0, tiled=True)  27.2 us
    pallas_call x2, Pallas kernels, run_layer(): call(expert_body, sds((EP * CAP, D), bf16), 4, name='expert')  8.92 us
  transfers between devices with their start and end apart: 7, of which 7 were waited for; matrix products, arithmetic and copies ran while one was open for 7% of the time, Pallas kernels for 0%

profile of v1, /device:TPU:96, one launch (start us, length us, event | category | flops | bytes accessed | tf_op | source)
XLA Modules:
  0.0 271.5 jit_solution(11129810546024587116)
XLA Ops:
  0.0 0.9 copy-done.17
  0.9 0.7 copy-done.25
  1.6 1.4 norm.1
  3.0 7.2 %all-to-all-start = ((bf16[16,16,3072]{2,1,0:T(8,128)(2,1)}), bf16[16,16,3072]{2,1,0:T(8,128)(2,1)S(1)}, u32[]{:S(2)}, u32[]{:S(2)}) async-start(bf16[16,16,3072]{2,1,0:T(8,128)(2,1)} %norm.1), calls=%async_computation | async-start | bytes 3145728 | tf_op jit(solution)/shard_map/all_to_all | solution.py:220
  10.2 0.8 dynamic_slice.3
  12.1 0.6 fusion.11
  12.8 0.6 fusion.10
  14.3 0.8 multiply_sine_fusion
  15.1 0.7 fusion.5
  15.8 18.9 %all-to-all-done = bf16[16,16,3072]{2,1,0:T(8,128)(2,1)S(1)} async-done(((bf16[16,16,3072]{2,1,0:T(8,128)(2,1)}), bf16[16,16,3072]{2,1,0:T(8,128)(2,1)S(1)}, u32[]{:S(2)}, u32[]{:S(2)}) %all-to-all-start) | async-done | bytes 1572896 | tf_op jit(solution)/shard_map/all_to_all | solution.py:220
  34.7 1.4 copy-done.9
  36.1 2.1 project.2
  38.2 3.7 %all-to-all-start.1 = ((bf16[16,16,384]{2,1,0:T(8,128)(2,1)}), bf16[16,16,384]{2,1,0:T(8,128)(2,1)S(1)}, u32[]{:S(2)}, u32[]{:S(2)}) async-start(bf16[16,16,384]{2,1,0:T(8,128)(2,1)} %bitcast.5), calls=%async_computation.1 | async-start | bytes 393216 | tf_op jit(solution)/shard_map/all_to_all | solution.py:220
  42.4 7.8 %all-to-all-done.1.got_ref = bf16[16,16,384]{2,1,0:T(8,128)(2,1)S(1)} async-done(((bf16[16,16,384]{2,1,0:T(8,128)(2,1)}), bf16[16,16,384]{2,1,0:T(8,128)(2,1)S(1)}, u32[]{:S(2)}, u32[]{:S(2)}) %all-to-all-start.1) | async-done | bytes 196640 | tf_op jit(solution)/shard_map/all_to_all | solution.py:220
  50.3 1.2 copy-done.11
  51.5 1.2 copy-done.13
  52.7 2.4 attend.2
  55.1 11.0 %all_to_all.60 = bf16[16,16,256]{2,1,0:T(8,128)(2,1)S(1)} all-to-all(bf16[16,16,256]{2,1,0:T(8,128)(2,1)S(1)} %attend.2), channel_id=1, replica_groups=mesh['section'=16,'ep'=16] {'ep'}, dimensions={0} | all-to-all | bytes 262144 | tf_op jit(solution)/shard_map/all_to_all | solution.py:220
  66.7 1.2 copy-done.7
  67.9 3.9 %all-to-all-start.3 = ((bf16[16,16,3072]{2,1,0:T(8,128)(2,1)}), bf16[16,16,3072]{2,1,0:T(8,128)(2,1)S(1)}, u32[]{:S(2)}, u32[]{:S(2)}) async-start(bf16[16,16,3072]{2,1,0:T(8,128)(2,1)} %bitcast.48), calls=%async_computation.3 | async-start | bytes 3145728 | tf_op jit(solution)/shard_map/all_to_all | solution.py:220
  73.1 0.6 slice_bitcast_fusion
  73.7 19.2 %all-to-all-done.3.got_ref = bf16[16,16,3072]{2,1,0:T(8,128)(2,1)S(1)} async-done(((bf16[16,16,3072]{2,1,0:T(8,128)(2,1)}), bf16[16,16,3072]{2,1,0:T(8,128)(2,1)S(1)}, u32[]{:S(2)}, u32[]{:S(2)}) %all-to-all-start.3) | async-done | bytes 1572896 | tf_op jit(solution)/shard_map/all_to_all | solution.py:220
  92.9 0.8 residual.2
  93.7 1.0 copy-done.16
  94.7 0.6 copy-done.22
  96.0 4.3 %all-to-all-start.4 = ((bf16[16,8,3072]{2,1,0:T(8,128)(2,1)}), bf16[16,8,3072]{2,1,0:T(8,128)(2,1)}, u32[]{:S(2)}, u32[]{:S(2)}) async-start(bf16[16,8,3072]{2,1,0:T(8,128)(2,1)} %copy-done.16), calls=%async_computation.4 | async-start | bytes 1572864 | tf_op jit(solution)/shard_map/all_to_all | solution.py:220
  100.3 4.6 %copy.53.gate_ref = bf16[1,3072,448]{2,1,0:T(8,128)(2,1)} copy(bf16[1,3072,448]{1,2,0:T(8,128)(2,1)} %param.29) | data formatting | bytes 5505024 | tf_op args[11]
  104.9 4.7 %copy.54.up_ref = bf16[1,3072,448]{2,1,0:T(8,128)(2,1)} copy(bf16[1,3072,448]{1,2,0:T(8,128)(2,1)} %param.30) | data formatting | bytes 5505024 | tf_op args[12]
  109.6 2.2 all-to-all-done.4
  111.9 4.6 %expert.2 = bf16[128,3072]{1,0:T(8,128)(2,1)S(1)} custom-call(bf16[128,3072]{1,0:T(8,128)(2,1)} %bitcast.16.x_ref, bf16[1,3072,448]{2,1,0:T(8,128)(2,1)} %copy.53.gate_ref, bf16[1,3072,448]{2,1,0:T(8,128)(2,1)} %copy.54.up_ref, bf16[1,448,3072]{2,1,0:T(8,128)(2,1)S(1)} %copy-done), custom_call_target="tpu_custom_call" | custom-call | tf_op jit(solution)/shard_map/expert/pallas_call | solution.py:284
  116.5 16.3 %all_to_all.61.got_ref = bf16[16,8,3072]{2,1,0:T(8,128)(2,1)S(1)} all-to-all(bf16[16,8,3072]{2,1,0:T(8,128)(2,1)S(1)} %bitcast.56), channel_id=1, replica_groups=mesh['section'=16,'ep'=16] {'ep'}, dimensions={0} | all-to-all | bytes 1572864 | tf_op jit(solution)/shard_map/all_to_all | solution.py:220
  132.8 0.9 combine.2
  133.7 1.9 collective-permute-start
  135.6 4.3 %collective-permute-done.shifted_ref = bf16[16,3072]{1,0:T(8,128)(2,1)} collective-permute-done((bf16[16,3072]{1,0:T(8,128)(2,1)}, bf16[16,3072]{1,0:T(8,128)(2,1)}, u32[]{:S(2)}, u32[]{:S(2)}) %collective-permute-start) | collective-permute-done | bytes 98336 | tf_op jit(solution)/shard_map/ppermute | solution.py:295
  140.0 0.9 copy-done.21
  140.8 0.7 copy-done.26
  141.6 1.1 select_norm.1
  142.7 0.6 copy-done.19
  143.3 26.9 %all_to_all.62 = bf16[16,16,3072]{2,1,0:T(8,128)(2,1)S(1)} all-to-all(bf16[16,16,3072]{2,1,0:T(8,128)(2,1)S(1)} %get-tuple-element.17), channel_id=1, replica_groups=mesh['section'=16,'ep'=16] {'ep'}, dimensions={0} | all-to-all | bytes 3145728 | tf_op jit(solution)/shard_map/all_to_all | solution.py:220
  170.2 1.5 project.3
  171.7 0.7 copy-done.15
  172.4 3.7 %all-to-all-start.7 = ((bf16[16,16,384]{2,1,0:T(8,128)(2,1)}), bf16[16,16,384]{2,1,0:T(8,128)(2,1)S(1)}, u32[]{:S(2)}, u32[]{:S(2)}) async-start(bf16[16,16,384]{2,1,0:T(8,128)(2,1)} %bitcast.57), calls=%async_computation.7 | async-start | bytes 393216 | tf_op jit(solution)/shard_map/all_to_all | solution.py:220
  176.1 0.8 copy.55.ks_ref
  176.9 0.8 copy.56.vs_ref
  177.7 6.6 %all-to-all-done.7.got_ref = bf16[16,16,384]{2,1,0:T(8,128)(2,1)S(1)} async-done(((bf16[16,16,384]{2,1,0:T(8,128)(2,1)}), bf16[16,16,384]{2,1,0:T(8,128)(2,1)S(1)}, u32[]{:S(2)}, u32[]{:S(2)}) %all-to-all-start.7) | async-done | bytes 196640 | tf_op jit(solution)/shard_map/all_to_all | solution.py:220
  184.2 0.8 broadcast_in_dim.36.lens_ref
  185.0 1.2 copy-done.12
  186.3 1.2 copy-done.14
  187.5 0.7 copy-done.27
  188.2 0.7 copy-done.28
  188.9 2.4 attend.3
  191.3 11.0 %all_to_all.63 = bf16[16,16,256]{2,1,0:T(8,128)(2,1)S(1)} all-to-all(bf16[16,16,256]{2,1,0:T(8,128)(2,1)S(1)} %attend.3), channel_id=1, replica_groups=mesh['section'=16,'ep'=16] {'ep'}, dimensions={0} | all-to-all | bytes 262144 | tf_op jit(solution)/shard_map/all_to_all | solution.py:220
  202.9 1.2 copy-done.8
  204.1 4.5 %all-to-all-start.9 = ((bf16[16,16,3072]{2,1,0:T(8,128)(2,1)}), bf16[16,16,3072]{2,1,0:T(8,128)(2,1)}, u32[]{:S(2)}, u32[]{:S(2)}) async-start(bf16[16,16,3072]{2,1,0:T(8,128)(2,1)} %bitcast.49), calls=%async_computation.9 | async-start | bytes 3145728 | tf_op jit(solution)/shard_map/all_to_all | solution.py:220
  208.6 1.4 copy.58.chosen_ref
  209.9 20.4 %all-to-all-done.9.got_ref = bf16[16,16,3072]{2,1,0:T(8,128)(2,1)} async-done(((bf16[16,16,3072]{2,1,0:T(8,128)(2,1)}), bf16[16,16,3072]{2,1,0:T(8,128)(2,1)}, u32[]{:S(2)}, u32[]{:S(2)}) %all-to-all-start.9) | async-done | bytes 1572896 | tf_op jit(solution)/shard_map/all_to_all | solution.py:220
  230.3 0.9 copy-done.20
  231.2 0.7 copy-done.29
  231.9 0.7 copy-done.30
  232.6 2.2 residual.3
  234.9 16.2 %all_to_all.64 = bf16[16,8,3072]{2,1,0:T(8,128)(2,1)S(1)} all-to-all(bf16[16,8,3072]{2,1,0:T(8,128)(2,1)S(1)} %get-tuple-element.20), channel_id=1, replica_groups=mesh['section'=16,'ep'=16] {'ep'}, dimensions={0} | all-to-all | bytes 1572864 | tf_op jit(solution)/shard_map/all_to_all | solution.py:220
  251.1 4.3 %expert.3 = bf16[128,3072]{1,0:T(8,128)(2,1)S(1)} custom-call(bf16[128,3072]{1,0:T(8,128)(2,1)S(1)} %bitcast.54, bf16[1,3072,448]{2,1,0:T(8,128)(2,1)} %copy.53.gate_ref, bf16[1,3072,448]{2,1,0:T(8,128)(2,1)} %copy.54.up_ref, bf16[1,448,3072]{2,1,0:T(8,128)(2,1)S(1)} %copy-done), custom_call_target="tpu_custom_call" | custom-call | tf_op jit(solution)/shard_map/expert/pallas_call | solution.py:284
  255.5 15.2 %all_to_all.65.got_ref = bf16[16,8,3072]{2,1,0:T(8,128)(2,1)S(1)} all-to-all(bf16[16,8,3072]{2,1,0:T(8,128)(2,1)S(1)} %bitcast.55), channel_id=1, replica_groups=mesh['section'=16,'ep'=16] {'ep'}, dimensions={0} | all-to-all | bytes 1572864 | tf_op jit(solution)/shard_map/all_to_all | solution.py:220
  270.6 0.9 combine.3
  (83 shorter events, 5.8 us)
Async XLA Ops:
  0.0 0.9 copy-start.17
  0.9 0.7 copy-start.25
  3.0 9.1 %copy-start.36 = (f32[1,2,16,8,4]{2,4,3,1,0:T(4,128)S(1)}, f32[1,2,16,8,4]{2,4,3,1,0:T(4,128)}, u32[]{:S(2)}) copy-start(f32[1,2,16,8,4]{2,4,3,1,0:T(4,128)} %param.34) | copy-start | bytes 12292
  3.0 9.8 %copy-start.37 = (f32[1,2,16,8,4]{2,4,3,1,0:T(4,128)S(1)}, f32[1,2,16,8,4]{2,4,3,1,0:T(4,128)}, u32[]{:S(2)}) copy-start(f32[1,2,16,8,4]{2,4,3,1,0:T(4,128)} %param.35) | copy-start | bytes 12292
  3.0 10.5 %copy-start.33 = (bf16[1,3072,64]{1,2,0:T(8,128)(2,1)S(1)}, bf16[1,3072,64]{1,2,0:T(8,128)(2,1)}, u32[]{:S(2)}) copy-start(bf16[1,3072,64]{1,2,0:T(8,128)(2,1)} %param.25) | copy-start | bytes 1179652
  3.0 10.8 %copy-start.34 = (bf16[1,3072,64]{1,2,0:T(8,128)(2,1)S(1)}, bf16[1,3072,64]{1,2,0:T(8,128)(2,1)}, u32[]{:S(2)}) copy-start(bf16[1,3072,64]{1,2,0:T(8,128)(2,1)} %param.26) | copy-start | bytes 1179652
  3.0 31.7 %all-to-all-start = ((bf16[16,16,3072]{2,1,0:T(8,128)(2,1)}), bf16[16,16,3072]{2,1,0:T(8,128)(2,1)S(1)}, u32[]{:S(2)}, u32[]{:S(2)}) async-start(bf16[16,16,3072]{2,1,0:T(8,128)(2,1)} %norm.1), calls=%async_computation | async-start | bytes 3145728 | tf_op jit(solution)/shard_map/all_to_all | solution.py:220
  11.0 0.6 copy-start.38
  14.3 24.0 %copy-start.1 = (bf16[1,3072,64]{2,1,0:T(8,128)(2,1)}, bf16[1,3072,64]{2,1,0:T(8,128)(2,1)S(1)}, u32[]{:S(2)}) copy-start(bf16[1,3072,64]{2,1,0:T(8,128)(2,1)S(1)} %copy.48) | copy-start | bytes 1179652
  34.7 1.4 copy-start.9
  36.1 5.8 %copy-start.39 = (s32[2,16]{1,0:T(2,128)S(1)}, s32[2,16]{1,0:T(2,128)}, u32[]{:S(2)}) copy-start(s32[2,16]{1,0:T(2,128)} %copy-done.38) | copy-start | bytes 388
  38.2 27.9 %copy-start.5 = (bf16[1,256,3072]{2,1,0:T(8,128)(2,1)S(1)}, bf16[1,256,3072]{2,1,0:T(8,128)(2,1)}, u32[]{:S(2)}) copy-start(bf16[1,256,3072]{2,1,0:T(8,128)(2,1)} %wo_ref.3) | copy-start | bytes 4718596
  38.2 12.0 %all-to-all-start.1 = ((bf16[16,16,384]{2,1,0:T(8,128)(2,1)}), bf16[16,16,384]{2,1,0:T(8,128)(2,1)S(1)}, u32[]{:S(2)}, u32[]{:S(2)}) async-start(bf16[16,16,384]{2,1,0:T(8,128)(2,1)} %bitcast.5), calls=%async_computation.1 | async-start | bytes 393216 | tf_op jit(solution)/shard_map/all_to_all | solution.py:220
  50.3 1.2 copy-start.11
  51.5 1.2 copy-start.13
  66.7 1.2 copy-start.7
  67.9 3.9 %copy-start.40 = (s32[1,2,16,2]{2,3,1,0:T(2,128)S(1)}, s32[1,2,16,2]{2,3,1,0:T(2,128)}, u32[]{:S(2)}) copy-start(s32[1,2,16,2]{2,3,1,0:T(2,128)} %param.21) | copy-start | bytes 772
  67.9 4.6 %copy-start.35 = (bf16[1,3072,8]{1,2,0:T(8,128)(2,1)S(1)}, bf16[1,3072,8]{1,2,0:T(8,128)(2,1)}, u32[]{:S(2)}) copy-start(bf16[1,3072,8]{1,2,0:T(8,128)(2,1)} %param.28) | copy-start | bytes 147460
  67.9 25.0 %copy-start.18 = (bf16[16,3072]{1,0:T(8,128)(2,1)S(1)}, bf16[16,3072]{1,0:T(8,128)(2,1)}, u32[]{:S(2)}) copy-start(bf16[16,3072]{1,0:T(8,128)(2,1)} %x_ref.3) | copy-start | bytes 294916
  67.9 25.0 %copy-start.24 = (bf16[1,3072]{1,0:T(2,128)(2,1)S(1)}, bf16[1,3072]{1,0:T(2,128)(2,1)}, u32[]{:S(2)}) copy-start(bf16[1,3072]{1,0:T(2,128)(2,1)} %gain_ref.7) | copy-start | bytes 18436
  67.9 25.0 %all-to-all-start.3 = ((bf16[16,16,3072]{2,1,0:T(8,128)(2,1)}), bf16[16,16,3072]{2,1,0:T(8,128)(2,1)S(1)}, u32[]{:S(2)}, u32[]{:S(2)}) async-start(bf16[16,16,3072]{2,1,0:T(8,128)(2,1)} %bitcast.48), calls=%async_computation.3 | async-start | bytes 3145728 | tf_op jit(solution)/shard_map/all_to_all | solution.py:220
  72.8 23.2 %copy-start.3 = (bf16[1,3072,8]{2,1,0:T(8,128)(2,1)}, bf16[1,3072,8]{2,1,0:T(8,128)(2,1)S(1)}, u32[]{:S(2)}) copy-start(bf16[1,3072,8]{2,1,0:T(8,128)(2,1)S(1)} %copy.51.router_ref) | copy-start | bytes 147460
  93.7 1.0 copy-start.16
  94.7 0.6 copy-start.22
  95.4 0.6 copy-start.31
  96.0 15.9 %all-to-all-start.4 = ((bf16[16,8,3072]{2,1,0:T(8,128)(2,1)}), bf16[16,8,3072]{2,1,0:T(8,128)(2,1)}, u32[]{:S(2)}, u32[]{:S(2)}) async-start(bf16[16,8,3072]{2,1,0:T(8,128)(2,1)} %copy-done.16), calls=%async_computation.4 | async-start | bytes 1572864 | tf_op jit(solution)/shard_map/all_to_all | solution.py:220
  104.9 7.0 %copy-start = (bf16[1,448,3072]{2,1,0:T(8,128)(2,1)S(1)}, bf16[1,448,3072]{2,1,0:T(8,128)(2,1)}, u32[]{:S(2)}) copy-start(bf16[1,448,3072]{2,1,0:T(8,128)(2,1)} %down_ref.3) | copy-start | bytes 8257540
  116.4 16.4 %copy-start.23 = (bf16[16,3072]{1,0:T(8,128)(2,1)S(1)}, bf16[16,3072]{1,0:T(8,128)(2,1)}, u32[]{:S(2)}) copy-start(bf16[16,3072]{1,0:T(8,128)(2,1)} %copy-done.22) | copy-start | bytes 294916
  116.5 16.3 %copy-start.32 = (f32[16,128]{1,0:T(8,128)S(1)}, f32[16,128]{1,0:T(8,128)}, u32[]{:S(2)}) copy-start(f32[16,128]{1,0:T(8,128)} %copy-done.31) | copy-start | bytes 24580
  133.7 6.2 %collective-permute-start = (bf16[16,3072]{1,0:T(8,128)(2,1)}, bf16[16,3072]{1,0:T(8,128)(2,1)}, u32[]{:S(2)}, u32[]{:S(2)}) collective-permute-start(bf16[16,3072]{1,0:T(8,128)(2,1)} %combine.2), channel_id=1, source_target_pairs={{0,16},{16,32},{32,48},{48,64},{64,80},{80,96},{96,112},{112,128},... | collective-permute-start | bytes 294920 | tf_op jit(solution)/shard_map/ppermute | solution.py:295
  140.0 0.9 copy-start.21
  140.8 0.7 copy-start.26
  142.7 0.6 copy-start.19
  143.3 26.9 %copy-start.2 = (bf16[1,3072,64]{2,1,0:T(8,128)(2,1)S(1)}, bf16[1,3072,64]{2,1,0:T(8,128)(2,1)}, u32[]{:S(2)}) copy-start(bf16[1,3072,64]{2,1,0:T(8,128)(2,1)} %copy-done.1) | copy-start | bytes 1179652
  143.3 26.9 %copy-start.10 = (bf16[1,3072,256]{2,1,0:T(8,128)(2,1)S(1)}, bf16[1,3072,256]{2,1,0:T(8,128)(2,1)}, u32[]{:S(2)}) copy-start(bf16[1,3072,256]{2,1,0:T(8,128)(2,1)} %param.24) | copy-start | bytes 4718596
  171.7 0.7 copy-start.15
  172.4 11.8 %all-to-all-start.7 = ((bf16[16,16,384]{2,1,0:T(8,128)(2,1)}), bf16[16,16,384]{2,1,0:T(8,128)(2,1)S(1)}, u32[]{:S(2)}, u32[]{:S(2)}) async-start(bf16[16,16,384]{2,1,0:T(8,128)(2,1)} %bitcast.57), calls=%async_computation.7 | async-start | bytes 393216 | tf_op jit(solution)/shard_map/all_to_all | solution.py:220
  184.2 18.0 %copy-start.6 = (bf16[1,256,3072]{2,1,0:T(8,128)(2,1)S(1)}, bf16[1,256,3072]{2,1,0:T(8,128)(2,1)}, u32[]{:S(2)}) copy-start(bf16[1,256,3072]{2,1,0:T(8,128)(2,1)} %wo_ref.3) | copy-start | bytes 4718596
  185.0 1.2 copy-start.12
  186.3 1.2 copy-start.14
  187.5 0.7 copy-start.27
  188.2 0.7 copy-start.28
  202.8 1.2 copy-start.8
  204.0 26.3 %copy-start.4 = (bf16[1,3072,8]{2,1,0:T(8,128)(2,1)S(1)}, bf16[1,3072,8]{2,1,0:T(8,128)(2,1)}, u32[]{:S(2)}) copy-start(bf16[1,3072,8]{2,1,0:T(8,128)(2,1)} %copy-done.3) | copy-start | bytes 147460
  204.1 26.3 %all-to-all-start.9 = ((bf16[16,16,3072]{2,1,0:T(8,128)(2,1)}), bf16[16,16,3072]{2,1,0:T(8,128)(2,1)}, u32[]{:S(2)}, u32[]{:S(2)}) async-start(bf16[16,16,3072]{2,1,0:T(8,128)(2,1)} %bitcast.49), calls=%async_computation.9 | async-start | bytes 3145728 | tf_op jit(solution)/shard_map/all_to_all | solution.py:220
  230.3 0.9 copy-start.20
  231.2 0.7 copy-start.29
  231.9 0.7 copy-start.30

commit v2 on v1

v2 whole, which is shorter than its diff:
```python
import functools

import jax
import jax.numpy as jnp
import numpy as np
from jax import lax
from jax.experimental import pallas as pl
from jax.experimental.pallas import tpu as pltpu
from jax.sharding import PartitionSpec as P

D = 3072
QH = 32
KVH = 8
HD = 128
EXPERTS = 8
EXP_WIN = 1
LEN = 16
BLK = 4
CAP = 8
EP = 16
TOK = 16
CHUNK = 512

rope_base = 1000000.0
norm_eps = 1e-05
f32 = jnp.float32
bf16 = jnp.bfloat16


def call(body, out_shape, n_in, smem=(), name=None, scratch=(), limit=12, space=pltpu.VMEM):
    specs = [pl.BlockSpec(memory_space=pltpu.SMEM if i in smem else space) for i in range(n_in)]
    outs = jax.tree.map(lambda _: pl.BlockSpec(memory_space=pltpu.VMEM), out_shape)
    return pl.pallas_call(
        body,
        out_shape=out_shape,
        in_specs=specs,
        out_specs=outs,
        scratch_shapes=list(scratch),
        compiler_params=pltpu.CompilerParams(vmem_limit_bytes=limit << 20),
        name=name,
    )


def dot_last(left, right):
    return lax.dot_general(left, right, (((1,), (1,)), ((), ())), preferred_element_type=f32)


def dot_first(left, right):
    return lax.dot_general(
        left,
        right,
        (((0,), (0,)), ((), ())),
        preferred_element_type=f32,
        precision=lax.Precision.HIGHEST,
    )


def columns():
    return [slice(c, c + CHUNK) for c in range(0, D, CHUNK)]


def spread_normed(x_ref, gain_ref, copies_ref):
    total = jnp.zeros((TOK, 1), f32)
    for cols in columns():
        wide = x_ref[:, cols].astype(f32)
        total = total + jnp.sum(wide * wide, axis=-1, keepdims=True)
    factor = lax.rsqrt(total / D + norm_eps)
    for cols in columns():
        wide = x_ref[:, cols].astype(f32)
        rows = (wide * factor * gain_ref[:, cols].astype(f32)).astype(bf16)
        for dest in range(EP):
            copies_ref[dest, :, cols] = rows


def norm_body(x_hbm, gain_hbm, copies_ref, x_ref, gain_ref, sems):
    fetches = [
        pltpu.make_async_copy(x_hbm, x_ref, sems.at[0]),
        pltpu.make_async_copy(gain_hbm, gain_ref, sems.at[1]),
    ]
    for fetch in fetches:
        fetch.start()
    for fetch in fetches:
        fetch.wait()
    spread_normed(x_ref, gain_ref, copies_ref)


def norm_select_body(entering_ref, shifted_ref, gain_ref, x_ref, copies_ref):
    is_first = lax.axis_index("section") == 0

    @pl.when(is_first)
    def _():
        x_ref[...] = entering_ref[...]

    @pl.when(jnp.logical_not(is_first))
    def _():
        x_ref[...] = shifted_ref[...]

    spread_normed(x_ref, gain_ref, copies_ref)


def project_body(x_ref, wq_ref, wk_ref, wv_ref, out_ref):
    x = x_ref[...]
    out_ref[:, 0:256] = jnp.dot(x, wq_ref[...], preferred_element_type=f32).astype(bf16)
    both = jnp.concatenate([wk_ref[...], wv_ref[...]], axis=0)
    out_ref[:, 256:384] = dot_last(x, both).astype(bf16)


def rotary_table():
    half = HD // 2
    inv_freq = rope_base ** (-np.arange(half, dtype=np.float64) * 2.0 / HD)
    angles = np.arange(2 * LEN, dtype=np.float64)[:, None] * inv_freq
    cos_vals, sin_vals = np.cos(angles), np.sin(angles)
    return np.concatenate([cos_vals, cos_vals, -sin_vals, sin_vals], axis=1).astype(np.float32)


def attention_body(
    tick, got_ref, lens_ref, rotary_ref, ks_ref, vs_ref, key_ref, value_ref, out_ref
):
    scale = HD ** (-0.5)
    group = QH // KVH
    pos = TOK * LEN
    lane = lax.broadcasted_iota(jnp.int32, (TOK, HD), 1)
    low = lane < HD // 2
    row_lens = lens_ref[pl.ds(lax.axis_index("section") + 1 - tick, 1), :].astype(f32)
    mine = lax.broadcasted_iota(jnp.int32, (TOK, row_lens.shape[1]), 0) + lax.axis_index("ep") * TOK
    there = lax.broadcasted_iota(jnp.int32, (TOK, row_lens.shape[1]), 1)
    lens = jnp.sum(jnp.where(mine == there, row_lens, 0.0), axis=-1, keepdims=True)
    lens = lens.astype(jnp.int32)
    length = lax.broadcasted_iota(jnp.int32, (TOK, 2 * LEN), 1)
    rotary = jnp.dot(
        jnp.where(length == lens, 1.0, 0.0).astype(f32),
        rotary_ref[...],
        preferred_element_type=f32,
        precision=lax.Precision.HIGHEST,
    )
    cos_vals = rotary[:, 0:HD]
    sin_vals = rotary[:, HD : 2 * HD]

    def turned(rows):
        return (rows * cos_vals + pltpu.roll(rows, HD // 2, 1) * sin_vals).astype(bf16)

    blocks = LEN // BLK
    which = lax.broadcasted_iota(jnp.int32, (KVH * blocks, KVH * pos), 0)
    at = lax.broadcasted_iota(jnp.int32, (KVH * blocks, KVH * pos), 1)
    spread = jnp.where(
        (which // blocks == at // pos) & (which % blocks == (at % LEN) // BLK), 1.0, 0.0
    ).astype(f32)
    k_all = dot_first(jnp.concatenate([ks_ref[tick, g] for g in range(KVH)], axis=0), spread)
    v_all = dot_first(jnp.concatenate([vs_ref[tick, g] for g in range(KVH)], axis=0), spread)
    row = lax.broadcasted_iota(jnp.int32, (TOK, pos), 0)
    col = lax.broadcasted_iota(jnp.int32, (TOK, pos), 1)
    live_one = (col // LEN == row) & (col % LEN < lens)
    live = jnp.concatenate([live_one.astype(f32)] * group, axis=0) > 0.5
    for g in range(KVH):
        first = got_ref[2 * g, :, 256:384].astype(f32)
        second = got_ref[2 * g + 1, :, 256:384].astype(f32)
        key_new = turned(jnp.where(low, first, pltpu.roll(second, HD // 2, 1))).astype(f32)
        value_new = jnp.where(low, pltpu.roll(first, HD // 2, 1), second)
        q = jnp.concatenate(
            [
                turned(got_ref[2 * g + r // 2, :, (r % 2) * HD : (r % 2 + 1) * HD].astype(f32))
                for r in range(group)
            ],
            axis=0,
        )
        keys = key_ref[0, tick, :, g].reshape(pos, HD)
        values = value_ref[0, tick, :, g].reshape(pos, HD)
        k_scale = jnp.concatenate([k_all[:, g * pos : (g + 1) * pos]] * group, axis=0)
        v_scale = jnp.concatenate([v_all[:, g * pos : (g + 1) * pos]] * group, axis=0)
        scores = dot_last(q, keys) * k_scale * scale
        own = (
            jnp.sum(
                q.astype(f32) * jnp.concatenate([key_new] * group, axis=0), axis=-1, keepdims=True
            )
            * scale
        )
        top = jnp.maximum(jnp.max(jnp.where(live, scores, -1e30), axis=-1, keepdims=True), own)
        e = jnp.where(live, jnp.exp(jnp.where(live, scores, -1e30) - top), 0.0)
        e_own = jnp.exp(own - top)
        denom = jnp.sum(e, axis=-1, keepdims=True) + e_own
        weight = jnp.where(live, e * v_scale, 0.0).astype(bf16)
        mixed = jnp.dot(weight, values, preferred_element_type=f32)
        mixed = mixed + e_own * jnp.concatenate([value_new] * group, axis=0)
        done = (mixed / denom).astype(bf16)
        for r in range(group):
            out_ref[2 * g + r // 2, :, (r % 2) * HD : (r % 2 + 1) * HD] = done[
                r * TOK : (r + 1) * TOK
            ]


def out_body(att_ref, wo_ref, part_ref):
    part_ref[...] = jnp.dot(att_ref[...], wo_ref[0], preferred_element_type=f32).astype(bf16)


def residual_body(
    tick, x_ref, got_ref, gain_ref, router_ref, chosen_ref, res_ref, copies_ref, coef_ref, ffn_ref
):
    one = chosen_ref[tick, 0:1, :]
    two = chosen_ref[tick, 1:2, :]
    held = jnp.where((one == 0) | (two == 0), 1.0, 0.0).astype(f32)
    held = jnp.broadcast_to(held, (CAP, TOK))
    before = lax.broadcasted_iota(jnp.int32, (TOK, TOK), 0) < lax.broadcasted_iota(
        jnp.int32, (TOK, TOK), 1
    )
    rank = jnp.dot(
        held.astype(bf16), before.astype(f32).astype(bf16), preferred_element_type=f32
    )
    slot = lax.broadcasted_iota(jnp.int32, (CAP, TOK), 0).astype(f32)
    sel = jnp.where((held > 0.5) & (rank == slot), 1.0, 0.0).astype(f32)
    total = jnp.zeros((TOK, 1), f32)
    for cols in columns():
        acc = got_ref[0, :, cols].astype(f32)
        for src in range(1, EP):
            acc = acc + got_ref[src, :, cols].astype(f32)
        rounded = (x_ref[:, cols].astype(f32) + acc).astype(bf16)
        res_ref[:, cols] = rounded
        wide = rounded.astype(f32)
        total = total + jnp.sum(wide * wide, axis=-1, keepdims=True)
    factor = lax.rsqrt(total / D + norm_eps)
    for cols in columns():
        wide = res_ref[:, cols].astype(f32)
        rows = (wide * factor * gain_ref[:, cols].astype(f32)).astype(bf16)
        ffn_ref[:, cols] = rows
        slots = jnp.dot(sel.astype(bf16), rows, preferred_element_type=f32).astype(bf16)
        for dest in range(EP):
            copies_ref[dest, :, cols] = slots
    logits = dot_last(router_ref[...], ffn_ref[...])
    expert = lax.broadcasted_iota(jnp.int32, (EXPERTS, TOK), 0)
    pick_one = jnp.sum(jnp.where(expert == one, logits, 0.0), axis=0, keepdims=True)
    pick_two = jnp.sum(jnp.where(expert == two, logits, 0.0), axis=0, keepdims=True)
    top = jnp.maximum(pick_one, pick_two)
    e_one = jnp.exp(pick_one - top)
    e_two = jnp.exp(pick_two - top)
    both = e_one + e_two
    share = jnp.where(one == 0, e_one / both, 0.0) + jnp.where(two == 0, e_two / both, 0.0)
    coef_ref[...] = share * sel


def expert_body(x_ref, gate_ref, up_ref, down_ref, part_ref):
    x = x_ref[...]
    gate = dot_last(x, gate_ref[...])
    up = dot_last(x, up_ref[...])
    hidden = (gate * jax.nn.sigmoid(gate) * up).astype(bf16)
    part_ref[...] = jnp.dot(hidden, down_ref[0], preferred_element_type=f32).astype(bf16)


def combine_body(res_ref, coef_ref, got_ref, out_ref):
    coef = coef_ref[...]
    for cols in columns():
        acc = got_ref[0, :, cols].astype(f32)
        for src in range(1, EP):
            acc = acc + got_ref[src, :, cols].astype(f32)
        out_ref[:, cols] = (res_ref[:, cols].astype(f32) + dot_first(coef, acc)).astype(bf16)


def sds(shape, dtype):
    return jax.ShapeDtypeStruct(shape, dtype)


def trade(pieces):
    return lax.all_to_all(pieces, "ep", split_axis=0, concat_axis=0, tiled=True)


def local(
    states,
    entering,
    seq_lens,
    routes,
    attn_norm,
    ffn_norm,
    wq,
    wk,
    wv,
    wo,
    router,
    w_gate,
    w_up,
    w_down,
    cache_k,
    cache_v,
    k_scale,
    v_scale,
):
    rotary = rotary_table()
    ks = jnp.transpose(k_scale[0], (0, 2, 3, 1))
    vs = jnp.transpose(v_scale[0], (0, 2, 3, 1))
    chosen = jnp.transpose(routes[0], (0, 2, 1))
    wk_t, wv_t, router_t, gate_t, up_t = (
        jnp.transpose(w[0], (1, 0)) for w in (wk, wv, router, w_gate, w_up)
    )

    def run_layer(x, copies, tick):
        everyone = trade(copies).reshape(EP * TOK, D)
        projected = call(project_body, sds((EP * TOK, 384), bf16), 4, name="project")(
            everyone, wq[0], wk_t, wv_t
        )
        got = trade(projected.reshape(EP, TOK, 384))
        attended = call(
            functools.partial(attention_body, tick),
            sds((EP, TOK, 256), bf16),
            7,
            name="attend",
        )(got, seq_lens, rotary, ks, vs, cache_k, cache_v)
        heads = trade(attended).reshape(EP * TOK, 256)
        part = call(out_body, sds((EP * TOK, D), bf16), 2, name="outproj")(heads, wo)
        sums = trade(part.reshape(EP, TOK, D))
        residual, slots, coef = call(
            functools.partial(residual_body, tick),
            (sds((TOK, D), bf16), sds((EP, CAP, D), bf16), sds((CAP, TOK), f32)),
            5,
            name="residual",
            scratch=[pltpu.VMEM((TOK, D), bf16)],
        )(x, sums, ffn_norm, router_t, chosen)
        landed = trade(slots).reshape(EP * CAP, D)
        pieces = call(expert_body, sds((EP * CAP, D), bf16), 4, name="expert", limit=16)(
            landed, gate_t, up_t, w_down
        )
        returned = trade(pieces.reshape(EP, CAP, D))
        return call(combine_body, sds((TOK, D), bf16), 3, name="combine")(
            residual, coef, returned
        )

    copies = call(
        norm_body,
        sds((EP, TOK, D), bf16),
        2,
        name="norm",
        scratch=[
            pltpu.VMEM((TOK, D), bf16),
            pltpu.VMEM((1, D), bf16),
            pltpu.SemaphoreType.DMA((2,)),
        ],
        space=pltpu.HBM,
    )(states, attn_norm)
    first_out = run_layer(states, copies, 0)
    count = lax.axis_size("section")
    shifted = lax.ppermute(first_out, "section", [(i, i + 1) for i in range(count - 1)])
    second_in, copies = call(
        norm_select_body,
        (sds((TOK, D), bf16), sds((EP, TOK, D), bf16)),
        3,
        name="select_norm",
    )(entering, shifted, attn_norm)
    return run_layer(second_in, copies, 1)


def solution(mesh):
    return jax.shard_map(
        local,
        mesh=mesh,
        in_specs=(
            P(("section", "ep"), None),
            P("ep", None),
            P(),
            P("section", None, "ep", None),
            P("section", None),
            P("section", None),
            P("section", None, "ep"),
            P("section", None, "ep"),
            P("section", None, "ep"),
            P("section", "ep", None),
            P("section", None, None),
            P("section", None, "ep"),
            P("section", None, "ep"),
            P("section", "ep", None),
            P("section", None, "ep", None, None, None),
            P("section", None, "ep", None, None, None),
            P("section", None, "ep", None, None),
            P("section", None, "ep", None, None),
        ),
        out_specs=P(("section", "ep"), None),
        check_vma=False,
    )
```

time: 273 us -> 230 us (0.84)
  blocking collectives: 96.6 us -> 206 us
  waiting for transfers between devices: 79.4 us -> 4.01 us
  local copies, waits for them, and re-layouts: 37.9 us -> 1.72 us
  starting transfers between devices: 29.1 us -> 1.92 us
  Pallas kernels: 25.9 us -> 15.3 us
    all_to_all x6 -> x12, blocking collectives: 96.6 us -> 206 us  [trade(): return lax.all_to_all(pieces, 'ep', split_axis=0, concat_axis=0, tiled=True)]
    all_to_all x6 -> x0, waiting for transfers between devices: 75.1 us -> none  [trade(): return lax.all_to_all(pieces, 'ep', split_axis=0, concat_axis=0, tiled=True)]
    unnamed x87 -> x42, local copies, waits for them, and re-layouts: 30.2 us -> 1.72 us
    all_to_all x6 -> x0, starting transfers between devices: 27.2 us -> none  [trade(): return lax.all_to_all(pieces, 'ep', split_axis=0, concat_axis=0, tiled=True)]
    pallas_call x6, Pallas kernels: 14.6 us -> 6.21 us  [the longest x2 4.5 us: run_layer(): call(expert_body, sds((EP * CAP, D), bf16), 4, name='expert', limit=16)]
    squeeze x9 -> x0, local copies, waits for them, and re-layouts: 4.33 us -> none  [the longest x3 2.02 us: run_layer(): routes[0, tick]]
  transfers between devices with their start and end apart: 7 -> 1, of which waited for: 7 -> 1; matrix products, arithmetic and copies ran while one was open for 7% -> 0% of each run, Pallas kernels for 0% -> 0%
where the time goes in v2:
time: 230 us; the launch traced here: 229 us
  blocking collectives  206 us (90%)
  Pallas kernels  15.3 us (7%)
  waiting for transfers between devices  4.01 us (2%)
    all_to_all x12, blocking collectives, trade(): return lax.all_to_all(pieces, 'ep', split_axis=0, concat_axis=0, tiled=True)  206 us
  transfers between devices with their start and end apart: 1, of which 1 were waited for; matrix products, arithmetic and copies ran while one was open for 0% of the time, Pallas kernels for 0%

profile of v2, /device:TPU:96, one launch (start us, length us, event | category | flops | bytes accessed | tf_op | source)
XLA Modules:
  0.0 229.0 jit_solution(271126081936401112)
XLA Ops:
  0.0 0.9 copy-done.9
  0.9 0.7 copy-done.18
  1.6 0.4 norm.1
  2.0 0.0 copy-start.4
  2.0 0.0 copy-start.7
  2.0 0.0 copy-start.8
  2.0 29.7 %all_to_all.60 = bf16[16,16,3072]{2,1,0:T(8,128)(2,1)S(1)} all-to-all(bf16[16,16,3072]{2,1,0:T(8,128)(2,1)S(1)} %norm.1), channel_id=1, replica_groups=mesh['section'=16,'ep'=16] {'ep'}, dimensions={0} | all-to-all | bytes 3145728 | tf_op jit(solution)/shard_map/all_to_all | solution.py:261
  31.8 0.0 copy-done.4
  31.8 0.0 copy-done.7
  31.8 0.0 copy-done.8
  31.8 0.0 copy-start.5
  31.8 0.0 copy-start.6
  31.8 0.0 copy-start.12
  31.8 0.0 copy-start.13
  31.8 0.0 copy-start.14
  31.8 0.0 copy-start.15
  31.8 1.0 project.2
  32.8 0.0 copy-start.3
  32.8 11.4 %all_to_all.61.got_ref = bf16[16,16,384]{2,1,0:T(8,128)(2,1)S(1)} all-to-all(bf16[16,16,384]{2,1,0:T(8,128)(2,1)S(1)} %bitcast.55), channel_id=1, replica_groups=mesh['section'=16,'ep'=16] {'ep'}, dimensions={0} | all-to-all | bytes 393216 | tf_op jit(solution)/shard_map/all_to_all | solution.py:261
  44.3 0.0 copy-done.5
  44.3 0.0 copy-done.6
  44.3 0.0 copy-done.12
  44.3 0.0 copy-done.13
  44.3 0.0 copy-done.14
  44.3 0.0 copy-done.15
  44.3 2.3 attend.2
  46.6 11.0 %all_to_all.62 = bf16[16,16,256]{2,1,0:T(8,128)(2,1)S(1)} all-to-all(bf16[16,16,256]{2,1,0:T(8,128)(2,1)S(1)} %attend.2), channel_id=1, replica_groups=mesh['section'=16,'ep'=16] {'ep'}, dimensions={0} | all-to-all | bytes 262144 | tf_op jit(solution)/shard_map/all_to_all | solution.py:261
  57.6 0.0 copy-done.3
  57.6 0.6 outproj.2
  58.1 0.0 copy-start.10
  58.2 0.0 copy-start.11
  58.2 0.0 copy-start.17
  58.2 0.0 copy-start.20
  58.2 0.0 copy-start.1
  58.2 22.8 %all_to_all.63.got_ref = bf16[16,16,3072]{2,1,0:T(8,128)(2,1)S(1)} all-to-all(bf16[16,16,3072]{2,1,0:T(8,128)(2,1)S(1)} %bitcast.41), channel_id=1, replica_groups=mesh['section'=16,'ep'=16] {'ep'}, dimensions={0} | all-to-all | bytes 3145728 | tf_op jit(solution)/shard_map/all_to_all | solution.py:261
  81.0 0.0 copy-done.10
  81.0 0.0 copy-done.11
  81.0 0.0 copy-done.17
  81.0 0.0 copy-done.20
  81.0 0.0 copy-start
  81.0 0.5 residual.2
  81.6 14.5 %all_to_all.64 = bf16[16,8,3072]{2,1,0:T(8,128)(2,1)S(1)} all-to-all(bf16[16,8,3072]{2,1,0:T(8,128)(2,1)S(1)} %get-tuple-element.15), channel_id=1, replica_groups=mesh['section'=16,'ep'=16] {'ep'}, dimensions={0} | all-to-all | bytes 1572864 | tf_op jit(solution)/shard_map/all_to_all | solution.py:261
  96.1 0.0 copy-done.1
  96.1 2.3 expert.2
  98.4 0.0 copy-start.16
  98.4 0.0 copy-start.19
  98.4 14.6 %all_to_all.65.got_ref = bf16[16,8,3072]{2,1,0:T(8,128)(2,1)S(1)} all-to-all(bf16[16,8,3072]{2,1,0:T(8,128)(2,1)S(1)} %bitcast.48), channel_id=1, replica_groups=mesh['section'=16,'ep'=16] {'ep'}, dimensions={0} | all-to-all | bytes 1572864 | tf_op jit(solution)/shard_map/all_to_all | solution.py:261
  113.0 0.4 combine.2
  113.4 1.9 collective-permute-start
  115.3 4.0 %collective-permute-done.shifted_ref = bf16[16,3072]{1,0:T(8,128)(2,1)S(1)} collective-permute-done((bf16[16,3072]{1,0:T(8,128)(2,1)S(1)}, bf16[16,3072]{1,0:T(8,128)(2,1)S(1)}, u32[]{:S(2)}, u32[]{:S(2)}) %collective-permute-start) | collective-permute-done | bytes 98336 | tf_op jit(solution)/shard_map/ppermute | solution.py:337
  119.3 0.0 copy-done.19
  119.3 0.3 select_norm.1
  119.6 26.8 %all_to_all.66 = bf16[16,16,3072]{2,1,0:T(8,128)(2,1)S(1)} all-to-all(bf16[16,16,3072]{2,1,0:T(8,128)(2,1)S(1)} %get-tuple-element.17), channel_id=1, replica_groups=mesh['section'=16,'ep'=16] {'ep'}, dimensions={0} | all-to-all | bytes 3145728 | tf_op jit(solution)/shard_map/all_to_all | solution.py:261
  146.4 1.0 project.3
  147.4 11.5 %all_to_all.67.got_ref = bf16[16,16,384]{2,1,0:T(8,128)(2,1)S(1)} all-to-all(bf16[16,16,384]{2,1,0:T(8,128)(2,1)S(1)} %bitcast.56), channel_id=1, replica_groups=mesh['section'=16,'ep'=16] {'ep'}, dimensions={0} | all-to-all | bytes 393216 | tf_op jit(solution)/shard_map/all_to_all | solution.py:261
  158.9 2.3 attend.3
  161.2 11.0 %all_to_all.68 = bf16[16,16,256]{2,1,0:T(8,128)(2,1)S(1)} all-to-all(bf16[16,16,256]{2,1,0:T(8,128)(2,1)S(1)} %attend.3), channel_id=1, replica_groups=mesh['section'=16,'ep'=16] {'ep'}, dimensions={0} | all-to-all | bytes 262144 | tf_op jit(solution)/shard_map/all_to_all | solution.py:261
  172.1 0.6 outproj.3
  172.7 23.6 %all_to_all.69.got_ref = bf16[16,16,3072]{2,1,0:T(8,128)(2,1)S(1)} all-to-all(bf16[16,16,3072]{2,1,0:T(8,128)(2,1)S(1)} %bitcast.42), channel_id=1, replica_groups=mesh['section'=16,'ep'=16] {'ep'}, dimensions={0} | all-to-all | bytes 3145728 | tf_op jit(solution)/shard_map/all_to_all | solution.py:261
  196.3 0.5 residual.3
  196.8 14.4 %all_to_all.70 = bf16[16,8,3072]{2,1,0:T(8,128)(2,1)S(1)} all-to-all(bf16[16,8,3072]{2,1,0:T(8,128)(2,1)S(1)} %get-tuple-element.20), channel_id=1, replica_groups=mesh['section'=16,'ep'=16] {'ep'}, dimensions={0} | all-to-all | bytes 1572864 | tf_op jit(solution)/shard_map/all_to_all | solution.py:261
  211.2 2.2 expert.3
  213.5 14.5 %all_to_all.71.got_ref = bf16[16,8,3072]{2,1,0:T(8,128)(2,1)S(1)} all-to-all(bf16[16,8,3072]{2,1,0:T(8,128)(2,1)S(1)} %bitcast.50), channel_id=1, replica_groups=mesh['section'=16,'ep'=16] {'ep'}, dimensions={0} | all-to-all | bytes 1572864 | tf_op jit(solution)/shard_map/all_to_all | solution.py:261
  228.0 1.1 combine.3
  (6 shorter events, 0.0 us)
Async XLA Ops:
  0.0 0.9 copy-start.9
  0.9 0.7 copy-start.18
  2.0 29.8 %copy-start.4 = (bf16[1,3072,256]{2,1,0:T(8,128)(2,1)S(1)}, bf16[1,3072,256]{2,1,0:T(8,128)(2,1)}, u32[]{:S(2)}) copy-start(bf16[1,3072,256]{2,1,0:T(8,128)(2,1)} %param.25) | copy-start | bytes 4718596
  2.0 29.8 %copy-start.7 = (bf16[1,3072,64]{1,2,0:T(8,128)(2,1)S(1)}, bf16[1,3072,64]{1,2,0:T(8,128)(2,1)}, u32[]{:S(2)}) copy-start(bf16[1,3072,64]{1,2,0:T(8,128)(2,1)} %param.26) | copy-start | bytes 1179652
  2.0 29.8 %copy-start.8 = (bf16[1,3072,64]{1,2,0:T(8,128)(2,1)S(1)}, bf16[1,3072,64]{1,2,0:T(8,128)(2,1)}, u32[]{:S(2)}) copy-start(bf16[1,3072,64]{1,2,0:T(8,128)(2,1)} %param.27) | copy-start | bytes 1179652
  31.8 12.5 %copy-start.5 = (bf16[1,2,16,8,16,128]{5,4,3,2,1,0:T(8,128)(2,1)S(1)}, bf16[1,2,16,8,16,128]{5,4,3,2,1,0:T(8,128)(2,1)}, u32[]{:S(2)}) copy-start(bf16[1,2,16,8,16,128]{5,4,3,2,1,0:T(8,128)(2,1)} %key_ref.3) | copy-start | bytes 3145732
  31.8 12.5 %copy-start.6 = (bf16[1,2,16,8,16,128]{5,4,3,2,1,0:T(8,128)(2,1)S(1)}, bf16[1,2,16,8,16,128]{5,4,3,2,1,0:T(8,128)(2,1)}, u32[]{:S(2)}) copy-start(bf16[1,2,16,8,16,128]{5,4,3,2,1,0:T(8,128)(2,1)} %value_ref.3) | copy-start | bytes 3145732
  31.8 12.5 %copy-start.12 = (f32[1,2,16,8,4]{2,4,3,1,0:T(4,128)S(1)}, f32[1,2,16,8,4]{2,4,3,1,0:T(4,128)}, u32[]{:S(2)}) copy-start(f32[1,2,16,8,4]{2,4,3,1,0:T(4,128)} %param.35) | copy-start | bytes 12292
  31.8 12.5 %copy-start.13 = (f32[1,2,16,8,4]{2,4,3,1,0:T(4,128)S(1)}, f32[1,2,16,8,4]{2,4,3,1,0:T(4,128)}, u32[]{:S(2)}) copy-start(f32[1,2,16,8,4]{2,4,3,1,0:T(4,128)} %param.36) | copy-start | bytes 12292
  31.8 12.5 %copy-start.14 = (f32[32,256]{1,0:T(8,128)S(1)}, f32[32,256]{1,0:T(8,128)}, u32[]{:S(2)}) copy-start(f32[32,256]{1,0:T(8,128)} %constant.2.clone.rotary_ref) | copy-start | bytes 98308
  31.8 12.5 %copy-start.15 = (s32[17,256]{1,0:T(8,128)S(1)}, s32[17,256]{1,0:T(8,128)}, u32[]{:S(2)}) copy-start(s32[17,256]{1,0:T(8,128)} %lens_ref.3) | copy-start | bytes 52228
  32.8 24.7 %copy-start.3 = (bf16[1,256,3072]{2,1,0:T(8,128)(2,1)S(1)}, bf16[1,256,3072]{2,1,0:T(8,128)(2,1)}, u32[]{:S(2)}) copy-start(bf16[1,256,3072]{2,1,0:T(8,128)(2,1)} %wo_ref.3) | copy-start | bytes 4718596
  57.6 38.5 %copy-start.2 = (bf16[1,448,3072]{2,1,0:T(8,128)(2,1)S(1)}, bf16[1,448,3072]{2,1,0:T(8,128)(2,1)}, u32[]{:S(2)}) copy-start(bf16[1,448,3072]{2,1,0:T(8,128)(2,1)} %down_ref.3) | copy-start | bytes 8257540
  58.1 22.8 %copy-start.10 = (bf16[16,3072]{1,0:T(8,128)(2,1)S(1)}, bf16[16,3072]{1,0:T(8,128)(2,1)}, u32[]{:S(2)}) copy-start(bf16[16,3072]{1,0:T(8,128)(2,1)} %x_ref.1) | copy-start | bytes 294916
  58.2 22.8 %copy-start.11 = (bf16[1,3072,8]{1,2,0:T(8,128)(2,1)S(1)}, bf16[1,3072,8]{1,2,0:T(8,128)(2,1)}, u32[]{:S(2)}) copy-start(bf16[1,3072,8]{1,2,0:T(8,128)(2,1)} %param.29) | copy-start | bytes 147460
  58.2 22.8 %copy-start.17 = (bf16[1,3072]{1,0:T(2,128)(2,1)S(1)}, bf16[1,3072]{1,0:T(2,128)(2,1)}, u32[]{:S(2)}) copy-start(bf16[1,3072]{1,0:T(2,128)(2,1)} %gain_ref.5) | copy-start | bytes 18436
  58.2 22.8 %copy-start.20 = (s32[1,2,16,2]{2,3,1,0:T(2,128)S(1)}, s32[1,2,16,2]{2,3,1,0:T(2,128)}, u32[]{:S(2)}) copy-start(s32[1,2,16,2]{2,3,1,0:T(2,128)} %param.22) | copy-start | bytes 772
  58.2 37.9 %copy-start.1 = (bf16[1,3072,448]{1,2,0:T(8,128)(2,1)S(1)}, bf16[1,3072,448]{1,2,0:T(8,128)(2,1)}, u32[]{:S(2)}) copy-start(bf16[1,3072,448]{1,2,0:T(8,128)(2,1)} %param.31) | copy-start | bytes 8257540
  81.0 15.1 %copy-start = (bf16[1,3072,448]{1,2,0:T(8,128)(2,1)S(1)}, bf16[1,3072,448]{1,2,0:T(8,128)(2,1)}, u32[]{:S(2)}) copy-start(bf16[1,3072,448]{1,2,0:T(8,128)(2,1)} %param.30) | copy-start | bytes 8257540
  98.4 20.9 %copy-start.16 = (bf16[16,3072]{1,0:T(8,128)(2,1)S(1)}, bf16[16,3072]{1,0:T(8,128)(2,1)}, u32[]{:S(2)}) copy-start(bf16[16,3072]{1,0:T(8,128)(2,1)} %entering_ref.1) | copy-start | bytes 294916
  98.4 20.9 %copy-start.19 = (bf16[1,3072]{1,0:T(2,128)(2,1)S(1)}, bf16[1,3072]{1,0:T(2,128)(2,1)}, u32[]{:S(2)}) copy-start(bf16[1,3072]{1,0:T(2,128)(2,1)} %gain_ref.4) | copy-start | bytes 18436
  113.4 5.9 %collective-permute-start = (bf16[16,3072]{1,0:T(8,128)(2,1)S(1)}, bf16[16,3072]{1,0:T(8,128)(2,1)S(1)}, u32[]{:S(2)}, u32[]{:S(2)}) collective-permute-start(bf16[16,3072]{1,0:T(8,128)(2,1)S(1)} %combine.2), channel_id=1, source_target_pairs={{0,16},{16,32},{32,48},{48,64},{64,80},{80,96},{96,112},{112,128},... | collective-permute-start | bytes 294920 | tf_op jit(solution)/shard_map/ppermute | solution.py:337

commit v3 on v2

--- a/solution.py
+++ b/solution.py
@@ -20,6 +20,8 @@
 EP = 16
 TOK = 16
 CHUNK = 512
+HALF = D // 2
+QKV = 384
 
 rope_base = 1000000.0
 norm_eps = 1e-05
@@ -59,17 +61,57 @@
     return [slice(c, c + CHUNK) for c in range(0, D, CHUNK)]
 
 
-def spread_normed(x_ref, gain_ref, copies_ref):
+def turn_of():
+    return lax.axis_index("section") & 1
+
+
+def x_partner(device, turn):
+    x = device & 3
+    odd = ((((x + 1) & 3) ^ 1) + 3) & 3
+    return (device - x) + jnp.where(turn == 0, x ^ 1, odd)
+
+
+def y_partner(device, turn):
+    y = device >> 2
+    odd = ((((y + 1) & 3) ^ 1) + 3) & 3
+    return (device & 3) + 4 * jnp.where(turn == 0, y ^ 1, odd)
+
+
+def partner_list(partner, sections):
+    def odd_pair(v):
+        return ((((v + 1) & 3) ^ 1) + 3) & 3
+
+    pairs = []
+    for section in range(sections):
+        for device in range(EP):
+            y, x = divmod(device, 4)
+            if partner == "x":
+                x = x ^ 1 if section % 2 == 0 else odd_pair(x)
+            else:
+                y = y ^ 1 if section % 2 == 0 else odd_pair(y)
+            pairs.append((section * EP + device, section * EP + 4 * y + x))
+    return pairs
+
+
+def spread_normed(x_ref, gain_ref, copies_ref, halves):
     total = jnp.zeros((TOK, 1), f32)
     for cols in columns():
         wide = x_ref[:, cols].astype(f32)
         total = total + jnp.sum(wide * wide, axis=-1, keepdims=True)
     factor = lax.rsqrt(total / D + norm_eps)
+    turn = turn_of()
     for cols in columns():
         wide = x_ref[:, cols].astype(f32)
         rows = (wide * factor * gain_ref[:, cols].astype(f32)).astype(bf16)
-        for dest in range(EP):
-            copies_ref[dest, :, cols] = rows
+        if not halves:
+            for dest in range(EP):
+                copies_ref[dest, :, cols] = rows
+        else:
+            part = cols.start // HALF
+            kept = slice(cols.start - part * HALF, cols.stop - part * HALF)
+            for k in range(2):
+                for x in range(4):
+                    copies_ref[(2 * k + (turn ^ part)) * 4 + x, :, kept] = rows
 
 
 def norm_body(x_hbm, gain_hbm, copies_ref, x_ref, gain_ref, sems):
@@ -81,7 +123,7 @@
         fetch.start()
     for fetch in fetches:
         fetch.wait()
-    spread_normed(x_ref, gain_ref, copies_ref)
+    spread_normed(x_ref, gain_ref, copies_ref, False)
 
 
 def norm_select_body(entering_ref, shifted_ref, gain_ref, x_ref, copies_ref):
@@ -95,7 +137,7 @@
     def _():
         x_ref[...] = shifted_ref[...]
 
-    spread_normed(x_ref, gain_ref, copies_ref)
+    spread_normed(x_ref, gain_ref, copies_ref, True)
 
 
 def project_body(x_ref, wq_ref, wk_ref, wv_ref, out_ref):
@@ -103,6 +145,17 @@
     out_ref[:, 0:256] = jnp.dot(x, wq_ref[...], preferred_element_type=f32).astype(bf16)
     both = jnp.concatenate([wk_ref[...], wv_ref[...]], axis=0)
     out_ref[:, 256:384] = dot_last(x, both).astype(bf16)
+
+
+def project_halves_body(x_ref, wq_ref, wk_ref, wv_ref, q_ref, kv_ref, out_ref):
+    x = x_ref[...]
+    at = pl.multiple_of(((lax.axis_index("ep") >> 2) + turn_of()) % 2 * HALF, HALF)
+    own_q = wq_ref[pl.ds(at, HALF), :]
+    own_kv = jnp.concatenate([wk_ref[:, pl.ds(at, HALF)], wv_ref[:, pl.ds(at, HALF)]], axis=0)
+    out_ref[:, 0:256] = jnp.dot(x, own_q, preferred_element_type=f32).astype(bf16)
+    out_ref[:, 256:QKV] = dot_last(x, own_kv).astype(bf16)
+    out_ref[:, QKV : QKV + 256] = jnp.dot(x, q_ref[...], preferred_element_type=f32).astype(bf16)
+    out_ref[:, QKV + 256 : 2 * QKV] = dot_last(x, kv_ref[...]).astype(bf16)
 
 
 def rotary_table():
@@ -121,6 +174,15 @@
     pos = TOK * LEN
     lane = lax.broadcasted_iota(jnp.int32, (TOK, HD), 1)
     low = lane < HD // 2
+    turn = turn_of()
+
+    def rows_of(src, start, stop):
+        rows = got_ref[src, :, start:stop].astype(f32)
+        if tick == 1:
+            other = got_ref[y_partner(src, turn), :, QKV + start : QKV + stop].astype(f32)
+            rows = (rows + other).astype(bf16).astype(f32)
+        return rows
+
     row_lens = lens_ref[pl.ds(lax.axis_index("section") + 1 - tick, 1), :].astype(f32)
     mine = lax.broadcasted_iota(jnp.int32, (TOK, row_lens.shape[1]), 0) + lax.axis_index("ep") * TOK
     there = lax.broadcasted_iota(jnp.int32, (TOK, row_lens.shape[1]), 1)
@@ -152,13 +214,13 @@
     live_one = (col // LEN == row) & (col % LEN < lens)
     live = jnp.concatenate([live_one.astype(f32)] * group, axis=0) > 0.5
     for g in range(KVH):
-        first = got_ref[2 * g, :, 256:384].astype(f32)
-        second = got_ref[2 * g + 1, :, 256:384].astype(f32)
+        first = rows_of(2 * g, 256, QKV)
+        second = rows_of(2 * g + 1, 256, QKV)
         key_new = turned(jnp.where(low, first, pltpu.roll(second, HD // 2, 1))).astype(f32)
         value_new = jnp.where(low, pltpu.roll(first, HD // 2, 1), second)
         q = jnp.concatenate(
             [
-                turned(got_ref[2 * g + r // 2, :, (r % 2) * HD : (r % 2 + 1) * HD].astype(f32))
+                turned(rows_of(2 * g + r // 2, (r % 2) * HD, (r % 2 + 1) * HD))
                 for r in range(group)
             ],
             axis=0,
@@ -183,13 +245,19 @@
         mixed = mixed + e_own * jnp.concatenate([value_new] * group, axis=0)
         done = (mixed / denom).astype(bf16)
         for r in range(group):
-            out_ref[2 * g + r // 2, :, (r % 2) * HD : (r % 2 + 1) * HD] = done[
-                r * TOK : (r + 1) * TOK
-            ]
-
-
-def out_body(att_ref, wo_ref, part_ref):
-    part_ref[...] = jnp.dot(att_ref[...], wo_ref[0], preferred_element_type=f32).astype(bf16)
+            rows = done[r * TOK : (r + 1) * TOK]
+            at = (r % 2) * HD
+            owner = 2 * g + r // 2
+            out_ref[owner, :, at : at + HD] = rows
+            out_ref[x_partner(owner, turn), :, 256 + at : 256 + at + HD] = rows
+
+
+def out_body(att_ref, wo_ref, other_ref, part_ref):
+    at = pl.multiple_of((lax.axis_index("ep") + turn_of()) % 2 * HALF, HALF)
+    own = wo_ref[0, :, pl.ds(at, HALF)]
+    total = jnp.dot(att_ref[:, 0:256], own, preferred_element_type=f32)
+    total = total + jnp.dot(att_ref[:, 256:512], other_ref[...], preferred_element_type=f32)
+    part_ref[...] = total.astype(bf16)
 
 
 def residual_body(
@@ -209,9 +277,12 @@
     sel = jnp.where((held > 0.5) & (rank == slot), 1.0, 0.0).astype(f32)
     total = jnp.zeros((TOK, 1), f32)
     for cols in columns():
-        acc = got_ref[0, :, cols].astype(f32)
-        for src in range(1, EP):
-            acc = acc + got_ref[src, :, cols].astype(f32)
+        part = cols.start // HALF
+        held_cols = slice(cols.start - part * HALF, cols.stop - part * HALF)
+        first = turn_of() ^ part
+        acc = got_ref[first, :, held_cols].astype(f32)
+        for pair in range(1, EP // 2):
+            acc = acc + got_ref[2 * pair + first, :, held_cols].astype(f32)
         rounded = (x_ref[:, cols].astype(f32) + acc).astype(bf16)
         res_ref[:, cols] = rounded
         wide = rounded.astype(f32)
@@ -289,21 +360,55 @@
         jnp.transpose(w[0], (1, 0)) for w in (wk, wv, router, w_gate, w_up)
     )
 
-    def run_layer(x, copies, tick):
-        everyone = trade(copies).reshape(EP * TOK, D)
-        projected = call(project_body, sds((EP * TOK, 384), bf16), 4, name="project")(
-            everyone, wq[0], wk_t, wv_t
-        )
-        got = trade(projected.reshape(EP, TOK, 384))
+    turn = turn_of()
+    ep_index = lax.axis_index("ep")
+    sections = lax.axis_size("section")
+    sent_depth = ((ep_index >> 2) + turn + 1) % 2 * HALF
+    sent_cols = (ep_index + turn + 1) % 2 * HALF
+    both = ("section", "ep")
+    sent_wo = lax.dynamic_slice(wo[0], (0, sent_cols), (256, HALF))
+    sent_q = lax.dynamic_slice(wq[0], (sent_depth, 0), (HALF, 256))
+    sent_kv = jnp.concatenate(
+        [lax.dynamic_slice(w, (0, sent_depth), (64, HALF)) for w in (wk_t, wv_t)], axis=0
+    )
+    others = (
+        lax.ppermute(sent_wo, both, partner_list("x", sections)),
+        lax.ppermute(sent_q, both, partner_list("y", sections)),
+        lax.ppermute(sent_kv, both, partner_list("y", sections)),
+    )
+
+    copies = call(
+        norm_body,
+        sds((EP, TOK, D), bf16),
+        2,
+        name="norm",
+        scratch=[
+            pltpu.VMEM((TOK, D), bf16),
+            pltpu.VMEM((1, D), bf16),
+            pltpu.SemaphoreType.DMA((2,)),
+        ],
+        space=pltpu.HBM,
+    )(states, attn_norm)
+    everyone = trade(copies)
+    projected = call(project_body, sds((EP * TOK, QKV), bf16), 4, name="project")(
+        everyone.reshape(EP * TOK, D), wq[0], wk_t, wv_t
+    )
+
+    def run_layer(x, projected, tick, others):
+        got = trade(projected.reshape(EP, TOK, projected.shape[1]))
         attended = call(
             functools.partial(attention_body, tick),
-            sds((EP, TOK, 256), bf16),
+            sds((EP, TOK, 512), bf16),
             7,
             name="attend",
         )(got, seq_lens, rotary, ks, vs, cache_k, cache_v)
-        heads = trade(attended).reshape(EP * TOK, 256)
-        part = call(out_body, sds((EP * TOK, D), bf16), 2, name="outproj")(heads, wo)
-        sums = trade(part.reshape(EP, TOK, D))
+        if tick == 0:
+            attended, *others = lax.optimization_barrier((attended, *others))
+        heads = trade(attended)
+        part = call(out_body, sds((EP * TOK, HALF), bf16), 3, name="outproj")(
+            heads.reshape(EP * TOK, 512), wo, others[0]
+        )
+        sums = trade(part.reshape(EP, TOK, HALF))
         residual, slots, coef = call(
             functools.partial(residual_body, tick),
             (sds((TOK, D), bf16), sds((EP, CAP, D), bf16), sds((CAP, TOK), f32)),
@@ -316,32 +421,22 @@
             landed, gate_t, up_t, w_down
         )
         returned = trade(pieces.reshape(EP, CAP, D))
-        return call(combine_body, sds((TOK, D), bf16), 3, name="combine")(
-            residual, coef, returned
-        )
-
-    copies = call(
-        norm_body,
-        sds((EP, TOK, D), bf16),
-        2,
-        name="norm",
-        scratch=[
-            pltpu.VMEM((TOK, D), bf16),
-            pltpu.VMEM((1, D), bf16),
-            pltpu.SemaphoreType.DMA((2,)),
-        ],
-        space=pltpu.HBM,
-    )(states, attn_norm)
-    first_out = run_layer(states, copies, 0)
-    count = lax.axis_size("section")
-    shifted = lax.ppermute(first_out, "section", [(i, i + 1) for i in range(count - 1)])
+        out = call(combine_body, sds((TOK, D), bf16), 3, name="combine")(residual, coef, returned)
+        return out, others
+
+    first_out, others = run_layer(states, projected, 0, others)
+    shifted = lax.ppermute(first_out, "section", [(i, i + 1) for i in range(sections - 1)])
     second_in, copies = call(
         norm_select_body,
-        (sds((TOK, D), bf16), sds((EP, TOK, D), bf16)),
+        (sds((TOK, D), bf16), sds((EP, TOK, HALF), bf16)),
         3,
         name="select_norm",
     )(entering, shifted, attn_norm)
-    return run_layer(second_in, copies, 1)
+    everyone = trade(copies).reshape(EP * TOK, HALF)
+    projected = call(project_halves_body, sds((EP * TOK, 2 * QKV), bf16), 6, name="project2")(
+        everyone, wq[0], wk_t, wv_t, others[1], others[2]
+    )
+    return run_layer(second_in, projected, 1, others)[0]
 
 
 def solution(mesh):

time: 230 us -> 216 us (0.939)
  blocking collectives: 206 us -> 154 us
  waiting for transfers between devices: 4.01 us -> 21.9 us
  starting transfers between devices: 1.92 us -> 13 us
  Pallas kernels: 15.3 us -> 21.4 us
  local copies, waits for them, and re-layouts: 1.72 us -> 4.63 us
    all_to_all x12 -> x11, blocking collectives: 206 us -> 154 us  [trade(): return lax.all_to_all(pieces, 'ep', split_axis=0, concat_axis=0, tiled=True)]
    all_to_all x0 -> x1, waiting for transfers between devices: none -> 17.9 us  [trade(): return lax.all_to_all(pieces, 'ep', split_axis=0, concat_axis=0, tiled=True)]
    all_to_all x0 -> x1, starting transfers between devices: none -> 7.22 us  [trade(): return lax.all_to_all(pieces, 'ep', split_axis=0, concat_axis=0, tiled=True)]
    pallas_call x7, Pallas kernels: 7.9 us -> 13 us  [the longest x2 4.58 us: run_layer(): call(functools.partial(attention_body, tick), sds((EP, TOK, 512), bf16),...]
    ppermute x1 -> x4, starting transfers between devices: 1.92 us -> 5.82 us  [the longest x1 1.92 us: local(): lax.ppermute(first_out, 'section', [(i, i + 1) for i in range(sections -...]
  transfers between devices with their start and end apart: 1 -> 5, of which waited for: 1 -> 2; matrix products, arithmetic and copies ran while one was open for 0% -> 1% of each run, Pallas kernels for 0% -> 2%
where the time goes in v3:
time: 216 us
  blocking collectives  154 us (71%)
  waiting for transfers between devices  21.9 us (10%)
  Pallas kernels  21.4 us (10%)
  starting transfers between devices  13 us (6%)
  local copies, waits for them, and re-layouts  4.63 us (2%)
    all_to_all x11, blocking collectives, trade(): return lax.all_to_all(pieces, 'ep', split_axis=0, concat_axis=0, tiled=True)  154 us
    all_to_all x1, waiting for transfers between devices, trade(): return lax.all_to_all(pieces, 'ep', split_axis=0, concat_axis=0, tiled=True)  17.9 us
    all_to_all x1, starting transfers between devices, trade(): return lax.all_to_all(pieces, 'ep', split_axis=0, concat_axis=0, tiled=True)  7.22 us
    pallas_call x2, Pallas kernels, run_layer(): call(functools.partial(attention_body, tick), sds((EP, TOK, 512), bf16),...  4.58 us
    pallas_call x2, Pallas kernels, run_layer(): call(expert_body, sds((EP * CAP, D), bf16), 4, name='expert', limit=16)  4.5 us
  transfers between devices with their start and end apart: 5, of which 2 were waited for; matrix products, arithmetic and copies ran while one was open for 1% of the time, Pallas kernels for 2%

profile of v3, /device:TPU:96, one launch (start us, length us, event | category | flops | bytes accessed | tf_op | source)
XLA Modules:
  0.0 215.7 jit_solution(748322016871701028)
XLA Ops:
  0.0 0.9 copy-done.11
  0.9 0.7 copy-done.19
  1.6 1.5 norm.1
  3.1 0.0 copy-start.4
  3.1 7.2 %all-to-all-start = ((bf16[16,16,3072]{2,1,0:T(8,128)(2,1)}), bf16[16,16,3072]{2,1,0:T(8,128)(2,1)}, u32[]{:S(2)}, u32[]{:S(2)}) async-start(bf16[16,16,3072]{2,1,0:T(8,128)(2,1)} %norm.1), calls=%async_computation | async-start | bytes 3145728 | tf_op jit(solution)/shard_map/all_to_all | solution.py:332
  10.4 0.0 copy-start.3
  10.4 0.0 copy-done.4
  10.4 0.0 copy-start.7
  10.4 0.9 dynamic-slice_bitcast_fusion.1
  11.4 1.9 collective-permute-start
  13.3 0.0 copy-done.3
  13.3 1.0 dynamic-slice_bitcast_fusion
  14.2 1.5 collective-permute-start.1
  15.7 0.0 copy-done.7
  15.7 0.0 copy-done.8
  15.7 0.8 pad_maximum_fusion
  16.5 0.6 collective-permute-start.2
  17.1 17.9 %all-to-all-done = bf16[16,16,3072]{2,1,0:T(8,128)(2,1)} async-done(((bf16[16,16,3072]{2,1,0:T(8,128)(2,1)}), bf16[16,16,3072]{2,1,0:T(8,128)(2,1)}, u32[]{:S(2)}, u32[]{:S(2)}) %all-to-all-start) | async-done | bytes 1572896 | tf_op jit(solution)/shard_map/all_to_all | solution.py:332
  35.0 1.0 copy-done.9
  36.0 0.0 copy-start.16
  36.0 0.0 copy-start.17
  36.0 2.5 %project.1 = bf16[256,384]{1,0:T(8,128)(2,1)S(1)} custom-call(bf16[256,3072]{1,0:T(8,128)(2,1)} %bitcast.x_ref, bf16[3072,256]{1,0:T(8,128)(2,1)S(1)} %bitcast.53, bf16[64,3072]{1,0:T(8,128)(2,1)S(1)} %bitcast.62, bf16[64,3072]{1,0:T(8,128)(2,1)S(1)} %bitcast.64), custom_call_target="tpu_custom_call" | custom-call | tf_op jit(solution)/shard_map/project/pallas_call | solution.py:393
  38.5 11.0 %all_to_all.60.got_ref = bf16[16,16,384]{2,1,0:T(8,128)(2,1)S(1)} all-to-all(bf16[16,16,384]{2,1,0:T(8,128)(2,1)S(1)} %bitcast.69), channel_id=1, replica_groups=mesh['section'=16,'ep'=16] {'ep'}, dimensions={0} | all-to-all | bytes 393216 | tf_op jit(solution)/shard_map/all_to_all | solution.py:332
  49.6 0.0 copy-done.15
  49.6 0.0 copy-done.16
  49.6 0.0 copy-done.17
  49.6 0.0 copy-start.2
  49.6 2.3 %attend.2 = bf16[16,16,512]{2,1,0:T(8,128)(2,1)S(1)} custom-call(bf16[16,16,384]{2,1,0:T(8,128)(2,1)S(1)} %all_to_all.60.got_ref, s32[17,256]{1,0:T(8,128)S(1)} %copy-done.17, f32[32,256]{1,0:T(8,128)S(1)} %copy-done.16, f32[2,8,4,16]{3,2,1,0:T(4,128)S(1)} %bitcast.72, f32[2,8,4,16]{3,2,1,0:T(4,128)S(1)} %bitcast.74, ...), custom_call_target="tpu_custom_call" | custom-call | tf_op jit(solution)/shard_map/attend/pallas_call | solution.py:399
  51.9 0.0 collective-permute-done.2.kv_ref
  51.9 0.0 collective-permute-done.other_ref
  52.0 0.0 collective-permute-done.1.q_ref
  52.0 11.7 %all_to_all.61 = bf16[16,16,512]{2,1,0:T(8,128)(2,1)S(1)} all-to-all(bf16[16,16,512]{2,1,0:T(8,128)(2,1)S(1)} %attend.2), channel_id=1, replica_groups=mesh['section'=16,'ep'=16] {'ep'}, dimensions={0} | all-to-all | bytes 524288 | tf_op jit(solution)/shard_map/all_to_all | solution.py:332
  63.6 1.8 outproj.2
  65.5 0.0 copy-start.12
  65.5 0.0 copy-start.13
  65.5 0.0 copy-start.21
  65.5 0.0 copy-start.22
  65.5 0.0 copy-start
  65.6 15.3 %all_to_all.62.got_ref = bf16[16,16,1536]{2,1,0:T(8,128)(2,1)S(1)} all-to-all(bf16[16,16,1536]{2,1,0:T(8,128)(2,1)S(1)} %bitcast.61), channel_id=1, replica_groups=mesh['section'=16,'ep'=16] {'ep'}, dimensions={0} | all-to-all | bytes 1572864 | tf_op jit(solution)/shard_map/all_to_all | solution.py:332
  80.9 0.4 residual.2
  81.3 14.4 %all_to_all.63 = bf16[16,8,3072]{2,1,0:T(8,128)(2,1)S(1)} all-to-all(bf16[16,8,3072]{2,1,0:T(8,128)(2,1)S(1)} %get-tuple-element.21), channel_id=1, replica_groups=mesh['section'=16,'ep'=16] {'ep'}, dimensions={0} | all-to-all | bytes 1572864 | tf_op jit(solution)/shard_map/all_to_all | solution.py:332
  95.8 0.0 copy-done.2
  95.8 2.3 %expert.2 = bf16[128,3072]{1,0:T(8,128)(2,1)S(1)} custom-call(bf16[128,3072]{1,0:T(8,128)(2,1)S(1)} %bitcast.56, bf16[448,3072]{1,0:T(8,128)(2,1)S(1)} %bitcast.49, bf16[448,3072]{1,0:T(8,128)(2,1)S(1)} %bitcast.51, bf16[1,448,3072]{2,1,0:T(8,128)(2,1)S(1)} %copy-done.2), custom_call_target="tpu_custom_call" | custom-call | tf_op jit(solution)/shard_map/expert/pallas_call | solution.py:420
  98.0 0.0 copy-start.18
  98.0 0.0 copy-start.20
  98.1 14.6 %all_to_all.64.got_ref = bf16[16,8,3072]{2,1,0:T(8,128)(2,1)S(1)} all-to-all(bf16[16,8,3072]{2,1,0:T(8,128)(2,1)S(1)} %bitcast.57), channel_id=1, replica_groups=mesh['section'=16,'ep'=16] {'ep'}, dimensions={0} | all-to-all | bytes 1572864 | tf_op jit(solution)/shard_map/all_to_all | solution.py:332
  112.6 0.4 combine.2
  113.0 1.9 collective-permute-start.3
  115.0 4.0 %collective-permute-done.3.shifted_ref = bf16[16,3072]{1,0:T(8,128)(2,1)S(1)} collective-permute-done((bf16[16,3072]{1,0:T(8,128)(2,1)S(1)}, bf16[16,3072]{1,0:T(8,128)(2,1)S(1)}, u32[]{:S(2)}, u32[]{:S(2)}) %collective-permute-start.3) | collective-permute-done | bytes 98336 | tf_op jit(solution)/shard_map/ppermute | solution.py:428
  119.0 0.0 copy-done.18
  119.0 0.2 select_norm.1
  119.2 18.3 %all_to_all.65 = bf16[16,16,1536]{2,1,0:T(8,128)(2,1)S(1)} all-to-all(bf16[16,16,1536]{2,1,0:T(8,128)(2,1)S(1)} %get-tuple-element.23), channel_id=1, replica_groups=mesh['section'=16,'ep'=16] {'ep'}, dimensions={0} | all-to-all | bytes 1572864 | tf_op jit(solution)/shard_map/all_to_all | solution.py:332
  137.5 0.0 copy-done.10
  137.5 2.2 %project2.1 = bf16[256,768]{1,0:T(8,128)(2,1)S(1)} custom-call(bf16[256,1536]{1,0:T(8,128)(2,1)S(1)} %bitcast.55, bf16[3072,256]{1,0:T(8,128)(2,1)S(1)} %bitcast.54, bf16[64,3072]{1,0:T(8,128)(2,1)S(1)} %bitcast.63, bf16[64,3072]{1,0:T(8,128)(2,1)S(1)} %bitcast.65, bf16[1536,256]{1,0:T(8,128)(2,1)} %collective-permute-done.1.q_ref, ...), custom_call_target="tpu_custom_call" | custom-call | tf_op jit(solution)/shard_map/project2/pallas_call | solution.py:436
  139.7 12.8 %all_to_all.66.got_ref = bf16[16,16,768]{2,1,0:T(8,128)(2,1)S(1)} all-to-all(bf16[16,16,768]{2,1,0:T(8,128)(2,1)S(1)} %bitcast.66), channel_id=1, replica_groups=mesh['section'=16,'ep'=16] {'ep'}, dimensions={0} | all-to-all | bytes 786432 | tf_op jit(solution)/shard_map/all_to_all | solution.py:332
  152.5 2.3 %attend.3 = bf16[16,16,512]{2,1,0:T(8,128)(2,1)S(1)} custom-call(bf16[16,16,768]{2,1,0:T(8,128)(2,1)S(1)} %all_to_all.66.got_ref, s32[17,256]{1,0:T(8,128)S(1)} %copy-done.17, f32[32,256]{1,0:T(8,128)S(1)} %copy-done.16, f32[2,8,4,16]{3,2,1,0:T(4,128)S(1)} %bitcast.73, f32[2,8,4,16]{3,2,1,0:T(4,128)S(1)} %bitcast.75, ...), custom_call_target="tpu_custom_call" | custom-call | tf_op jit(solution)/shard_map/attend/pallas_call | solution.py:399
  154.8 11.6 %all_to_all.67 = bf16[16,16,512]{2,1,0:T(8,128)(2,1)S(1)} all-to-all(bf16[16,16,512]{2,1,0:T(8,128)(2,1)S(1)} %attend.3), channel_id=1, replica_groups=mesh['section'=16,'ep'=16] {'ep'}, dimensions={0} | all-to-all | bytes 524288 | tf_op jit(solution)/shard_map/all_to_all | solution.py:332
  166.4 1.7 outproj.3
  168.1 14.9 %all_to_all.68.got_ref = bf16[16,16,1536]{2,1,0:T(8,128)(2,1)S(1)} all-to-all(bf16[16,16,1536]{2,1,0:T(8,128)(2,1)S(1)} %bitcast.60), channel_id=1, replica_groups=mesh['section'=16,'ep'=16] {'ep'}, dimensions={0} | all-to-all | bytes 1572864 | tf_op jit(solution)/shard_map/all_to_all | solution.py:332
  183.0 0.4 residual.3
  183.5 14.4 %all_to_all.69 = bf16[16,8,3072]{2,1,0:T(8,128)(2,1)S(1)} all-to-all(bf16[16,8,3072]{2,1,0:T(8,128)(2,1)S(1)} %get-tuple-element.28), channel_id=1, replica_groups=mesh['section'=16,'ep'=16] {'ep'}, dimensions={0} | all-to-all | bytes 1572864 | tf_op jit(solution)/shard_map/all_to_all | solution.py:332
  197.9 2.3 %expert.3 = bf16[128,3072]{1,0:T(8,128)(2,1)S(1)} custom-call(bf16[128,3072]{1,0:T(8,128)(2,1)S(1)} %bitcast.58, bf16[448,3072]{1,0:T(8,128)(2,1)S(1)} %bitcast.50, bf16[448,3072]{1,0:T(8,128)(2,1)S(1)} %bitcast.52, bf16[1,448,3072]{2,1,0:T(8,128)(2,1)S(1)} %copy-done.2), custom_call_target="tpu_custom_call" | custom-call | tf_op jit(solution)/shard_map/expert/pallas_call | solution.py:420
  200.1 14.4 %all_to_all.70.got_ref = bf16[16,8,3072]{2,1,0:T(8,128)(2,1)S(1)} all-to-all(bf16[16,8,3072]{2,1,0:T(8,128)(2,1)S(1)} %bitcast.59), channel_id=1, replica_groups=mesh['section'=16,'ep'=16] {'ep'}, dimensions={0} | all-to-all | bytes 1572864 | tf_op jit(solution)/shard_map/all_to_all | solution.py:332
  214.6 1.1 combine.3
  (21 shorter events, 0.1 us)
Async XLA Ops:
  0.0 0.9 copy-start.11
  0.9 0.7 copy-start.19
  3.1 7.3 %copy-start.4 = (bf16[1,256,3072]{2,1,0:T(8,128)(2,1)S(1)}, bf16[1,256,3072]{2,1,0:T(8,128)(2,1)}, u32[]{:S(2)}) copy-start(bf16[1,256,3072]{2,1,0:T(8,128)(2,1)} %wo_ref.3) | copy-start | bytes 4718596
  3.1 31.8 %all-to-all-start = ((bf16[16,16,3072]{2,1,0:T(8,128)(2,1)}), bf16[16,16,3072]{2,1,0:T(8,128)(2,1)}, u32[]{:S(2)}, u32[]{:S(2)}) async-start(bf16[16,16,3072]{2,1,0:T(8,128)(2,1)} %norm.1), calls=%async_computation | async-start | bytes 3145728 | tf_op jit(solution)/shard_map/all_to_all | solution.py:332
  10.4 2.9 %copy-start.3 = (bf16[1,3072,256]{2,1,0:T(8,128)(2,1)S(1)}, bf16[1,3072,256]{2,1,0:T(8,128)(2,1)}, u32[]{:S(2)}) copy-start(bf16[1,3072,256]{2,1,0:T(8,128)(2,1)} %param.25) | copy-start | bytes 4718596
  10.4 5.3 %copy-start.7 = (bf16[1,3072,64]{1,2,0:T(8,128)(2,1)S(1)}, bf16[1,3072,64]{1,2,0:T(8,128)(2,1)}, u32[]{:S(2)}) copy-start(bf16[1,3072,64]{1,2,0:T(8,128)(2,1)} %param.26) | copy-start | bytes 1179652
  11.4 40.6 %collective-permute-start = (bf16[256,1536]{1,0:T(8,128)(2,1)}, bf16[256,1536]{1,0:T(8,128)(2,1)}, u32[]{:S(2)}, u32[]{:S(2)}) collective-permute-start(bf16[256,1536]{1,0:T(8,128)(2,1)} %dynamic-slice_bitcast_fusion.1), channel_id=1, source_target_pairs={{0,1},{1,0},{2,3},{3,2},{4,5},{5,4},{6,7},{7,6},{8,9},{9,8},{10,11... | collective-permute-start | bytes 2359304 | tf_op jit(solution)/shard_map/ppermute | solution.py:375
  13.3 2.4 %copy-start.8 = (bf16[1,3072,64]{1,2,0:T(8,128)(2,1)S(1)}, bf16[1,3072,64]{1,2,0:T(8,128)(2,1)}, u32[]{:S(2)}) copy-start(bf16[1,3072,64]{1,2,0:T(8,128)(2,1)} %param.27) | copy-start | bytes 1179652
  14.2 37.7 %collective-permute-start.1 = (bf16[1536,256]{1,0:T(8,128)(2,1)}, bf16[1536,256]{1,0:T(8,128)(2,1)}, u32[]{:S(2)}, u32[]{:S(2)}) collective-permute-start(bf16[1536,256]{1,0:T(8,128)(2,1)} %dynamic-slice_bitcast_fusion), channel_id=1, source_target_pairs={{0,4},{1,5},{2,6},{3,7},{4,0},{5,1},{6,2},{7,3},{8,12},{9,13},{10,... | collective-permute-start | bytes 2359304 | tf_op jit(solution)/shard_map/ppermute | solution.py:376
  16.5 35.4 %collective-permute-start.2 = (bf16[128,1536]{1,0:T(8,128)(2,1)}, bf16[128,1536]{1,0:T(8,128)(2,1)}, u32[]{:S(2)}, u32[]{:S(2)}) collective-permute-start(bf16[128,1536]{1,0:T(8,128)(2,1)} %pad_maximum_fusion), channel_id=1, source_target_pairs={{0,4},{1,5},{2,6},{3,7},{4,0},{5,1},{6,2},{7,3},{8,12},{9,13},{10,... | collective-permute-start | bytes 1179656 | tf_op jit(solution)/shard_map/ppermute | solution.py:377
  35.0 1.0 copy-start.9
  36.0 13.6 %copy-start.5 = (bf16[1,2,16,8,16,128]{5,4,3,2,1,0:T(8,128)(2,1)S(1)}, bf16[1,2,16,8,16,128]{5,4,3,2,1,0:T(8,128)(2,1)}, u32[]{:S(2)}) copy-start(bf16[1,2,16,8,16,128]{5,4,3,2,1,0:T(8,128)(2,1)} %key_ref.3) | copy-start | bytes 3145732
  36.0 13.6 %copy-start.6 = (bf16[1,2,16,8,16,128]{5,4,3,2,1,0:T(8,128)(2,1)S(1)}, bf16[1,2,16,8,16,128]{5,4,3,2,1,0:T(8,128)(2,1)}, u32[]{:S(2)}) copy-start(bf16[1,2,16,8,16,128]{5,4,3,2,1,0:T(8,128)(2,1)} %value_ref.3) | copy-start | bytes 3145732
  36.0 13.6 %copy-start.14 = (f32[1,2,16,8,4]{2,4,3,1,0:T(4,128)S(1)}, f32[1,2,16,8,4]{2,4,3,1,0:T(4,128)}, u32[]{:S(2)}) copy-start(f32[1,2,16,8,4]{2,4,3,1,0:T(4,128)} %param.35) | copy-start | bytes 12292
  36.0 13.6 %copy-start.15 = (f32[1,2,16,8,4]{2,4,3,1,0:T(4,128)S(1)}, f32[1,2,16,8,4]{2,4,3,1,0:T(4,128)}, u32[]{:S(2)}) copy-start(f32[1,2,16,8,4]{2,4,3,1,0:T(4,128)} %param.36) | copy-start | bytes 12292
  36.0 13.6 %copy-start.16 = (f32[32,256]{1,0:T(8,128)S(1)}, f32[32,256]{1,0:T(8,128)}, u32[]{:S(2)}) copy-start(f32[32,256]{1,0:T(8,128)} %constant.36.clone.rotary_ref) | copy-start | bytes 98308
  36.0 13.6 %copy-start.17 = (s32[17,256]{1,0:T(8,128)S(1)}, s32[17,256]{1,0:T(8,128)}, u32[]{:S(2)}) copy-start(s32[17,256]{1,0:T(8,128)} %lens_ref.3) | copy-start | bytes 52228
  49.6 46.1 %copy-start.2 = (bf16[1,448,3072]{2,1,0:T(8,128)(2,1)S(1)}, bf16[1,448,3072]{2,1,0:T(8,128)(2,1)}, u32[]{:S(2)}) copy-start(bf16[1,448,3072]{2,1,0:T(8,128)(2,1)} %down_ref.3) | copy-start | bytes 8257540
  63.6 32.1 %copy-start.1 = (bf16[1,3072,448]{1,2,0:T(8,128)(2,1)S(1)}, bf16[1,3072,448]{1,2,0:T(8,128)(2,1)}, u32[]{:S(2)}) copy-start(bf16[1,3072,448]{1,2,0:T(8,128)(2,1)} %param.31) | copy-start | bytes 8257540
  65.5 15.4 %copy-start.12 = (bf16[16,3072]{1,0:T(8,128)(2,1)S(1)}, bf16[16,3072]{1,0:T(8,128)(2,1)}, u32[]{:S(2)}) copy-start(bf16[16,3072]{1,0:T(8,128)(2,1)} %x_ref.1) | copy-start | bytes 294916
  65.5 15.4 %copy-start.13 = (bf16[1,3072,8]{1,2,0:T(8,128)(2,1)S(1)}, bf16[1,3072,8]{1,2,0:T(8,128)(2,1)}, u32[]{:S(2)}) copy-start(bf16[1,3072,8]{1,2,0:T(8,128)(2,1)} %param.29) | copy-start | bytes 147460
  65.5 15.4 %copy-start.21 = (bf16[1,3072]{1,0:T(2,128)(2,1)S(1)}, bf16[1,3072]{1,0:T(2,128)(2,1)}, u32[]{:S(2)}) copy-start(bf16[1,3072]{1,0:T(2,128)(2,1)} %gain_ref.5) | copy-start | bytes 18436
  65.5 15.3 %copy-start.22 = (s32[1,2,16,2]{2,3,1,0:T(2,128)S(1)}, s32[1,2,16,2]{2,3,1,0:T(2,128)}, u32[]{:S(2)}) copy-start(s32[1,2,16,2]{2,3,1,0:T(2,128)} %param.22) | copy-start | bytes 772
  65.5 30.2 %copy-start = (bf16[1,3072,448]{1,2,0:T(8,128)(2,1)S(1)}, bf16[1,3072,448]{1,2,0:T(8,128)(2,1)}, u32[]{:S(2)}) copy-start(bf16[1,3072,448]{1,2,0:T(8,128)(2,1)} %param.30) | copy-start | bytes 8257540
  98.0 20.9 %copy-start.18 = (bf16[16,3072]{1,0:T(8,128)(2,1)S(1)}, bf16[16,3072]{1,0:T(8,128)(2,1)}, u32[]{:S(2)}) copy-start(bf16[16,3072]{1,0:T(8,128)(2,1)} %entering_ref.1) | copy-start | bytes 294916
  98.0 20.9 %copy-start.20 = (bf16[1,3072]{1,0:T(2,128)(2,1)S(1)}, bf16[1,3072]{1,0:T(2,128)(2,1)}, u32[]{:S(2)}) copy-start(bf16[1,3072]{1,0:T(2,128)(2,1)} %gain_ref.4) | copy-start | bytes 18436
  112.6 24.9 %copy-start.10 = (bf16[1,3072,64]{1,2,0:T(8,128)(2,1)S(1)}, bf16[1,3072,64]{1,2,0:T(8,128)(2,1)}, u32[]{:S(2)}) copy-start(bf16[1,3072,64]{1,2,0:T(8,128)(2,1)} %param.27) | copy-start | bytes 1179652
  113.0 5.9 %collective-permute-start.3 = (bf16[16,3072]{1,0:T(8,128)(2,1)S(1)}, bf16[16,3072]{1,0:T(8,128)(2,1)S(1)}, u32[]{:S(2)}, u32[]{:S(2)}) collective-permute-start(bf16[16,3072]{1,0:T(8,128)(2,1)S(1)} %combine.2), channel_id=1, source_target_pairs={{0,16},{16,32},{32,48},{48,64},{64,80},{80,96},{96,112},{112,128},... | collective-permute-start | bytes 294920 | tf_op jit(solution)/shard_map/ppermute | solution.py:428

commit v4 on v3

--- a/solution.py
+++ b/solution.py
@@ -29,9 +29,12 @@
 bf16 = jnp.bfloat16
 
 
-def call(body, out_shape, n_in, smem=(), name=None, scratch=(), limit=12, space=pltpu.VMEM):
-    specs = [pl.BlockSpec(memory_space=pltpu.SMEM if i in smem else space) for i in range(n_in)]
-    outs = jax.tree.map(lambda _: pl.BlockSpec(memory_space=pltpu.VMEM), out_shape)
+def call(body, out_shape, n_in, far=(), far_out=False, name=None, scratch=(), limit=4):
+    specs = [
+        pl.BlockSpec(memory_space=pl.ANY if i in far else pltpu.VMEM) for i in range(n_in)
+    ]
+    space = pl.ANY if far_out else pltpu.VMEM
+    outs = jax.tree.map(lambda _: pl.BlockSpec(memory_space=space), out_shape)
     return pl.pallas_call(
         body,
         out_shape=out_shape,
@@ -93,7 +96,7 @@
     return pairs
 
 
-def spread_normed(x_ref, gain_ref, copies_ref, halves):
+def spread_halves(x_ref, gain_ref, copies_ref):
     total = jnp.zeros((TOK, 1), f32)
     for cols in columns():
         wide = x_ref[:, cols].astype(f32)
@@ -103,27 +106,29 @@
     for cols in columns():
         wide = x_ref[:, cols].astype(f32)
         rows = (wide * factor * gain_ref[:, cols].astype(f32)).astype(bf16)
-        if not halves:
-            for dest in range(EP):
-                copies_ref[dest, :, cols] = rows
-        else:
-            part = cols.start // HALF
-            kept = slice(cols.start - part * HALF, cols.stop - part * HALF)
-            for k in range(2):
-                for x in range(4):
-                    copies_ref[(2 * k + (turn ^ part)) * 4 + x, :, kept] = rows
-
-
-def norm_body(x_hbm, gain_hbm, copies_ref, x_ref, gain_ref, sems):
-    fetches = [
-        pltpu.make_async_copy(x_hbm, x_ref, sems.at[0]),
-        pltpu.make_async_copy(gain_hbm, gain_ref, sems.at[1]),
+        part = cols.start // HALF
+        kept = slice(cols.start - part * HALF, cols.stop - part * HALF)
+        for k in range(2):
+            for x in range(4):
+                copies_ref[(2 * k + (turn ^ part)) * 4 + x, :, kept] = rows
+
+
+def norm_body(x_ref, gain_ref, copies_hbm, rows_ref, sems):
+    total = jnp.zeros((TOK, 1), f32)
+    for cols in columns():
+        wide = x_ref[:, cols].astype(f32)
+        total = total + jnp.sum(wide * wide, axis=-1, keepdims=True)
+    factor = lax.rsqrt(total / D + norm_eps)
+    for cols in columns():
+        wide = x_ref[:, cols].astype(f32)
+        rows_ref[:, cols] = (wide * factor * gain_ref[:, cols].astype(f32)).astype(bf16)
+    sends = [
+        pltpu.make_async_copy(rows_ref, copies_hbm.at[dest], sems.at[dest]) for dest in range(EP)
     ]
-    for fetch in fetches:
-        fetch.start()
-    for fetch in fetches:
-        fetch.wait()
-    spread_normed(x_ref, gain_ref, copies_ref, False)
+    for send in sends:
+        send.start()
+    for send in sends:
+        send.wait()
 
 
 def norm_select_body(entering_ref, shifted_ref, gain_ref, x_ref, copies_ref):
@@ -137,23 +142,19 @@
     def _():
         x_ref[...] = shifted_ref[...]
 
-    spread_normed(x_ref, gain_ref, copies_ref, True)
-
-
-def project_body(x_ref, wq_ref, wk_ref, wv_ref, out_ref):
+    spread_halves(x_ref, gain_ref, copies_ref)
+
+
+def project_body(x_ref, wq_ref, kv_ref, out_ref):
     x = x_ref[...]
     out_ref[:, 0:256] = jnp.dot(x, wq_ref[...], preferred_element_type=f32).astype(bf16)
-    both = jnp.concatenate([wk_ref[...], wv_ref[...]], axis=0)
-    out_ref[:, 256:384] = dot_last(x, both).astype(bf16)
-
-
-def project_halves_body(x_ref, wq_ref, wk_ref, wv_ref, q_ref, kv_ref, out_ref):
+    out_ref[:, 256:QKV] = dot_last(x, kv_ref[...]).astype(bf16)
+
+
+def project_halves_body(x_ref, own_q_ref, own_kv_ref, q_ref, kv_ref, out_ref):
     x = x_ref[...]
-    at = pl.multiple_of(((lax.axis_index("ep") >> 2) + turn_of()) % 2 * HALF, HALF)
-    own_q = wq_ref[pl.ds(at, HALF), :]
-    own_kv = jnp.concatenate([wk_ref[:, pl.ds(at, HALF)], wv_ref[:, pl.ds(at, HALF)]], axis=0)
-    out_ref[:, 0:256] = jnp.dot(x, own_q, preferred_element_type=f32).astype(bf16)
-    out_ref[:, 256:QKV] = dot_last(x, own_kv).astype(bf16)
+    out_ref[:, 0:256] = jnp.dot(x, own_q_ref[...], preferred_element_type=f32).astype(bf16)
+    out_ref[:, 256:QKV] = dot_last(x, own_kv_ref[...]).astype(bf16)
     out_ref[:, QKV : QKV + 256] = jnp.dot(x, q_ref[...], preferred_element_type=f32).astype(bf16)
     out_ref[:, QKV + 256 : 2 * QKV] = dot_last(x, kv_ref[...]).astype(bf16)
 
@@ -253,11 +254,23 @@
 
 
 def out_body(att_ref, wo_ref, other_ref, part_ref):
-    at = pl.multiple_of((lax.axis_index("ep") + turn_of()) % 2 * HALF, HALF)
-    own = wo_ref[0, :, pl.ds(at, HALF)]
-    total = jnp.dot(att_ref[:, 0:256], own, preferred_element_type=f32)
+    total = jnp.dot(att_ref[:, 0:256], wo_ref[...], preferred_element_type=f32)
     total = total + jnp.dot(att_ref[:, 256:512], other_ref[...], preferred_element_type=f32)
     part_ref[...] = total.astype(bf16)
+
+
+def out_fetch_body(att_ref, wo_ref, *refs):
+    swapped, part_ref, fetched, sems = refs[:3], refs[3], refs[4:7], refs[7]
+    fetches = [
+        pltpu.make_async_copy(there, here, sems.at[i])
+        for i, (there, here) in enumerate(zip(swapped, fetched))
+    ]
+    for fetch in fetches:
+        fetch.start()
+    fetches[0].wait()
+    out_body(att_ref, wo_ref, fetched[0], part_ref)
+    for fetch in fetches[1:]:
+        fetch.wait()
 
 
 def residual_body(
@@ -366,11 +379,13 @@
     sent_depth = ((ep_index >> 2) + turn + 1) % 2 * HALF
     sent_cols = (ep_index + turn + 1) % 2 * HALF
     both = ("section", "ep")
+    kv = jnp.concatenate([wk_t, wv_t], axis=0)
     sent_wo = lax.dynamic_slice(wo[0], (0, sent_cols), (256, HALF))
     sent_q = lax.dynamic_slice(wq[0], (sent_depth, 0), (HALF, 256))
-    sent_kv = jnp.concatenate(
-        [lax.dynamic_slice(w, (0, sent_depth), (64, HALF)) for w in (wk_t, wv_t)], axis=0
-    )
+    sent_kv = lax.dynamic_slice(kv, (0, sent_depth), (128, HALF))
+    own_wo = lax.dynamic_slice(wo[0], (0, HALF - sent_cols), (256, HALF))
+    own_q = lax.dynamic_slice(wq[0], (HALF - sent_depth, 0), (HALF, 256))
+    own_kv = lax.dynamic_slice(kv, (0, HALF - sent_depth), (128, HALF))
     others = (
         lax.ppermute(sent_wo, both, partner_list("x", sections)),
         lax.ppermute(sent_q, both, partner_list("y", sections)),
@@ -381,33 +396,37 @@
         norm_body,
         sds((EP, TOK, D), bf16),
         2,
+        far_out=True,
         name="norm",
-        scratch=[
-            pltpu.VMEM((TOK, D), bf16),
-            pltpu.VMEM((1, D), bf16),
-            pltpu.SemaphoreType.DMA((2,)),
-        ],
-        space=pltpu.HBM,
+        scratch=[pltpu.VMEM((TOK, D), bf16), pltpu.SemaphoreType.DMA((EP,))],
     )(states, attn_norm)
-    everyone = trade(copies)
-    projected = call(project_body, sds((EP * TOK, QKV), bf16), 4, name="project")(
-        everyone.reshape(EP * TOK, D), wq[0], wk_t, wv_t
+    everyone, kv, own_wo, own_q, own_kv = lax.optimization_barrier(
+        (trade(copies).reshape(EP * TOK, D), kv, own_wo, own_q, own_kv)
+    )
+    projected = call(project_body, sds((EP * TOK, QKV), bf16), 3, name="project", limit=6)(
+        everyone, wq[0], kv
     )
 
     def run_layer(x, projected, tick, others):
         got = trade(projected.reshape(EP, TOK, projected.shape[1]))
         attended = call(
-            functools.partial(attention_body, tick),
-            sds((EP, TOK, 512), bf16),
-            7,
-            name="attend",
+            functools.partial(attention_body, tick), sds((EP, TOK, 512), bf16), 7, name="attend"
         )(got, seq_lens, rotary, ks, vs, cache_k, cache_v)
+        part = sds((EP * TOK, HALF), bf16)
         if tick == 0:
             attended, *others = lax.optimization_barrier((attended, *others))
-        heads = trade(attended)
-        part = call(out_body, sds((EP * TOK, HALF), bf16), 3, name="outproj")(
-            heads.reshape(EP * TOK, 512), wo, others[0]
-        )
+            heads = trade(attended).reshape(EP * TOK, 512)
+            part, *others = call(
+                out_fetch_body,
+                (part, *(sds(o.shape, bf16) for o in others)),
+                5,
+                far=(2, 3, 4),
+                name="outproj",
+                scratch=[pltpu.SemaphoreType.DMA((3,))],
+            )(heads, own_wo, *others)
+        else:
+            heads = trade(attended).reshape(EP * TOK, 512)
+            part = call(out_body, part, 3, name="outproj")(heads, own_wo, others[0])
         sums = trade(part.reshape(EP, TOK, HALF))
         residual, slots, coef = call(
             functools.partial(residual_body, tick),
@@ -417,7 +436,7 @@
             scratch=[pltpu.VMEM((TOK, D), bf16)],
         )(x, sums, ffn_norm, router_t, chosen)
         landed = trade(slots).reshape(EP * CAP, D)
-        pieces = call(expert_body, sds((EP * CAP, D), bf16), 4, name="expert", limit=16)(
+        pieces = call(expert_body, sds((EP * CAP, D), bf16), 4, name="expert", limit=8)(
             landed, gate_t, up_t, w_down
         )
         returned = trade(pieces.reshape(EP, CAP, D))
@@ -433,8 +452,8 @@
         name="select_norm",
     )(entering, shifted, attn_norm)
     everyone = trade(copies).reshape(EP * TOK, HALF)
-    projected = call(project_halves_body, sds((EP * TOK, 2 * QKV), bf16), 6, name="project2")(
-        everyone, wq[0], wk_t, wv_t, others[1], others[2]
+    projected = call(project_halves_body, sds((EP * TOK, 2 * QKV), bf16), 5, name="project2")(
+        everyone, own_q, own_kv, others[1], others[2]
     )
     return run_layer(second_in, projected, 1, others)[0]
 

time: 216 us -> 214 us (level)
  Pallas kernels: 21.4 us -> 18.9 us
  waiting for transfers between devices: 21.9 us -> 19.4 us
    all_to_all x1, waiting for transfers between devices: 17.9 us -> 15.4 us  [trade(): return lax.all_to_all(pieces, 'ep', split_axis=0, concat_axis=0, tiled=True)]
    pallas_call x7, Pallas kernels: 14.3 us -> 11.8 us  [the longest x2 4.49 us: run_layer(): call(expert_body, sds((EP * CAP, D), bf16), 4, name='expert', limit=8)]
  transfers between devices with their start and end apart: 5 -> 5, of which waited for: 2 -> 2; matrix products, arithmetic and copies ran while one was open for 1% -> 2% of each run, Pallas kernels for 2% -> 2%
where the time goes in v4:
time: 214 us; the launch traced here: 213 us
  blocking collectives  154 us (72%)
  waiting for transfers between devices  19.4 us (9%)
  Pallas kernels  18.9 us (9%)
  starting transfers between devices  12.9 us (6%)
  local copies, waits for them, and re-layouts  6.31 us (3%)
    all_to_all x11, blocking collectives, trade(): return lax.all_to_all(pieces, 'ep', split_axis=0, concat_axis=0, tiled=True)  154 us
    all_to_all x1, waiting for transfers between devices, trade(): return lax.all_to_all(pieces, 'ep', split_axis=0, concat_axis=0, tiled=True)  15.4 us
    all_to_all x1, starting transfers between devices, trade(): return lax.all_to_all(pieces, 'ep', split_axis=0, concat_axis=0, tiled=True)  7.09 us
    pallas_call x2, Pallas kernels, run_layer(): call(functools.partial(attention_body, tick), sds((EP, TOK, 512), bf16),...  4.57 us
    pallas_call x2, Pallas kernels, run_layer(): call(expert_body, sds((EP * CAP, D), bf16), 4, name='expert', limit=8)  4.49 us
  transfers between devices with their start and end apart: 5, of which 2 were waited for; matrix products, arithmetic and copies ran while one was open for 2% of the time, Pallas kernels for 2%

profile of v4, /device:TPU:96, one launch (start us, length us, event | category | flops | bytes accessed | tf_op | source)
XLA Modules:
  0.0 213.1 jit_solution(3856561399227376228)
XLA Ops:
  0.0 0.9 copy-done.7
  0.9 0.7 copy-done.15
  1.6 1.4 norm.1
  3.0 7.1 %all-to-all-start = ((bf16[16,16,3072]{2,1,0:T(8,128)(2,1)}), bf16[16,16,3072]{2,1,0:T(8,128)(2,1)}, u32[]{:S(2)}, u32[]{:S(2)}) async-start(bf16[16,16,3072]{2,1,0:T(8,128)(2,1)} %norm.1), calls=%async_computation | async-start | bytes 3145728 | tf_op jit(solution)/shard_map/all_to_all | solution.py:345
  10.1 0.0 copy-start.3
  10.1 2.5 %dynamic-slice_bitcast_fusion.1 = (bf16[256,1536]{1,0:T(8,128)(2,1)}, bf16[256,1536]{1,0:T(8,128)(2,1)S(1)}) fusion(bf16[1,256,3072]{2,1,0:T(8,128)(2,1)} %param.28, s32[]{:T(128)S(6)} %select_n.29, s32[]{:T(128)S(6)} %select_n.26), kind=kLoop, calls=%fused_computation.6 | loop fusion | bytes 3145736 | tf_op jit(solution)/shard_map/dynamic_slice | solution.py:383
  12.6 1.9 collective-permute-start
  14.5 0.0 copy-done.3
  14.5 1.0 dynamic-slice_bitcast_fusion
  15.5 1.5 collective-permute-start.1
  17.0 0.0 copy-done.19
  17.0 0.0 copy-done.20
  17.0 0.8 fusion.1
  17.8 0.6 collective-permute-start.2
  18.4 0.9 pad_maximum_fusion.kv_ref
  19.3 15.4 %all-to-all-done = bf16[16,16,3072]{2,1,0:T(8,128)(2,1)} async-done(((bf16[16,16,3072]{2,1,0:T(8,128)(2,1)}), bf16[16,16,3072]{2,1,0:T(8,128)(2,1)}, u32[]{:S(2)}, u32[]{:S(2)}) %all-to-all-start) | async-done | bytes 1572896 | tf_op jit(solution)/shard_map/all_to_all | solution.py:345
  34.7 1.1 copy-done.6
  35.9 0.0 copy-start.12
  35.9 0.0 copy-start.13
  35.9 2.5 %project.1 = bf16[256,384]{1,0:T(8,128)(2,1)S(1)} custom-call(bf16[256,3072]{1,0:T(8,128)(2,1)} %bitcast.x_ref, bf16[3072,256]{1,0:T(8,128)(2,1)S(1)} %bitcast.49, bf16[128,3072]{1,0:T(8,128)(2,1)S(1)} %copy-done.6), custom_call_target="tpu_custom_call" | custom-call | tf_op jit(solution)/shard_map/project/pallas_call | solution.py:406
  38.4 11.0 %all_to_all.60.got_ref = bf16[16,16,384]{2,1,0:T(8,128)(2,1)S(1)} all-to-all(bf16[16,16,384]{2,1,0:T(8,128)(2,1)S(1)} %bitcast.59), channel_id=1, replica_groups=mesh['section'=16,'ep'=16] {'ep'}, dimensions={0} | all-to-all | bytes 393216 | tf_op jit(solution)/shard_map/all_to_all | solution.py:345
  49.5 0.0 copy-done.4
  49.5 0.0 copy-done.5
  49.5 0.0 copy-done.10
  49.5 0.0 copy-done.11
  49.5 0.0 copy-done.12
  49.5 0.0 copy-done.13
  49.5 0.0 copy-start.2
  49.5 2.3 %attend.2 = bf16[16,16,512]{2,1,0:T(8,128)(2,1)S(1)} custom-call(bf16[16,16,384]{2,1,0:T(8,128)(2,1)S(1)} %all_to_all.60.got_ref, s32[17,256]{1,0:T(8,128)S(1)} %copy-done.13, f32[32,256]{1,0:T(8,128)S(1)} %copy-done.12, f32[2,8,4,16]{3,2,1,0:T(4,128)S(1)} %bitcast.63, f32[2,8,4,16]{3,2,1,0:T(4,128)S(1)} %bitcast.65, ...), custom_call_target="tpu_custom_call" | custom-call | tf_op jit(solution)/shard_map/attend/pallas_call | solution.py:412
  51.8 0.0 collective-permute-done.2.refs_2_
  51.8 0.0 collective-permute-done.refs_0_
  51.8 0.0 collective-permute-done.1.refs_1_
  51.8 11.7 %all_to_all.61 = bf16[16,16,512]{2,1,0:T(8,128)(2,1)S(1)} all-to-all(bf16[16,16,512]{2,1,0:T(8,128)(2,1)S(1)} %attend.2), channel_id=1, replica_groups=mesh['section'=16,'ep'=16] {'ep'}, dimensions={0} | all-to-all | bytes 524288 | tf_op jit(solution)/shard_map/all_to_all | solution.py:345
  63.5 0.0 copy-start.1
  63.5 1.9 outproj.2
  65.4 0.0 copy-start
  65.4 15.3 %all_to_all.62.got_ref = bf16[16,16,1536]{2,1,0:T(8,128)(2,1)S(1)} all-to-all(bf16[16,16,1536]{2,1,0:T(8,128)(2,1)S(1)} %bitcast.60), channel_id=1, replica_groups=mesh['section'=16,'ep'=16] {'ep'}, dimensions={0} | all-to-all | bytes 1572864 | tf_op jit(solution)/shard_map/all_to_all | solution.py:345
  80.8 0.0 copy-done.8
  80.8 0.0 copy-done.9
  80.8 0.0 copy-done.17
  80.8 0.4 residual.2
  81.2 14.4 %all_to_all.63 = bf16[16,8,3072]{2,1,0:T(8,128)(2,1)S(1)} all-to-all(bf16[16,8,3072]{2,1,0:T(8,128)(2,1)S(1)} %get-tuple-element.36), channel_id=1, replica_groups=mesh['section'=16,'ep'=16] {'ep'}, dimensions={0} | all-to-all | bytes 1572864 | tf_op jit(solution)/shard_map/all_to_all | solution.py:345
  95.7 0.0 copy-done.1
  95.7 2.3 %expert.2 = bf16[128,3072]{1,0:T(8,128)(2,1)S(1)} custom-call(bf16[128,3072]{1,0:T(8,128)(2,1)S(1)} %bitcast.51, bf16[448,3072]{1,0:T(8,128)(2,1)S(1)} %bitcast.45, bf16[448,3072]{1,0:T(8,128)(2,1)S(1)} %bitcast.47, bf16[1,448,3072]{2,1,0:T(8,128)(2,1)S(1)} %copy-done.2), custom_call_target="tpu_custom_call" | custom-call | tf_op jit(solution)/shard_map/expert/pallas_call | solution.py:439
  97.9 0.0 copy-start.14
  97.9 0.0 copy-start.16
  98.0 14.6 %all_to_all.64.got_ref = bf16[16,8,3072]{2,1,0:T(8,128)(2,1)S(1)} all-to-all(bf16[16,8,3072]{2,1,0:T(8,128)(2,1)S(1)} %bitcast.52), channel_id=1, replica_groups=mesh['section'=16,'ep'=16] {'ep'}, dimensions={0} | all-to-all | bytes 1572864 | tf_op jit(solution)/shard_map/all_to_all | solution.py:345
  112.5 0.4 combine.2
  112.9 1.9 collective-permute-start.3
  114.9 4.0 %collective-permute-done.3.shifted_ref = bf16[16,3072]{1,0:T(8,128)(2,1)S(1)} collective-permute-done((bf16[16,3072]{1,0:T(8,128)(2,1)S(1)}, bf16[16,3072]{1,0:T(8,128)(2,1)S(1)}, u32[]{:S(2)}, u32[]{:S(2)}) %collective-permute-start.3) | collective-permute-done | bytes 98336 | tf_op jit(solution)/shard_map/ppermute | solution.py:447
  118.9 0.0 copy-done.14
  118.9 0.2 select_norm.1
  119.0 18.3 %all_to_all.65 = bf16[16,16,1536]{2,1,0:T(8,128)(2,1)S(1)} all-to-all(bf16[16,16,1536]{2,1,0:T(8,128)(2,1)S(1)} %get-tuple-element.38), channel_id=1, replica_groups=mesh['section'=16,'ep'=16] {'ep'}, dimensions={0} | all-to-all | bytes 1572864 | tf_op jit(solution)/shard_map/all_to_all | solution.py:345
  137.4 1.0 project2.1
  138.4 12.8 %all_to_all.66.got_ref = bf16[16,16,768]{2,1,0:T(8,128)(2,1)S(1)} all-to-all(bf16[16,16,768]{2,1,0:T(8,128)(2,1)S(1)} %bitcast.56), channel_id=1, replica_groups=mesh['section'=16,'ep'=16] {'ep'}, dimensions={0} | all-to-all | bytes 786432 | tf_op jit(solution)/shard_map/all_to_all | solution.py:345
  151.2 2.3 %attend.3 = bf16[16,16,512]{2,1,0:T(8,128)(2,1)S(1)} custom-call(bf16[16,16,768]{2,1,0:T(8,128)(2,1)S(1)} %all_to_all.66.got_ref, s32[17,256]{1,0:T(8,128)S(1)} %copy-done.13, f32[32,256]{1,0:T(8,128)S(1)} %copy-done.12, f32[2,8,4,16]{3,2,1,0:T(4,128)S(1)} %bitcast.64, f32[2,8,4,16]{3,2,1,0:T(4,128)S(1)} %bitcast.66, ...), custom_call_target="tpu_custom_call" | custom-call | tf_op jit(solution)/shard_map/attend/pallas_call | solution.py:412
  153.4 11.6 %all_to_all.67 = bf16[16,16,512]{2,1,0:T(8,128)(2,1)S(1)} all-to-all(bf16[16,16,512]{2,1,0:T(8,128)(2,1)S(1)} %attend.3), channel_id=1, replica_groups=mesh['section'=16,'ep'=16] {'ep'}, dimensions={0} | all-to-all | bytes 524288 | tf_op jit(solution)/shard_map/all_to_all | solution.py:345
  165.0 0.6 outproj.3
  165.6 14.9 %all_to_all.68.got_ref = bf16[16,16,1536]{2,1,0:T(8,128)(2,1)S(1)} all-to-all(bf16[16,16,1536]{2,1,0:T(8,128)(2,1)S(1)} %bitcast.55), channel_id=1, replica_groups=mesh['section'=16,'ep'=16] {'ep'}, dimensions={0} | all-to-all | bytes 1572864 | tf_op jit(solution)/shard_map/all_to_all | solution.py:345
  180.5 0.4 residual.3
  181.0 14.4 %all_to_all.69 = bf16[16,8,3072]{2,1,0:T(8,128)(2,1)S(1)} all-to-all(bf16[16,8,3072]{2,1,0:T(8,128)(2,1)S(1)} %get-tuple-element.46), channel_id=1, replica_groups=mesh['section'=16,'ep'=16] {'ep'}, dimensions={0} | all-to-all | bytes 1572864 | tf_op jit(solution)/shard_map/all_to_all | solution.py:345
  195.4 2.2 %expert.3 = bf16[128,3072]{1,0:T(8,128)(2,1)S(1)} custom-call(bf16[128,3072]{1,0:T(8,128)(2,1)S(1)} %bitcast.53, bf16[448,3072]{1,0:T(8,128)(2,1)S(1)} %bitcast.46, bf16[448,3072]{1,0:T(8,128)(2,1)S(1)} %bitcast.48, bf16[1,448,3072]{2,1,0:T(8,128)(2,1)S(1)} %copy-done.2), custom_call_target="tpu_custom_call" | custom-call | tf_op jit(solution)/shard_map/expert/pallas_call | solution.py:439
  197.6 14.4 %all_to_all.70.got_ref = bf16[16,8,3072]{2,1,0:T(8,128)(2,1)S(1)} all-to-all(bf16[16,8,3072]{2,1,0:T(8,128)(2,1)S(1)} %bitcast.54), channel_id=1, replica_groups=mesh['section'=16,'ep'=16] {'ep'}, dimensions={0} | all-to-all | bytes 1572864 | tf_op jit(solution)/shard_map/all_to_all | solution.py:345
  212.1 1.1 combine.3
  (17 shorter events, 0.0 us)
Async XLA Ops:
  0.0 0.9 copy-start.7
  0.9 0.7 copy-start.15
  3.0 31.7 %all-to-all-start = ((bf16[16,16,3072]{2,1,0:T(8,128)(2,1)}), bf16[16,16,3072]{2,1,0:T(8,128)(2,1)}, u32[]{:S(2)}, u32[]{:S(2)}) async-start(bf16[16,16,3072]{2,1,0:T(8,128)(2,1)} %norm.1), calls=%async_computation | async-start | bytes 3145728 | tf_op jit(solution)/shard_map/all_to_all | solution.py:345
  10.1 4.3 %copy-start.3 = (bf16[1,3072,256]{2,1,0:T(8,128)(2,1)S(1)}, bf16[1,3072,256]{2,1,0:T(8,128)(2,1)}, u32[]{:S(2)}) copy-start(bf16[1,3072,256]{2,1,0:T(8,128)(2,1)} %param.25) | copy-start | bytes 4718596
  12.6 39.2 %collective-permute-start = (bf16[256,1536]{1,0:T(8,128)(2,1)}, bf16[256,1536]{1,0:T(8,128)(2,1)}, u32[]{:S(2)}, u32[]{:S(2)}) collective-permute-start(bf16[256,1536]{1,0:T(8,128)(2,1)} %get-tuple-element.49), channel_id=1, source_target_pairs={{0,1},{1,0},{2,3},{3,2},{4,5},{5,4},{6,7},{7,6},{8,9},{9,8},{10,11... | collective-permute-start | bytes 2359304 | tf_op jit(solution)/shard_map/ppermute | solution.py:390
  14.5 2.5 %copy-start.19 = (bf16[1,3072,64]{1,2,0:T(8,128)(2,1)S(1)}, bf16[1,3072,64]{1,2,0:T(8,128)(2,1)}, u32[]{:S(2)}) copy-start(bf16[1,3072,64]{1,2,0:T(8,128)(2,1)} %param.27) | copy-start | bytes 1179652
  14.5 2.5 %copy-start.20 = (bf16[1,3072,64]{1,2,0:T(8,128)(2,1)S(1)}, bf16[1,3072,64]{1,2,0:T(8,128)(2,1)}, u32[]{:S(2)}) copy-start(bf16[1,3072,64]{1,2,0:T(8,128)(2,1)} %param.26) | copy-start | bytes 1179652
  15.5 36.3 %collective-permute-start.1 = (bf16[1536,256]{1,0:T(8,128)(2,1)}, bf16[1536,256]{1,0:T(8,128)(2,1)}, u32[]{:S(2)}, u32[]{:S(2)}) collective-permute-start(bf16[1536,256]{1,0:T(8,128)(2,1)} %get-tuple-element.47), channel_id=1, source_target_pairs={{0,4},{1,5},{2,6},{3,7},{4,0},{5,1},{6,2},{7,3},{8,12},{9,13},{10,... | collective-permute-start | bytes 2359304 | tf_op jit(solution)/shard_map/ppermute | solution.py:391
  17.8 34.0 %collective-permute-start.2 = (bf16[128,1536]{1,0:T(8,128)(2,1)}, bf16[128,1536]{1,0:T(8,128)(2,1)}, u32[]{:S(2)}, u32[]{:S(2)}) collective-permute-start(bf16[128,1536]{1,0:T(8,128)(2,1)} %get-tuple-element.51), channel_id=1, source_target_pairs={{0,4},{1,5},{2,6},{3,7},{4,0},{5,1},{6,2},{7,3},{8,12},{9,13},{10,... | collective-permute-start | bytes 1179656 | tf_op jit(solution)/shard_map/ppermute | solution.py:392
  34.7 1.1 copy-start.6
  35.8 13.6 %copy-start.4 = (bf16[1,2,16,8,16,128]{5,4,3,2,1,0:T(8,128)(2,1)S(1)}, bf16[1,2,16,8,16,128]{5,4,3,2,1,0:T(8,128)(2,1)}, u32[]{:S(2)}) copy-start(bf16[1,2,16,8,16,128]{5,4,3,2,1,0:T(8,128)(2,1)} %key_ref.3) | copy-start | bytes 3145732
  35.8 13.6 %copy-start.5 = (bf16[1,2,16,8,16,128]{5,4,3,2,1,0:T(8,128)(2,1)S(1)}, bf16[1,2,16,8,16,128]{5,4,3,2,1,0:T(8,128)(2,1)}, u32[]{:S(2)}) copy-start(bf16[1,2,16,8,16,128]{5,4,3,2,1,0:T(8,128)(2,1)} %value_ref.3) | copy-start | bytes 3145732
  35.9 13.6 %copy-start.10 = (f32[1,2,16,8,4]{2,4,3,1,0:T(4,128)S(1)}, f32[1,2,16,8,4]{2,4,3,1,0:T(4,128)}, u32[]{:S(2)}) copy-start(f32[1,2,16,8,4]{2,4,3,1,0:T(4,128)} %param.35) | copy-start | bytes 12292
  35.9 13.6 %copy-start.11 = (f32[1,2,16,8,4]{2,4,3,1,0:T(4,128)S(1)}, f32[1,2,16,8,4]{2,4,3,1,0:T(4,128)}, u32[]{:S(2)}) copy-start(f32[1,2,16,8,4]{2,4,3,1,0:T(4,128)} %param.36) | copy-start | bytes 12292
  35.9 13.6 %copy-start.12 = (f32[32,256]{1,0:T(8,128)S(1)}, f32[32,256]{1,0:T(8,128)}, u32[]{:S(2)}) copy-start(f32[32,256]{1,0:T(8,128)} %constant.39.clone.rotary_ref) | copy-start | bytes 98308
  35.9 13.6 %copy-start.13 = (s32[17,256]{1,0:T(8,128)S(1)}, s32[17,256]{1,0:T(8,128)}, u32[]{:S(2)}) copy-start(s32[17,256]{1,0:T(8,128)} %lens_ref.3) | copy-start | bytes 52228
  49.5 46.2 %copy-start.2 = (bf16[1,448,3072]{2,1,0:T(8,128)(2,1)S(1)}, bf16[1,448,3072]{2,1,0:T(8,128)(2,1)}, u32[]{:S(2)}) copy-start(bf16[1,448,3072]{2,1,0:T(8,128)(2,1)} %down_ref.3) | copy-start | bytes 8257540
  63.5 17.2 %copy-start.8 = (bf16[16,3072]{1,0:T(8,128)(2,1)S(1)}, bf16[16,3072]{1,0:T(8,128)(2,1)}, u32[]{:S(2)}) copy-start(bf16[16,3072]{1,0:T(8,128)(2,1)} %x_ref.3) | copy-start | bytes 294916
  63.5 17.2 %copy-start.9 = (bf16[1,3072,8]{1,2,0:T(8,128)(2,1)S(1)}, bf16[1,3072,8]{1,2,0:T(8,128)(2,1)}, u32[]{:S(2)}) copy-start(bf16[1,3072,8]{1,2,0:T(8,128)(2,1)} %param.29) | copy-start | bytes 147460
  63.5 17.2 %copy-start.17 = (bf16[1,3072]{1,0:T(2,128)(2,1)S(1)}, bf16[1,3072]{1,0:T(2,128)(2,1)}, u32[]{:S(2)}) copy-start(bf16[1,3072]{1,0:T(2,128)(2,1)} %gain_ref.7) | copy-start | bytes 18436
  63.5 17.3 %copy-start.18 = (s32[1,2,16,2]{2,3,1,0:T(2,128)S(1)}, s32[1,2,16,2]{2,3,1,0:T(2,128)}, u32[]{:S(2)}) copy-start(s32[1,2,16,2]{2,3,1,0:T(2,128)} %param.22) | copy-start | bytes 772
  63.5 32.1 %copy-start.1 = (bf16[1,3072,448]{1,2,0:T(8,128)(2,1)S(1)}, bf16[1,3072,448]{1,2,0:T(8,128)(2,1)}, u32[]{:S(2)}) copy-start(bf16[1,3072,448]{1,2,0:T(8,128)(2,1)} %param.31) | copy-start | bytes 8257540
  65.4 30.2 %copy-start = (bf16[1,3072,448]{1,2,0:T(8,128)(2,1)S(1)}, bf16[1,3072,448]{1,2,0:T(8,128)(2,1)}, u32[]{:S(2)}) copy-start(bf16[1,3072,448]{1,2,0:T(8,128)(2,1)} %param.30) | copy-start | bytes 8257540
  97.9 20.9 %copy-start.14 = (bf16[16,3072]{1,0:T(8,128)(2,1)S(1)}, bf16[16,3072]{1,0:T(8,128)(2,1)}, u32[]{:S(2)}) copy-start(bf16[16,3072]{1,0:T(8,128)(2,1)} %entering_ref.1) | copy-start | bytes 294916
  97.9 20.9 %copy-start.16 = (bf16[1,3072]{1,0:T(2,128)(2,1)S(1)}, bf16[1,3072]{1,0:T(2,128)(2,1)}, u32[]{:S(2)}) copy-start(bf16[1,3072]{1,0:T(2,128)(2,1)} %gain_ref.6) | copy-start | bytes 18436
  112.9 5.9 %collective-permute-start.3 = (bf16[16,3072]{1,0:T(8,128)(2,1)S(1)}, bf16[16,3072]{1,0:T(8,128)(2,1)S(1)}, u32[]{:S(2)}, u32[]{:S(2)}) collective-permute-start(bf16[16,3072]{1,0:T(8,128)(2,1)S(1)} %combine.2), channel_id=1, source_target_pairs={{0,16},{16,32},{32,48},{48,64},{64,80},{80,96},{96,112},{112,128},... | collective-permute-start | bytes 294920 | tf_op jit(solution)/shard_map/ppermute | solution.py:447

commit v5 on v4

--- a/solution.py
+++ b/solution.py
@@ -145,18 +145,14 @@
     spread_halves(x_ref, gain_ref, copies_ref)
 
 
-def project_body(x_ref, wq_ref, kv_ref, out_ref):
+def project_body(x_ref, joined_ref, out_ref):
+    out_ref[...] = jnp.dot(x_ref[...], joined_ref[...], preferred_element_type=f32).astype(bf16)
+
+
+def project_halves_body(x_ref, own_ref, other_ref, out_ref):
     x = x_ref[...]
-    out_ref[:, 0:256] = jnp.dot(x, wq_ref[...], preferred_element_type=f32).astype(bf16)
-    out_ref[:, 256:QKV] = dot_last(x, kv_ref[...]).astype(bf16)
-
-
-def project_halves_body(x_ref, own_q_ref, own_kv_ref, q_ref, kv_ref, out_ref):
-    x = x_ref[...]
-    out_ref[:, 0:256] = jnp.dot(x, own_q_ref[...], preferred_element_type=f32).astype(bf16)
-    out_ref[:, 256:QKV] = dot_last(x, own_kv_ref[...]).astype(bf16)
-    out_ref[:, QKV : QKV + 256] = jnp.dot(x, q_ref[...], preferred_element_type=f32).astype(bf16)
-    out_ref[:, QKV + 256 : 2 * QKV] = dot_last(x, kv_ref[...]).astype(bf16)
+    out_ref[:, 0:QKV] = jnp.dot(x, own_ref[...], preferred_element_type=f32).astype(bf16)
+    out_ref[:, QKV : 2 * QKV] = jnp.dot(x, other_ref[...], preferred_element_type=f32).astype(bf16)
 
 
 def rotary_table():
@@ -203,22 +199,32 @@
         return (rows * cos_vals + pltpu.roll(rows, HD // 2, 1) * sin_vals).astype(bf16)
 
     blocks = LEN // BLK
-    which = lax.broadcasted_iota(jnp.int32, (KVH * blocks, KVH * pos), 0)
-    at = lax.broadcasted_iota(jnp.int32, (KVH * blocks, KVH * pos), 1)
-    spread = jnp.where(
-        (which // blocks == at // pos) & (which % blocks == (at % LEN) // BLK), 1.0, 0.0
-    ).astype(f32)
-    k_all = dot_first(jnp.concatenate([ks_ref[tick, g] for g in range(KVH)], axis=0), spread)
-    v_all = dot_first(jnp.concatenate([vs_ref[tick, g] for g in range(KVH)], axis=0), spread)
+    eye = lax.broadcasted_iota(jnp.int32, (KVH * blocks, KVH * blocks), 0)
+    eye = (eye == lax.broadcasted_iota(jnp.int32, (KVH * blocks, KVH * blocks), 1)).astype(f32)
+    k_rows = dot_first(jnp.concatenate([ks_ref[tick, g] for g in range(KVH)], axis=0), eye)
+    v_rows = dot_first(jnp.concatenate([vs_ref[tick, g] for g in range(KVH)], axis=0), eye)
+    block_at = lane % LEN // BLK
+
+    def spread(rows, g):
+        wide = jnp.broadcast_to(rows[:, g * blocks : g * blocks + 1], (TOK, HD))
+        for k in range(1, blocks):
+            at = g * blocks + k
+            wide = jnp.where(block_at == k, rows[:, at : at + 1], wide)
+        one = jnp.concatenate([wide] * (pos // HD), axis=1)
+        return jnp.concatenate([one] * group, axis=0)
+
     row = lax.broadcasted_iota(jnp.int32, (TOK, pos), 0)
     col = lax.broadcasted_iota(jnp.int32, (TOK, pos), 1)
     live_one = (col // LEN == row) & (col % LEN < lens)
     live = jnp.concatenate([live_one.astype(f32)] * group, axis=0) > 0.5
-    for g in range(KVH):
+    heads = range(KVH)
+    queries, fresh_keys, fresh_values, scores = [], [], [], []
+    for g in heads:
         first = rows_of(2 * g, 256, QKV)
         second = rows_of(2 * g + 1, 256, QKV)
         key_new = turned(jnp.where(low, first, pltpu.roll(second, HD // 2, 1))).astype(f32)
-        value_new = jnp.where(low, pltpu.roll(first, HD // 2, 1), second)
+        fresh_keys.append(key_new)
+        fresh_values.append(jnp.where(low, pltpu.roll(first, HD // 2, 1), second))
         q = jnp.concatenate(
             [
                 turned(rows_of(2 * g + r // 2, (r % 2) * HD, (r % 2 + 1) * HD))
@@ -226,25 +232,34 @@
             ],
             axis=0,
         )
-        keys = key_ref[0, tick, :, g].reshape(pos, HD)
-        values = value_ref[0, tick, :, g].reshape(pos, HD)
-        k_scale = jnp.concatenate([k_all[:, g * pos : (g + 1) * pos]] * group, axis=0)
-        v_scale = jnp.concatenate([v_all[:, g * pos : (g + 1) * pos]] * group, axis=0)
-        scores = dot_last(q, keys) * k_scale * scale
+        queries.append(q)
+        scores.append(dot_last(q, key_ref[0, tick, :, g].reshape(pos, HD)))
+    weights, owns, denoms = [], [], []
+    for g in heads:
+        score = jnp.where(live, scores[g] * spread(k_rows, g) * scale, -1e30)
         own = (
             jnp.sum(
-                q.astype(f32) * jnp.concatenate([key_new] * group, axis=0), axis=-1, keepdims=True
+                queries[g].astype(f32) * jnp.concatenate([fresh_keys[g]] * group, axis=0),
+                axis=-1,
+                keepdims=True,
             )
             * scale
         )
-        top = jnp.maximum(jnp.max(jnp.where(live, scores, -1e30), axis=-1, keepdims=True), own)
-        e = jnp.where(live, jnp.exp(jnp.where(live, scores, -1e30) - top), 0.0)
+        top = jnp.maximum(jnp.max(score, axis=-1, keepdims=True), own)
+        e = jnp.where(live, jnp.exp(score - top), 0.0)
         e_own = jnp.exp(own - top)
-        denom = jnp.sum(e, axis=-1, keepdims=True) + e_own
-        weight = jnp.where(live, e * v_scale, 0.0).astype(bf16)
-        mixed = jnp.dot(weight, values, preferred_element_type=f32)
-        mixed = mixed + e_own * jnp.concatenate([value_new] * group, axis=0)
-        done = (mixed / denom).astype(bf16)
+        owns.append(e_own)
+        denoms.append(jnp.sum(e, axis=-1, keepdims=True) + e_own)
+        weights.append((e * spread(v_rows, g)).astype(bf16))
+    mixes = [
+        jnp.dot(
+            weights[g], value_ref[0, tick, :, g].reshape(pos, HD), preferred_element_type=f32
+        )
+        for g in heads
+    ]
+    for g in heads:
+        mixed = mixes[g] + owns[g] * jnp.concatenate([fresh_values[g]] * group, axis=0)
+        done = (mixed / denoms[g]).astype(bf16)
         for r in range(group):
             rows = done[r * TOK : (r + 1) * TOK]
             at = (r % 2) * HD
@@ -260,7 +275,7 @@
 
 
 def out_fetch_body(att_ref, wo_ref, *refs):
-    swapped, part_ref, fetched, sems = refs[:3], refs[3], refs[4:7], refs[7]
+    swapped, part_ref, fetched, sems = refs[:2], refs[2], refs[3:5], refs[5]
     fetches = [
         pltpu.make_async_copy(there, here, sems.at[i])
         for i, (there, here) in enumerate(zip(swapped, fetched))
@@ -322,10 +337,12 @@
 
 def expert_body(x_ref, gate_ref, up_ref, down_ref, part_ref):
     x = x_ref[...]
-    gate = dot_last(x, gate_ref[...])
-    up = dot_last(x, up_ref[...])
+    gate = dot_last(gate_ref[...], x)
+    up = dot_last(up_ref[...], x)
     hidden = (gate * jax.nn.sigmoid(gate) * up).astype(bf16)
-    part_ref[...] = jnp.dot(hidden, down_ref[0], preferred_element_type=f32).astype(bf16)
+    part_ref[...] = lax.dot_general(
+        hidden, down_ref[0], (((0,), (0,)), ((), ())), preferred_element_type=f32
+    ).astype(bf16)
 
 
 def combine_body(res_ref, coef_ref, got_ref, out_ref):
@@ -369,8 +386,8 @@
     ks = jnp.transpose(k_scale[0], (0, 2, 3, 1))
     vs = jnp.transpose(v_scale[0], (0, 2, 3, 1))
     chosen = jnp.transpose(routes[0], (0, 2, 1))
-    wk_t, wv_t, router_t, gate_t, up_t = (
-        jnp.transpose(w[0], (1, 0)) for w in (wk, wv, router, w_gate, w_up)
+    router_t, gate_t, up_t = (
+        jnp.transpose(w[0], (1, 0)) for w in (router, w_gate, w_up)
     )
 
     turn = turn_of()
@@ -379,17 +396,14 @@
     sent_depth = ((ep_index >> 2) + turn + 1) % 2 * HALF
     sent_cols = (ep_index + turn + 1) % 2 * HALF
     both = ("section", "ep")
-    kv = jnp.concatenate([wk_t, wv_t], axis=0)
+    joined = jnp.concatenate([wq[0], wk[0], wv[0]], axis=1)
     sent_wo = lax.dynamic_slice(wo[0], (0, sent_cols), (256, HALF))
-    sent_q = lax.dynamic_slice(wq[0], (sent_depth, 0), (HALF, 256))
-    sent_kv = lax.dynamic_slice(kv, (0, sent_depth), (128, HALF))
+    sent_qkv = lax.dynamic_slice(joined, (sent_depth, 0), (HALF, QKV))
     own_wo = lax.dynamic_slice(wo[0], (0, HALF - sent_cols), (256, HALF))
-    own_q = lax.dynamic_slice(wq[0], (HALF - sent_depth, 0), (HALF, 256))
-    own_kv = lax.dynamic_slice(kv, (0, HALF - sent_depth), (128, HALF))
+    own_qkv = lax.dynamic_slice(joined, (HALF - sent_depth, 0), (HALF, QKV))
     others = (
         lax.ppermute(sent_wo, both, partner_list("x", sections)),
-        lax.ppermute(sent_q, both, partner_list("y", sections)),
-        lax.ppermute(sent_kv, both, partner_list("y", sections)),
+        lax.ppermute(sent_qkv, both, partner_list("y", sections)),
     )
 
     copies = call(
@@ -400,11 +414,11 @@
         name="norm",
         scratch=[pltpu.VMEM((TOK, D), bf16), pltpu.SemaphoreType.DMA((EP,))],
     )(states, attn_norm)
-    everyone, kv, own_wo, own_q, own_kv = lax.optimization_barrier(
-        (trade(copies).reshape(EP * TOK, D), kv, own_wo, own_q, own_kv)
-    )
-    projected = call(project_body, sds((EP * TOK, QKV), bf16), 3, name="project", limit=6)(
-        everyone, wq[0], kv
+    everyone, own_wo, own_qkv = lax.optimization_barrier(
+        (trade(copies).reshape(EP * TOK, D), own_wo, own_qkv)
+    )
+    projected = call(project_body, sds((EP * TOK, QKV), bf16), 2, name="project", limit=8)(
+        everyone, joined
     )
 
     def run_layer(x, projected, tick, others):
@@ -419,10 +433,10 @@
             part, *others = call(
                 out_fetch_body,
                 (part, *(sds(o.shape, bf16) for o in others)),
-                5,
-                far=(2, 3, 4),
+                4,
+                far=(2, 3),
                 name="outproj",
-                scratch=[pltpu.SemaphoreType.DMA((3,))],
+                scratch=[pltpu.SemaphoreType.DMA((2,))],
             )(heads, own_wo, *others)
         else:
             heads = trade(attended).reshape(EP * TOK, 512)
@@ -452,8 +466,8 @@
         name="select_norm",
     )(entering, shifted, attn_norm)
     everyone = trade(copies).reshape(EP * TOK, HALF)
-    projected = call(project_halves_body, sds((EP * TOK, 2 * QKV), bf16), 5, name="project2")(
-        everyone, own_q, own_kv, others[1], others[2]
+    projected = call(project_halves_body, sds((EP * TOK, 2 * QKV), bf16), 3, name="project2")(
+        everyone, own_qkv, others[1]
     )
     return run_layer(second_in, projected, 1, others)[0]
 

time: 214 us -> 211 us (0.986)
  transfers between devices with their start and end apart: 5 -> 4, of which waited for: 2 -> 2; matrix products, arithmetic and copies ran while one was open for 2% -> 4% of each run, Pallas kernels for 2% -> 2%
where the time goes in v5:
time: 211 us; the launch traced here: 210 us
  blocking collectives  153 us (73%)
  waiting for transfers between devices  17.3 us (8%)
  Pallas kernels  17 us (8%)
  starting transfers between devices  12.6 us (6%)
  local copies, waits for them, and re-layouts  7.3 us (3%)
  other arithmetic  2.15 us (1%)
    all_to_all x11, blocking collectives, trade(): return lax.all_to_all(pieces, 'ep', split_axis=0, concat_axis=0, tiled=True)  153 us
    all_to_all x1, waiting for transfers between devices, trade(): return lax.all_to_all(pieces, 'ep', split_axis=0, concat_axis=0, tiled=True)  13.3 us
    all_to_all x1, starting transfers between devices, trade(): return lax.all_to_all(pieces, 'ep', split_axis=0, concat_axis=0, tiled=True)  7.22 us
    pallas_call x2, Pallas kernels, run_layer(): call(expert_body, sds((EP * CAP, D), bf16), 4, name='expert', limit=8)  4.29 us
  transfers between devices with their start and end apart: 4, of which 2 were waited for; matrix products, arithmetic and copies ran while one was open for 4% of the time, Pallas kernels for 2%

profile of v5, /device:TPU:96, one launch (start us, length us, event | category | flops | bytes accessed | tf_op | source)
XLA Modules:
  0.0 210.1 jit_solution(18081585895380086487)
XLA Ops:
  0.0 0.9 copy-done.6
  0.9 0.7 copy-done.14
  1.6 1.4 norm.1
  3.0 0.0 copy-start.19
  3.0 7.2 %all-to-all-start = ((bf16[16,16,3072]{2,1,0:T(8,128)(2,1)}), bf16[16,16,3072]{2,1,0:T(8,128)(2,1)}, u32[]{:S(2)}, u32[]{:S(2)}) async-start(bf16[16,16,3072]{2,1,0:T(8,128)(2,1)} %norm.1), calls=%async_computation | async-start | bytes 3145728 | tf_op jit(solution)/shard_map/all_to_all | solution.py:362
  10.3 0.0 copy-done.18
  10.3 0.4 copy.20
  10.6 0.0 copy-done.19
  10.7 1.2 copy.21
  11.8 2.1 %pad_maximum_fusion.joined_ref = bf16[3072,384]{1,0:T(8,128)(2,1)S(1)} fusion(bf16[3072,64]{1,0:T(8,128)(2,1)} %bitcast.61, bf16[3072,64]{1,0:T(8,128)(2,1)S(1)} %bitcast.60, bf16[3072,256]{1,0:T(8,128)(2,1)} %bitcast.62), kind=kLoop, calls=%fused_computation | loop fusion | flops 7077888 | bytes 4718592 | tf_op jit(solution)/shard_map/concatenate | solution.py:399
  14.0 1.7 constant_dynamic-slice_fusion
  15.7 1.9 collective-permute-start.1
  17.5 2.4 %dynamic-slice_bitcast_fusion = (bf16[256,1536]{1,0:T(8,128)(2,1)}, bf16[256,1536]{1,0:T(8,128)(2,1)S(1)}) fusion(bf16[1,256,3072]{2,1,0:T(8,128)(2,1)} %param.28, s32[]{:T(128)S(6)} %select_n.27, s32[]{:T(128)S(6)} %select_n.24), kind=kLoop, calls=%fused_computation.1 | loop fusion | bytes 3145736 | tf_op jit(solution)/shard_map/dynamic_slice | solution.py:400
  20.0 1.5 collective-permute-start
  21.5 13.3 %all-to-all-done = bf16[16,16,3072]{2,1,0:T(8,128)(2,1)} async-done(((bf16[16,16,3072]{2,1,0:T(8,128)(2,1)}), bf16[16,16,3072]{2,1,0:T(8,128)(2,1)}, u32[]{:S(2)}, u32[]{:S(2)}) %all-to-all-start) | async-done | bytes 1572896 | tf_op jit(solution)/shard_map/all_to_all | solution.py:362
  34.9 2.5 %project.1 = bf16[256,384]{1,0:T(8,128)(2,1)S(1)} custom-call(bf16[256,3072]{1,0:T(8,128)(2,1)} %bitcast.x_ref, bf16[3072,384]{1,0:T(8,128)(2,1)S(1)} %pad_maximum_fusion.joined_ref), custom_call_target="tpu_custom_call" | custom-call | tf_op jit(solution)/shard_map/project/pallas_call | solution.py:420
  37.4 11.0 %all_to_all.60.got_ref = bf16[16,16,384]{2,1,0:T(8,128)(2,1)S(1)} all-to-all(bf16[16,16,384]{2,1,0:T(8,128)(2,1)S(1)} %bitcast.50), channel_id=1, replica_groups=mesh['section'=16,'ep'=16] {'ep'}, dimensions={0} | all-to-all | bytes 393216 | tf_op jit(solution)/shard_map/all_to_all | solution.py:362
  48.4 0.0 copy-done.9
  48.4 0.0 copy-done.10
  48.4 0.0 copy-done.11
  48.4 0.0 copy-done.12
  48.5 0.0 copy-done.4
  48.5 0.0 copy-done.5
  48.5 0.0 copy-start.2
  48.5 1.5 attend.2
  50.0 0.0 collective-permute-done.refs_0_
  50.0 0.0 collective-permute-done.1.refs_1_
  50.0 11.7 %all_to_all.61 = bf16[16,16,512]{2,1,0:T(8,128)(2,1)S(1)} all-to-all(bf16[16,16,512]{2,1,0:T(8,128)(2,1)S(1)} %attend.2), channel_id=1, replica_groups=mesh['section'=16,'ep'=16] {'ep'}, dimensions={0} | all-to-all | bytes 524288 | tf_op jit(solution)/shard_map/all_to_all | solution.py:362
  61.7 0.0 copy-start.1
  61.7 1.9 outproj.2
  63.6 0.0 copy-start
  63.6 15.3 %all_to_all.62.got_ref = bf16[16,16,1536]{2,1,0:T(8,128)(2,1)S(1)} all-to-all(bf16[16,16,1536]{2,1,0:T(8,128)(2,1)S(1)} %bitcast.51), channel_id=1, replica_groups=mesh['section'=16,'ep'=16] {'ep'}, dimensions={0} | all-to-all | bytes 1572864 | tf_op jit(solution)/shard_map/all_to_all | solution.py:362
  78.9 0.0 copy-done.7
  78.9 0.0 copy-done.8
  78.9 0.0 copy-done.16
  78.9 0.0 copy-done.17
  78.9 0.4 residual.2
  79.4 14.4 %all_to_all.63 = bf16[16,8,3072]{2,1,0:T(8,128)(2,1)S(1)} all-to-all(bf16[16,8,3072]{2,1,0:T(8,128)(2,1)S(1)} %get-tuple-element.30), channel_id=1, replica_groups=mesh['section'=16,'ep'=16] {'ep'}, dimensions={0} | all-to-all | bytes 1572864 | tf_op jit(solution)/shard_map/all_to_all | solution.py:362
  93.8 0.0 copy-done.2
  93.8 0.0 copy-done.1
  93.8 0.0 copy-done
  93.8 2.1 %expert.2 = bf16[128,3072]{1,0:T(8,128)(2,1)S(1)} custom-call(bf16[128,3072]{1,0:T(8,128)(2,1)S(1)} %bitcast.42, bf16[448,3072]{1,0:T(8,128)(2,1)S(1)} %bitcast.37, bf16[448,3072]{1,0:T(8,128)(2,1)S(1)} %bitcast.39, bf16[1,448,3072]{2,1,0:T(8,128)(2,1)S(1)} %copy-done.2), custom_call_target="tpu_custom_call" | custom-call | tf_op jit(solution)/shard_map/expert/pallas_call | solution.py:453
  95.9 0.0 copy-start.13
  95.9 0.0 copy-start.15
  96.0 0.0 copy-start.3
  96.0 14.6 %all_to_all.64.got_ref = bf16[16,8,3072]{2,1,0:T(8,128)(2,1)S(1)} all-to-all(bf16[16,8,3072]{2,1,0:T(8,128)(2,1)S(1)} %bitcast.43), channel_id=1, replica_groups=mesh['section'=16,'ep'=16] {'ep'}, dimensions={0} | all-to-all | bytes 1572864 | tf_op jit(solution)/shard_map/all_to_all | solution.py:362
  110.5 0.4 combine.2
  111.0 1.9 collective-permute-start.2
  112.9 4.0 %collective-permute-done.2.shifted_ref = bf16[16,3072]{1,0:T(8,128)(2,1)S(1)} collective-permute-done((bf16[16,3072]{1,0:T(8,128)(2,1)S(1)}, bf16[16,3072]{1,0:T(8,128)(2,1)S(1)}, u32[]{:S(2)}, u32[]{:S(2)}) %collective-permute-start.2) | collective-permute-done | bytes 98336 | tf_op jit(solution)/shard_map/ppermute | solution.py:461
  116.9 0.0 copy-done.13
  116.9 0.2 select_norm.1
  117.1 18.3 %all_to_all.65 = bf16[16,16,1536]{2,1,0:T(8,128)(2,1)S(1)} all-to-all(bf16[16,16,1536]{2,1,0:T(8,128)(2,1)S(1)} %get-tuple-element.32), channel_id=1, replica_groups=mesh['section'=16,'ep'=16] {'ep'}, dimensions={0} | all-to-all | bytes 1572864 | tf_op jit(solution)/shard_map/all_to_all | solution.py:362
  135.4 0.0 copy-done.3
  135.4 1.0 project2.1
  136.4 12.8 %all_to_all.66.got_ref = bf16[16,16,768]{2,1,0:T(8,128)(2,1)S(1)} all-to-all(bf16[16,16,768]{2,1,0:T(8,128)(2,1)S(1)} %bitcast.47), channel_id=1, replica_groups=mesh['section'=16,'ep'=16] {'ep'}, dimensions={0} | all-to-all | bytes 786432 | tf_op jit(solution)/shard_map/all_to_all | solution.py:362
  149.2 1.4 attend.3
  150.5 11.6 %all_to_all.67 = bf16[16,16,512]{2,1,0:T(8,128)(2,1)S(1)} all-to-all(bf16[16,16,512]{2,1,0:T(8,128)(2,1)S(1)} %attend.3), channel_id=1, replica_groups=mesh['section'=16,'ep'=16] {'ep'}, dimensions={0} | all-to-all | bytes 524288 | tf_op jit(solution)/shard_map/all_to_all | solution.py:362
  162.1 0.6 outproj.3
  162.7 14.9 %all_to_all.68.got_ref = bf16[16,16,1536]{2,1,0:T(8,128)(2,1)S(1)} all-to-all(bf16[16,16,1536]{2,1,0:T(8,128)(2,1)S(1)} %bitcast.46), channel_id=1, replica_groups=mesh['section'=16,'ep'=16] {'ep'}, dimensions={0} | all-to-all | bytes 1572864 | tf_op jit(solution)/shard_map/all_to_all | solution.py:362
  177.6 0.4 residual.3
  178.1 14.4 %all_to_all.69 = bf16[16,8,3072]{2,1,0:T(8,128)(2,1)S(1)} all-to-all(bf16[16,8,3072]{2,1,0:T(8,128)(2,1)S(1)} %get-tuple-element.38), channel_id=1, replica_groups=mesh['section'=16,'ep'=16] {'ep'}, dimensions={0} | all-to-all | bytes 1572864 | tf_op jit(solution)/shard_map/all_to_all | solution.py:362
  192.5 2.1 %expert.3 = bf16[128,3072]{1,0:T(8,128)(2,1)S(1)} custom-call(bf16[128,3072]{1,0:T(8,128)(2,1)S(1)} %bitcast.44, bf16[448,3072]{1,0:T(8,128)(2,1)S(1)} %bitcast.38, bf16[448,3072]{1,0:T(8,128)(2,1)S(1)} %bitcast.40, bf16[1,448,3072]{2,1,0:T(8,128)(2,1)S(1)} %copy-done.2), custom_call_target="tpu_custom_call" | custom-call | tf_op jit(solution)/shard_map/expert/pallas_call | solution.py:453
  194.6 14.4 %all_to_all.70.got_ref = bf16[16,8,3072]{2,1,0:T(8,128)(2,1)S(1)} all-to-all(bf16[16,8,3072]{2,1,0:T(8,128)(2,1)S(1)} %bitcast.45), channel_id=1, replica_groups=mesh['section'=16,'ep'=16] {'ep'}, dimensions={0} | all-to-all | bytes 1572864 | tf_op jit(solution)/shard_map/all_to_all | solution.py:362
  209.1 1.1 combine.3
  (14 shorter events, 0.0 us)
Async XLA Ops:
  0.0 0.9 copy-start.6
  0.9 0.7 copy-start.14
  1.6 8.7 %copy-start.18 = (bf16[1,3072,64]{1,2,0:T(8,128)(2,1)S(1)}, bf16[1,3072,64]{1,2,0:T(8,128)(2,1)}, u32[]{:S(2)}) copy-start(bf16[1,3072,64]{1,2,0:T(8,128)(2,1)} %param.26) | copy-start | bytes 1179652
  3.0 7.6 %copy-start.19 = (bf16[1,3072,64]{1,2,0:T(8,128)(2,1)S(1)}, bf16[1,3072,64]{1,2,0:T(8,128)(2,1)}, u32[]{:S(2)}) copy-start(bf16[1,3072,64]{1,2,0:T(8,128)(2,1)} %param.27) | copy-start | bytes 1179652
  3.0 31.8 %all-to-all-start = ((bf16[16,16,3072]{2,1,0:T(8,128)(2,1)}), bf16[16,16,3072]{2,1,0:T(8,128)(2,1)}, u32[]{:S(2)}, u32[]{:S(2)}) async-start(bf16[16,16,3072]{2,1,0:T(8,128)(2,1)} %norm.1), calls=%async_computation | async-start | bytes 3145728 | tf_op jit(solution)/shard_map/all_to_all | solution.py:362
  15.7 34.3 %collective-permute-start.1 = (bf16[1536,384]{1,0:T(8,128)(2,1)}, bf16[1536,384]{1,0:T(8,128)(2,1)}, u32[]{:S(2)}, u32[]{:S(2)}) collective-permute-start(bf16[1536,384]{1,0:T(8,128)(2,1)} %get-tuple-element.39), channel_id=1, source_target_pairs={{0,4},{1,5},{2,6},{3,7},{4,0},{5,1},{6,2},{7,3},{8,12},{9,13},{10,... | collective-permute-start | bytes 3538952 | tf_op jit(solution)/shard_map/ppermute | solution.py:406
  20.0 28.5 %copy-start.9 = (f32[1,2,16,8,4]{2,4,3,1,0:T(4,128)S(1)}, f32[1,2,16,8,4]{2,4,3,1,0:T(4,128)}, u32[]{:S(2)}) copy-start(f32[1,2,16,8,4]{2,4,3,1,0:T(4,128)} %param.35) | copy-start | bytes 12292
  20.0 28.5 %copy-start.10 = (f32[1,2,16,8,4]{2,4,3,1,0:T(4,128)S(1)}, f32[1,2,16,8,4]{2,4,3,1,0:T(4,128)}, u32[]{:S(2)}) copy-start(f32[1,2,16,8,4]{2,4,3,1,0:T(4,128)} %param.36) | copy-start | bytes 12292
  20.0 28.5 %copy-start.11 = (f32[32,256]{1,0:T(8,128)S(1)}, f32[32,256]{1,0:T(8,128)}, u32[]{:S(2)}) copy-start(f32[32,256]{1,0:T(8,128)} %constant.37.clone.rotary_ref) | copy-start | bytes 98308
  20.0 28.5 %copy-start.12 = (s32[17,256]{1,0:T(8,128)S(1)}, s32[17,256]{1,0:T(8,128)}, u32[]{:S(2)}) copy-start(s32[17,256]{1,0:T(8,128)} %lens_ref.3) | copy-start | bytes 52228
  20.0 30.0 %collective-permute-start = (bf16[256,1536]{1,0:T(8,128)(2,1)}, bf16[256,1536]{1,0:T(8,128)(2,1)}, u32[]{:S(2)}, u32[]{:S(2)}) collective-permute-start(bf16[256,1536]{1,0:T(8,128)(2,1)} %get-tuple-element.41), channel_id=1, source_target_pairs={{0,1},{1,0},{2,3},{3,2},{4,5},{5,4},{6,7},{7,6},{8,9},{9,8},{10,11... | collective-permute-start | bytes 2359304 | tf_op jit(solution)/shard_map/ppermute | solution.py:405
  34.9 13.6 %copy-start.4 = (bf16[1,2,16,8,16,128]{5,4,3,2,1,0:T(8,128)(2,1)S(1)}, bf16[1,2,16,8,16,128]{5,4,3,2,1,0:T(8,128)(2,1)}, u32[]{:S(2)}) copy-start(bf16[1,2,16,8,16,128]{5,4,3,2,1,0:T(8,128)(2,1)} %key_ref.3) | copy-start | bytes 3145732
  34.9 13.6 %copy-start.5 = (bf16[1,2,16,8,16,128]{5,4,3,2,1,0:T(8,128)(2,1)S(1)}, bf16[1,2,16,8,16,128]{5,4,3,2,1,0:T(8,128)(2,1)}, u32[]{:S(2)}) copy-start(bf16[1,2,16,8,16,128]{5,4,3,2,1,0:T(8,128)(2,1)} %value_ref.3) | copy-start | bytes 3145732
  48.5 45.3 %copy-start.2 = (bf16[1,448,3072]{2,1,0:T(8,128)(2,1)S(1)}, bf16[1,448,3072]{2,1,0:T(8,128)(2,1)}, u32[]{:S(2)}) copy-start(bf16[1,448,3072]{2,1,0:T(8,128)(2,1)} %down_ref.3) | copy-start | bytes 8257540
  61.6 17.2 %copy-start.7 = (bf16[16,3072]{1,0:T(8,128)(2,1)S(1)}, bf16[16,3072]{1,0:T(8,128)(2,1)}, u32[]{:S(2)}) copy-start(bf16[16,3072]{1,0:T(8,128)(2,1)} %x_ref.3) | copy-start | bytes 294916
  61.6 17.2 %copy-start.8 = (bf16[1,3072,8]{1,2,0:T(8,128)(2,1)S(1)}, bf16[1,3072,8]{1,2,0:T(8,128)(2,1)}, u32[]{:S(2)}) copy-start(bf16[1,3072,8]{1,2,0:T(8,128)(2,1)} %param.29) | copy-start | bytes 147460
  61.6 17.2 %copy-start.16 = (bf16[1,3072]{1,0:T(2,128)(2,1)S(1)}, bf16[1,3072]{1,0:T(2,128)(2,1)}, u32[]{:S(2)}) copy-start(bf16[1,3072]{1,0:T(2,128)(2,1)} %gain_ref.7) | copy-start | bytes 18436
  61.7 17.2 %copy-start.17 = (s32[1,2,16,2]{2,3,1,0:T(2,128)S(1)}, s32[1,2,16,2]{2,3,1,0:T(2,128)}, u32[]{:S(2)}) copy-start(s32[1,2,16,2]{2,3,1,0:T(2,128)} %param.22) | copy-start | bytes 772
  61.7 32.1 %copy-start.1 = (bf16[1,3072,448]{1,2,0:T(8,128)(2,1)S(1)}, bf16[1,3072,448]{1,2,0:T(8,128)(2,1)}, u32[]{:S(2)}) copy-start(bf16[1,3072,448]{1,2,0:T(8,128)(2,1)} %param.31) | copy-start | bytes 8257540
  63.6 30.2 %copy-start = (bf16[1,3072,448]{1,2,0:T(8,128)(2,1)S(1)}, bf16[1,3072,448]{1,2,0:T(8,128)(2,1)}, u32[]{:S(2)}) copy-start(bf16[1,3072,448]{1,2,0:T(8,128)(2,1)} %param.30) | copy-start | bytes 8257540
  95.9 21.0 %copy-start.13 = (bf16[16,3072]{1,0:T(8,128)(2,1)S(1)}, bf16[16,3072]{1,0:T(8,128)(2,1)}, u32[]{:S(2)}) copy-start(bf16[16,3072]{1,0:T(8,128)(2,1)} %entering_ref.1) | copy-start | bytes 294916
  95.9 21.0 %copy-start.15 = (bf16[1,3072]{1,0:T(2,128)(2,1)S(1)}, bf16[1,3072]{1,0:T(2,128)(2,1)}, u32[]{:S(2)}) copy-start(bf16[1,3072]{1,0:T(2,128)(2,1)} %gain_ref.6) | copy-start | bytes 18436
  96.0 39.4 %copy-start.3 = (bf16[1536,384]{1,0:T(8,128)(2,1)S(1)}, bf16[1536,384]{1,0:T(8,128)(2,1)}, u32[]{:S(2)}) copy-start(bf16[1536,384]{1,0:T(8,128)(2,1)} %get-tuple-element.33.own_ref) | copy-start | bytes 3538948
  111.0 5.9 %collective-permute-start.2 = (bf16[16,3072]{1,0:T(8,128)(2,1)S(1)}, bf16[16,3072]{1,0:T(8,128)(2,1)S(1)}, u32[]{:S(2)}, u32[]{:S(2)}) collective-permute-start(bf16[16,3072]{1,0:T(8,128)(2,1)S(1)} %combine.2), channel_id=1, source_target_pairs={{0,16},{16,32},{32,48},{48,64},{64,80},{80,96},{96,112},{112,128},... | collective-permute-start | bytes 294920 | tf_op jit(solution)/shard_map/ppermute | solution.py:461

commit v6 on v5

--- a/solution.py
+++ b/solution.py
@@ -113,7 +113,9 @@
                 copies_ref[(2 * k + (turn ^ part)) * 4 + x, :, kept] = rows
 
 
-def norm_body(x_ref, gain_ref, copies_hbm, rows_ref, sems):
+def norm_body(both_ref, copies_hbm, rows_ref, sems):
+    x_ref = both_ref.at[0:TOK]
+    gain_ref = both_ref.at[TOK : TOK + 1]
     total = jnp.zeros((TOK, 1), f32)
     for cols in columns():
         wide = x_ref[:, cols].astype(f32)
@@ -409,11 +411,11 @@
     copies = call(
         norm_body,
         sds((EP, TOK, D), bf16),
-        2,
+        1,
         far_out=True,
         name="norm",
         scratch=[pltpu.VMEM((TOK, D), bf16), pltpu.SemaphoreType.DMA((EP,))],
-    )(states, attn_norm)
+    )(jnp.concatenate([states, attn_norm], axis=0))
     everyone, own_wo, own_qkv = lax.optimization_barrier(
         (trade(copies).reshape(EP * TOK, D), own_wo, own_qkv)
     )

time: 211 us -> 210 us (level)
  no operation moved by 1% of the time
where the time goes in v6:
time: 210 us; the launch traced here: 209 us
  blocking collectives  153 us (73%)
  waiting for transfers between devices  17.3 us (8%)
  Pallas kernels  17 us (8%)
  starting transfers between devices  12.6 us (6%)
  local copies, waits for them, and re-layouts  5.73 us (3%)
  other arithmetic  3.07 us (1%)
    all_to_all x11, blocking collectives, trade(): return lax.all_to_all(pieces, 'ep', split_axis=0, concat_axis=0, tiled=True)  153 us
    all_to_all x1, waiting for transfers between devices, trade(): return lax.all_to_all(pieces, 'ep', split_axis=0, concat_axis=0, tiled=True)  13.3 us
    all_to_all x1, starting transfers between devices, trade(): return lax.all_to_all(pieces, 'ep', split_axis=0, concat_axis=0, tiled=True)  7.22 us
    pallas_call x2, Pallas kernels, run_layer(): call(expert_body, sds((EP * CAP, D), bf16), 4, name='expert', limit=8)  4.29 us
  transfers between devices with their start and end apart: 4, of which 2 were waited for; matrix products, arithmetic and copies ran while one was open for 4% of the time, Pallas kernels for 2%

profile of v6, /device:TPU:96, one launch (start us, length us, event | category | flops | bytes accessed | tf_op | source)
XLA Modules:
  0.0 209.5 jit_solution(13730446969890174144)
XLA Ops:
  0.0 0.9 pad_maximum_fusion.1.both_ref
  0.9 0.0 copy-start.16
  0.9 1.4 norm.1
  2.4 0.0 copy-start.17
  2.4 7.2 %all-to-all-start = ((bf16[16,16,3072]{2,1,0:T(8,128)(2,1)}), bf16[16,16,3072]{2,1,0:T(8,128)(2,1)}, u32[]{:S(2)}, u32[]{:S(2)}) async-start(bf16[16,16,3072]{2,1,0:T(8,128)(2,1)} %norm.1), calls=%async_computation | async-start | bytes 3145728 | tf_op jit(solution)/shard_map/all_to_all | solution.py:364
  9.6 0.0 copy-done.16
  9.6 0.4 copy.20
  10.0 0.0 copy-done.17
  10.0 1.2 copy.21
  11.2 2.1 %pad_maximum_fusion.joined_ref = bf16[3072,384]{1,0:T(8,128)(2,1)S(1)} fusion(bf16[3072,64]{1,0:T(8,128)(2,1)} %bitcast.61, bf16[3072,64]{1,0:T(8,128)(2,1)S(1)} %bitcast.60, bf16[3072,256]{1,0:T(8,128)(2,1)} %bitcast.62), kind=kLoop, calls=%fused_computation | loop fusion | flops 7077888 | bytes 4718592 | tf_op jit(solution)/shard_map/concatenate | solution.py:401
  13.3 1.7 constant_dynamic-slice_fusion
  15.0 1.9 collective-permute-start.1
  16.9 2.4 %dynamic-slice_bitcast_fusion = (bf16[256,1536]{1,0:T(8,128)(2,1)}, bf16[256,1536]{1,0:T(8,128)(2,1)S(1)}) fusion(bf16[1,256,3072]{2,1,0:T(8,128)(2,1)} %param.28, s32[]{:T(128)S(6)} %select_n.27, s32[]{:T(128)S(6)} %select_n.24), kind=kLoop, calls=%fused_computation.1 | loop fusion | bytes 3145736 | tf_op jit(solution)/shard_map/dynamic_slice | solution.py:402
  19.3 1.5 collective-permute-start
  20.9 13.3 %all-to-all-done = bf16[16,16,3072]{2,1,0:T(8,128)(2,1)} async-done(((bf16[16,16,3072]{2,1,0:T(8,128)(2,1)}), bf16[16,16,3072]{2,1,0:T(8,128)(2,1)}, u32[]{:S(2)}, u32[]{:S(2)}) %all-to-all-start) | async-done | bytes 1572896 | tf_op jit(solution)/shard_map/all_to_all | solution.py:364
  34.2 2.5 %project.1 = bf16[256,384]{1,0:T(8,128)(2,1)S(1)} custom-call(bf16[256,3072]{1,0:T(8,128)(2,1)} %bitcast.x_ref, bf16[3072,384]{1,0:T(8,128)(2,1)S(1)} %pad_maximum_fusion.joined_ref), custom_call_target="tpu_custom_call" | custom-call | tf_op jit(solution)/shard_map/project/pallas_call | solution.py:422
  36.7 11.0 %all_to_all.60.got_ref = bf16[16,16,384]{2,1,0:T(8,128)(2,1)S(1)} all-to-all(bf16[16,16,384]{2,1,0:T(8,128)(2,1)S(1)} %bitcast.50), channel_id=1, replica_groups=mesh['section'=16,'ep'=16] {'ep'}, dimensions={0} | all-to-all | bytes 393216 | tf_op jit(solution)/shard_map/all_to_all | solution.py:364
  47.8 0.0 copy-done.8
  47.8 0.0 copy-done.9
  47.8 0.0 copy-done.10
  47.8 0.0 copy-done.11
  47.8 0.0 copy-done.4
  47.8 0.0 copy-done.5
  47.8 0.0 copy-start.2
  47.8 1.5 attend.2
  49.3 0.0 collective-permute-done.refs_0_
  49.3 0.0 collective-permute-done.1.refs_1_
  49.3 11.7 %all_to_all.61 = bf16[16,16,512]{2,1,0:T(8,128)(2,1)S(1)} all-to-all(bf16[16,16,512]{2,1,0:T(8,128)(2,1)S(1)} %attend.2), channel_id=1, replica_groups=mesh['section'=16,'ep'=16] {'ep'}, dimensions={0} | all-to-all | bytes 524288 | tf_op jit(solution)/shard_map/all_to_all | solution.py:364
  61.0 0.0 copy-start.1
  61.0 1.9 outproj.2
  62.9 0.0 copy-start
  62.9 15.3 %all_to_all.62.got_ref = bf16[16,16,1536]{2,1,0:T(8,128)(2,1)S(1)} all-to-all(bf16[16,16,1536]{2,1,0:T(8,128)(2,1)S(1)} %bitcast.51), channel_id=1, replica_groups=mesh['section'=16,'ep'=16] {'ep'}, dimensions={0} | all-to-all | bytes 1572864 | tf_op jit(solution)/shard_map/all_to_all | solution.py:364
  78.2 0.0 copy-done.6
  78.2 0.0 copy-done.7
  78.2 0.0 copy-done.14
  78.2 0.0 copy-done.15
  78.2 0.4 residual.2
  78.7 14.4 %all_to_all.63 = bf16[16,8,3072]{2,1,0:T(8,128)(2,1)S(1)} all-to-all(bf16[16,8,3072]{2,1,0:T(8,128)(2,1)S(1)} %get-tuple-element.30), channel_id=1, replica_groups=mesh['section'=16,'ep'=16] {'ep'}, dimensions={0} | all-to-all | bytes 1572864 | tf_op jit(solution)/shard_map/all_to_all | solution.py:364
  93.1 0.0 copy-done.2
  93.1 0.0 copy-done.1
  93.1 0.0 copy-done
  93.1 2.1 %expert.2 = bf16[128,3072]{1,0:T(8,128)(2,1)S(1)} custom-call(bf16[128,3072]{1,0:T(8,128)(2,1)S(1)} %bitcast.42, bf16[448,3072]{1,0:T(8,128)(2,1)S(1)} %bitcast.37, bf16[448,3072]{1,0:T(8,128)(2,1)S(1)} %bitcast.39, bf16[1,448,3072]{2,1,0:T(8,128)(2,1)S(1)} %copy-done.2), custom_call_target="tpu_custom_call" | custom-call | tf_op jit(solution)/shard_map/expert/pallas_call | solution.py:455
  95.3 0.0 copy-start.12
  95.3 0.0 copy-start.13
  95.3 0.0 copy-start.3
  95.3 14.6 %all_to_all.64.got_ref = bf16[16,8,3072]{2,1,0:T(8,128)(2,1)S(1)} all-to-all(bf16[16,8,3072]{2,1,0:T(8,128)(2,1)S(1)} %bitcast.43), channel_id=1, replica_groups=mesh['section'=16,'ep'=16] {'ep'}, dimensions={0} | all-to-all | bytes 1572864 | tf_op jit(solution)/shard_map/all_to_all | solution.py:364
  109.9 0.4 combine.2
  110.3 1.9 collective-permute-start.2
  112.2 4.0 %collective-permute-done.2.shifted_ref = bf16[16,3072]{1,0:T(8,128)(2,1)S(1)} collective-permute-done((bf16[16,3072]{1,0:T(8,128)(2,1)S(1)}, bf16[16,3072]{1,0:T(8,128)(2,1)S(1)}, u32[]{:S(2)}, u32[]{:S(2)}) %collective-permute-start.2) | collective-permute-done | bytes 98336 | tf_op jit(solution)/shard_map/ppermute | solution.py:463
  116.2 0.0 copy-done.12
  116.3 0.0 copy-done.13
  116.3 0.2 select_norm.1
  116.4 18.3 %all_to_all.65 = bf16[16,16,1536]{2,1,0:T(8,128)(2,1)S(1)} all-to-all(bf16[16,16,1536]{2,1,0:T(8,128)(2,1)S(1)} %get-tuple-element.32), channel_id=1, replica_groups=mesh['section'=16,'ep'=16] {'ep'}, dimensions={0} | all-to-all | bytes 1572864 | tf_op jit(solution)/shard_map/all_to_all | solution.py:364
  134.8 1.0 project2.1
  135.7 12.8 %all_to_all.66.got_ref = bf16[16,16,768]{2,1,0:T(8,128)(2,1)S(1)} all-to-all(bf16[16,16,768]{2,1,0:T(8,128)(2,1)S(1)} %bitcast.47), channel_id=1, replica_groups=mesh['section'=16,'ep'=16] {'ep'}, dimensions={0} | all-to-all | bytes 786432 | tf_op jit(solution)/shard_map/all_to_all | solution.py:364
  148.5 1.4 attend.3
  149.9 11.6 %all_to_all.67 = bf16[16,16,512]{2,1,0:T(8,128)(2,1)S(1)} all-to-all(bf16[16,16,512]{2,1,0:T(8,128)(2,1)S(1)} %attend.3), channel_id=1, replica_groups=mesh['section'=16,'ep'=16] {'ep'}, dimensions={0} | all-to-all | bytes 524288 | tf_op jit(solution)/shard_map/all_to_all | solution.py:364
  161.5 0.6 outproj.3
  162.1 14.9 %all_to_all.68.got_ref = bf16[16,16,1536]{2,1,0:T(8,128)(2,1)S(1)} all-to-all(bf16[16,16,1536]{2,1,0:T(8,128)(2,1)S(1)} %bitcast.46), channel_id=1, replica_groups=mesh['section'=16,'ep'=16] {'ep'}, dimensions={0} | all-to-all | bytes 1572864 | tf_op jit(solution)/shard_map/all_to_all | solution.py:364
  177.0 0.4 residual.3
  177.4 14.4 %all_to_all.69 = bf16[16,8,3072]{2,1,0:T(8,128)(2,1)S(1)} all-to-all(bf16[16,8,3072]{2,1,0:T(8,128)(2,1)S(1)} %get-tuple-element.38), channel_id=1, replica_groups=mesh['section'=16,'ep'=16] {'ep'}, dimensions={0} | all-to-all | bytes 1572864 | tf_op jit(solution)/shard_map/all_to_all | solution.py:364
  191.8 2.1 %expert.3 = bf16[128,3072]{1,0:T(8,128)(2,1)S(1)} custom-call(bf16[128,3072]{1,0:T(8,128)(2,1)S(1)} %bitcast.44, bf16[448,3072]{1,0:T(8,128)(2,1)S(1)} %bitcast.38, bf16[448,3072]{1,0:T(8,128)(2,1)S(1)} %bitcast.40, bf16[1,448,3072]{2,1,0:T(8,128)(2,1)S(1)} %copy-done.2), custom_call_target="tpu_custom_call" | custom-call | tf_op jit(solution)/shard_map/expert/pallas_call | solution.py:455
  194.0 14.4 %all_to_all.70.got_ref = bf16[16,8,3072]{2,1,0:T(8,128)(2,1)S(1)} all-to-all(bf16[16,8,3072]{2,1,0:T(8,128)(2,1)S(1)} %bitcast.45), channel_id=1, replica_groups=mesh['section'=16,'ep'=16] {'ep'}, dimensions={0} | all-to-all | bytes 1572864 | tf_op jit(solution)/shard_map/all_to_all | solution.py:364
  208.4 1.1 combine.3
  (11 shorter events, 0.0 us)
Async XLA Ops:
  0.9 8.7 %copy-start.16 = (bf16[1,3072,64]{1,2,0:T(8,128)(2,1)S(1)}, bf16[1,3072,64]{1,2,0:T(8,128)(2,1)}, u32[]{:S(2)}) copy-start(bf16[1,3072,64]{1,2,0:T(8,128)(2,1)} %param.26) | copy-start | bytes 1179652
  2.4 7.6 %copy-start.17 = (bf16[1,3072,64]{1,2,0:T(8,128)(2,1)S(1)}, bf16[1,3072,64]{1,2,0:T(8,128)(2,1)}, u32[]{:S(2)}) copy-start(bf16[1,3072,64]{1,2,0:T(8,128)(2,1)} %param.27) | copy-start | bytes 1179652
  2.4 31.8 %all-to-all-start = ((bf16[16,16,3072]{2,1,0:T(8,128)(2,1)}), bf16[16,16,3072]{2,1,0:T(8,128)(2,1)}, u32[]{:S(2)}, u32[]{:S(2)}) async-start(bf16[16,16,3072]{2,1,0:T(8,128)(2,1)} %norm.1), calls=%async_computation | async-start | bytes 3145728 | tf_op jit(solution)/shard_map/all_to_all | solution.py:364
  15.0 34.3 %collective-permute-start.1 = (bf16[1536,384]{1,0:T(8,128)(2,1)}, bf16[1536,384]{1,0:T(8,128)(2,1)}, u32[]{:S(2)}, u32[]{:S(2)}) collective-permute-start(bf16[1536,384]{1,0:T(8,128)(2,1)} %get-tuple-element.39), channel_id=1, source_target_pairs={{0,4},{1,5},{2,6},{3,7},{4,0},{5,1},{6,2},{7,3},{8,12},{9,13},{10,... | collective-permute-start | bytes 3538952 | tf_op jit(solution)/shard_map/ppermute | solution.py:408
  19.3 28.5 %copy-start.8 = (f32[1,2,16,8,4]{2,4,3,1,0:T(4,128)S(1)}, f32[1,2,16,8,4]{2,4,3,1,0:T(4,128)}, u32[]{:S(2)}) copy-start(f32[1,2,16,8,4]{2,4,3,1,0:T(4,128)} %param.35) | copy-start | bytes 12292
  19.3 28.5 %copy-start.9 = (f32[1,2,16,8,4]{2,4,3,1,0:T(4,128)S(1)}, f32[1,2,16,8,4]{2,4,3,1,0:T(4,128)}, u32[]{:S(2)}) copy-start(f32[1,2,16,8,4]{2,4,3,1,0:T(4,128)} %param.36) | copy-start | bytes 12292
  19.3 28.5 %copy-start.10 = (f32[32,256]{1,0:T(8,128)S(1)}, f32[32,256]{1,0:T(8,128)}, u32[]{:S(2)}) copy-start(f32[32,256]{1,0:T(8,128)} %constant.37.clone.rotary_ref) | copy-start | bytes 98308
  19.3 28.5 %copy-start.11 = (s32[17,256]{1,0:T(8,128)S(1)}, s32[17,256]{1,0:T(8,128)}, u32[]{:S(2)}) copy-start(s32[17,256]{1,0:T(8,128)} %lens_ref.3) | copy-start | bytes 52228
  19.3 30.0 %collective-permute-start = (bf16[256,1536]{1,0:T(8,128)(2,1)}, bf16[256,1536]{1,0:T(8,128)(2,1)}, u32[]{:S(2)}, u32[]{:S(2)}) collective-permute-start(bf16[256,1536]{1,0:T(8,128)(2,1)} %get-tuple-element.41), channel_id=1, source_target_pairs={{0,1},{1,0},{2,3},{3,2},{4,5},{5,4},{6,7},{7,6},{8,9},{9,8},{10,11... | collective-permute-start | bytes 2359304 | tf_op jit(solution)/shard_map/ppermute | solution.py:407
  34.2 13.6 %copy-start.4 = (bf16[1,2,16,8,16,128]{5,4,3,2,1,0:T(8,128)(2,1)S(1)}, bf16[1,2,16,8,16,128]{5,4,3,2,1,0:T(8,128)(2,1)}, u32[]{:S(2)}) copy-start(bf16[1,2,16,8,16,128]{5,4,3,2,1,0:T(8,128)(2,1)} %key_ref.3) | copy-start | bytes 3145732
  34.2 13.6 %copy-start.5 = (bf16[1,2,16,8,16,128]{5,4,3,2,1,0:T(8,128)(2,1)S(1)}, bf16[1,2,16,8,16,128]{5,4,3,2,1,0:T(8,128)(2,1)}, u32[]{:S(2)}) copy-start(bf16[1,2,16,8,16,128]{5,4,3,2,1,0:T(8,128)(2,1)} %value_ref.3) | copy-start | bytes 3145732
  47.8 45.3 %copy-start.2 = (bf16[1,448,3072]{2,1,0:T(8,128)(2,1)S(1)}, bf16[1,448,3072]{2,1,0:T(8,128)(2,1)}, u32[]{:S(2)}) copy-start(bf16[1,448,3072]{2,1,0:T(8,128)(2,1)} %down_ref.3) | copy-start | bytes 8257540
  61.0 17.2 %copy-start.6 = (bf16[16,3072]{1,0:T(8,128)(2,1)S(1)}, bf16[16,3072]{1,0:T(8,128)(2,1)}, u32[]{:S(2)}) copy-start(bf16[16,3072]{1,0:T(8,128)(2,1)} %x_ref.1) | copy-start | bytes 294916
  61.0 17.2 %copy-start.7 = (bf16[1,3072,8]{1,2,0:T(8,128)(2,1)S(1)}, bf16[1,3072,8]{1,2,0:T(8,128)(2,1)}, u32[]{:S(2)}) copy-start(bf16[1,3072,8]{1,2,0:T(8,128)(2,1)} %param.29) | copy-start | bytes 147460
  61.0 17.2 %copy-start.14 = (bf16[1,3072]{1,0:T(2,128)(2,1)S(1)}, bf16[1,3072]{1,0:T(2,128)(2,1)}, u32[]{:S(2)}) copy-start(bf16[1,3072]{1,0:T(2,128)(2,1)} %gain_ref.5) | copy-start | bytes 18436
  61.0 17.2 %copy-start.15 = (s32[1,2,16,2]{2,3,1,0:T(2,128)S(1)}, s32[1,2,16,2]{2,3,1,0:T(2,128)}, u32[]{:S(2)}) copy-start(s32[1,2,16,2]{2,3,1,0:T(2,128)} %param.22) | copy-start | bytes 772
  61.0 32.1 %copy-start.1 = (bf16[1,3072,448]{1,2,0:T(8,128)(2,1)S(1)}, bf16[1,3072,448]{1,2,0:T(8,128)(2,1)}, u32[]{:S(2)}) copy-start(bf16[1,3072,448]{1,2,0:T(8,128)(2,1)} %param.31) | copy-start | bytes 8257540
  62.9 30.2 %copy-start = (bf16[1,3072,448]{1,2,0:T(8,128)(2,1)S(1)}, bf16[1,3072,448]{1,2,0:T(8,128)(2,1)}, u32[]{:S(2)}) copy-start(bf16[1,3072,448]{1,2,0:T(8,128)(2,1)} %param.30) | copy-start | bytes 8257540
  95.3 21.0 %copy-start.12 = (bf16[16,3072]{1,0:T(8,128)(2,1)S(1)}, bf16[16,3072]{1,0:T(8,128)(2,1)}, u32[]{:S(2)}) copy-start(bf16[16,3072]{1,0:T(8,128)(2,1)} %entering_ref.1) | copy-start | bytes 294916
  95.3 21.0 %copy-start.13 = (bf16[1,3072]{1,0:T(2,128)(2,1)S(1)}, bf16[1,3072]{1,0:T(2,128)(2,1)}, u32[]{:S(2)}) copy-start(bf16[1,3072]{1,0:T(2,128)(2,1)} %gain_ref.4) | copy-start | bytes 18436
  95.3 39.4 %copy-start.3 = (bf16[1536,384]{1,0:T(8,128)(2,1)S(1)}, bf16[1536,384]{1,0:T(8,128)(2,1)}, u32[]{:S(2)}) copy-start(bf16[1536,384]{1,0:T(8,128)(2,1)} %get-tuple-element.33.own_ref) | copy-start | bytes 3538948
  110.3 5.9 %collective-permute-start.2 = (bf16[16,3072]{1,0:T(8,128)(2,1)S(1)}, bf16[16,3072]{1,0:T(8,128)(2,1)S(1)}, u32[]{:S(2)}, u32[]{:S(2)}) collective-permute-start(bf16[16,3072]{1,0:T(8,128)(2,1)S(1)} %combine.2), channel_id=1, source_target_pairs={{0,16},{16,32},{32,48},{48,64},{64,80},{80,96},{96,112},{112,128},... | collective-permute-start | bytes 294920 | tf_op jit(solution)/shard_map/ppermute | solution.py:463
